TPU v7x, 512 devices: a whole 4x4x16 slice. The times are simulated.
512 devices in a mesh: grp: 32 (over z, x_lo), ep: 16 (over y, x_hi, core).
Axes of the slice: x: 4 (x_hi: 2, x_lo: 2; x = x_hi * 2 + x_lo), y: 4, z: 16, core: 2. Of those that a mesh axis runs over, the one named last changes fastest.
Arguments:
- hidden: bfloat16 [256, 1536], P('grp', 'ep'), may hold values from -12 to 12
- query: bfloat16 [256, 1536], P('grp'), may hold values from -16 to 16
- new_kv: bfloat16 [256, 2, 512], P('grp'), may hold values from -4 to 4
- key_cache: bfloat16 [98304, 512], P(('grp', 'ep')), may hold values from -6 to 6
- value_cache: bfloat16 [98304, 512], P(('grp', 'ep')), may hold values from -4 to 4
- page_owner: int32 [6144], P(('grp', 'ep')), may hold values from 0 to 15, as said below
- page_fill: int32 [6144], P(('grp', 'ep')), may hold values from 1 to 16, as said below
- out_weight: bfloat16 [1536, 1536], P('grp', 'ep'), may hold values from -0.75 to 0.75
- norm_gain: float32 [1536], P('ep'), may hold values from 0.25 to 1.75
- gate_up: bfloat16 [32, 1536, 1024], P('grp'), may hold values from -0.15625 to 0.15625
- down: bfloat16 [32, 512, 1536], P('grp'), may hold values from -0.25 to 0.25
- routes: int32 [256, 8], P('grp'), may hold values from 0 to 31, all different within a row; in each aligned block of 8 rows (0 to 7, 8 to 15, ...) at most 4 rows name the same one
- route_weight: bfloat16 [256, 8], P('grp'), may hold values from 0.049804688 to 0.3984375
Outputs:
- layer_out: bfloat16 [256, 1536], P('grp', 'ep')
- attn_out: bfloat16 [256, 1536], P('grp')
Inputs may be any that keep to these rules, and one draw needn't show every extreme that they name: `routes`: each row names 8 different experts. In each group's 8 rows (aligned blocks of 8 rows) no expert is named by more than 4 rows, a bound that some block reaches. `page_owner`: A value r under 8 names row r of the page's own group; a value 8 + r names row r of the partner group, whose index differs in the lowest bit. The first page_fill[p] tokens of page p are cached; the rest of the page is unused. The first page of every device is full.
All inputs are finite; a program needn't handle non-finite values.
Results may differ from a plain program's by a relative error of at most 0.017.
Values may be sent and summed in bfloat16 or wider, within the bound.
A program may use at most 64 MiB of HBM per device.

v0:
```python
import jax
import jax.numpy as jnp
from jax import lax
from jax.sharding import PartitionSpec as P

D = 1536
HEADS = 24
KV_HEADS = 8
HD = 64
FF = 512
TOP = 8


masked_score = -1e30
norm_epsilon = 1e-05


def from_partner(block, axis, apart):
    count = lax.axis_size(axis)
    route = []
    for low in range(count):
        high = low | 1 << apart
        if high != low and high < count:
            route += [(low, high), (high, low)]
    return lax.ppermute(block, axis, route)


def combined_all(part, axis, combine):
    gathered = jax.tree.map(lambda a: lax.all_gather(a, axis), part)

    def take(source):
        return jax.tree.map(lambda a: lax.dynamic_index_in_dim(a, source, 0, False), gathered)

    return lax.fori_loop(
        1, lax.axis_size(axis), lambda source, state: combine(state, take(source)), take(0)
    )


def merge_parts(earlier, later):
    max_one, total_one, accum_one = earlier
    max_two, total_two, accum_two = later
    highest = jnp.maximum(max_one, max_two)
    factor_one = jnp.exp(max_one - highest)
    factor_two = jnp.exp(max_two - highest)
    return (
        highest,
        total_one * factor_one + total_two * factor_two,
        accum_one * factor_one[..., None] + accum_two * factor_two[..., None],
    )


def per_device(
    hidden,
    query,
    new_kv,
    key_cache,
    value_cache,
    page_owner,
    page_fill,
    out_weight,
    norm_gain,
    gate_up,
    down,
    routes,
    route_weight,
):
    row_count = query.shape[0]
    group_count = lax.axis_size("grp")
    head_group = HEADS // KV_HEADS
    page_count = page_owner.shape[0]
    token_count = key_cache.shape[0]
    page_length = token_count // page_count
    both_rows = 2 * row_count
    scale = HD ** (-0.5)
    partner_query = from_partner(query, "grp", 0)
    all_queries = jnp.concatenate([query, partner_query], 0)
    query_heads = (
        all_queries.reshape(both_rows, KV_HEADS, head_group, HD)
        .transpose(1, 0, 2, 3)
        .reshape(KV_HEADS, both_rows * head_group, HD)
    )
    key_heads = key_cache.reshape(token_count, KV_HEADS, HD)
    value_heads = value_cache.reshape(token_count, KV_HEADS, HD)
    scores = (
        jnp.einsum("kqd,tkd->kqt", query_heads, key_heads, preferred_element_type=jnp.float32)
        * scale
    )
    scores = scores.reshape(KV_HEADS, both_rows, head_group, token_count)
    row_index = jnp.arange(both_rows, dtype=jnp.int32)
    in_page = jnp.arange(page_length, dtype=jnp.int32)
    usable = (page_owner[None, :, None] == row_index[:, None, None]) & (
        in_page[None, None, :] < page_fill[None, :, None]
    )
    usable = usable.reshape(both_rows, token_count)[None, :, None, :]
    local_top = jnp.max(jnp.where(usable, scores, masked_score), -1)
    weights = jnp.where(usable, jnp.exp(scores - local_top[..., None]), 0.0)
    local_total = jnp.sum(weights, -1)
    rounded = weights.astype(jnp.bfloat16).reshape(KV_HEADS, both_rows * head_group, token_count)
    local_accum = jnp.einsum(
        "kqt,tkd->kqd", rounded, value_heads, preferred_element_type=jnp.float32
    )
    part_max = local_top.transpose(1, 0, 2).reshape(both_rows, HEADS)
    part_total = local_total.transpose(1, 0, 2).reshape(both_rows, HEADS)
    part_accum = (
        local_accum.reshape(KV_HEADS, both_rows, head_group, HD)
        .transpose(1, 0, 2, 3)
        .reshape(both_rows, HEADS, HD)
    )
    merged = combined_all((part_max, part_total, part_accum), "ep", merge_parts)
    returned = from_partner(
        (merged[0][row_count:], merged[1][row_count:], merged[2][row_count:]), "grp", 0
    )
    combined = merge_parts(
        (merged[0][:row_count], merged[1][:row_count], merged[2][:row_count]), returned
    )
    own_query = query.reshape(row_count, KV_HEADS, head_group, HD)
    fresh_key = new_kv[:, 0].reshape(row_count, KV_HEADS, HD)
    fresh_value = new_kv[:, 1].astype(jnp.float32).reshape(row_count, KV_HEADS, HD)
    own_score = (
        jnp.einsum(
            "rkgd,rkd->rkg", own_query, fresh_key, preferred_element_type=jnp.float32
        ).reshape(row_count, HEADS)
        * scale
    )
    cache_max, cache_total, cache_accum = combined
    highest = jnp.maximum(cache_max, own_score)
    cache_factor = jnp.exp(cache_max - highest)
    own_weight = jnp.exp(own_score - highest)
    value_rows = jnp.broadcast_to(
        fresh_value[:, :, None, :], (row_count, KV_HEADS, head_group, HD)
    ).reshape(row_count, HEADS, HD)
    numerator = cache_accum * cache_factor[..., None] + own_weight[..., None] * value_rows
    denominator = cache_total * cache_factor + own_weight
    attn_out = (
        (numerator / denominator[..., None]).reshape(row_count, HEADS * HD).astype(jnp.bfloat16)
    )
    head_share = out_weight.shape[0]
    feature_share = hidden.shape[1]
    every_head = lax.all_gather(attn_out, "grp", axis=0, tiled=True)
    head_columns = lax.dynamic_slice_in_dim(
        every_head, lax.axis_index("grp") * head_share, head_share, 1
    )
    projected = lax.psum_scatter(
        jnp.dot(head_columns, out_weight, preferred_element_type=jnp.float32).astype(jnp.bfloat16),
        "grp",
        scatter_dimension=0,
        tiled=True,
    ).astype(jnp.float32)
    mixed = hidden.astype(jnp.float32) + projected
    squares = lax.psum(jnp.sum(mixed * mixed, -1), "ep")
    normed = (mixed * lax.rsqrt(squares / D + norm_epsilon)[:, None] * norm_gain).astype(
        jnp.bfloat16
    )
    capacity = min(row_count, 2 * row_count * TOP // group_count)
    expert_ids = jnp.arange(group_count, dtype=jnp.int32)
    flat_routes = routes.reshape(-1)
    hits = (flat_routes[:, None] == expert_ids[None, :]).astype(jnp.int32)
    earlier_hits = jnp.cumsum(hits, 0) - hits
    position = jnp.sum(earlier_hits * hits, 1)
    slot_index = flat_routes * capacity + position
    slots_all = jnp.arange(group_count * capacity, dtype=jnp.int32)
    picker = jnp.any(
        slot_index.reshape(row_count, TOP)[None, :, :] == slots_all[:, None, None], 2
    ).astype(jnp.bfloat16)
    sender = (
        jnp.dot(picker, normed, preferred_element_type=jnp.float32)
        .astype(jnp.bfloat16)
        .reshape(group_count, capacity, feature_share)
    )
    arrived = lax.all_to_all(sender, "grp", split_axis=0, concat_axis=0, tiled=True)
    whole_rows = lax.all_to_all(
        arrived.reshape(group_count * capacity, feature_share),
        "ep",
        split_axis=0,
        concat_axis=1,
        tiled=True,
    )
    pre_sum = jnp.dot(whole_rows, gate_up[0], preferred_element_type=jnp.float32)
    activated = (jax.nn.silu(pre_sum[:, :FF]) * pre_sum[:, FF:]).astype(jnp.bfloat16)
    result = jnp.dot(activated, down[0], preferred_element_type=jnp.float32).astype(jnp.bfloat16)
    served = lax.all_to_all(result, "ep", split_axis=1, concat_axis=0, tiled=True).reshape(
        group_count, capacity, feature_share
    )
    returned_rows = lax.all_to_all(served, "grp", split_axis=0, concat_axis=0, tiled=True)
    gathered_rows = returned_rows.reshape(group_count * capacity, feature_share)[
        slot_index
    ].reshape(row_count, TOP, feature_share)
    expert_mix = jnp.sum(
        route_weight.astype(jnp.float32)[:, :, None] * gathered_rows.astype(jnp.float32), 1
    )
    layer_out = (mixed + expert_mix).astype(jnp.bfloat16)
    return (layer_out, attn_out)


def solution(mesh):
    placed = (
        P("grp", "ep"),
        P("grp", None),
        P("grp", None, None),
        P(("grp", "ep"), None),
        P(("grp", "ep"), None),
        P(("grp", "ep")),
        P(("grp", "ep")),
        P("grp", "ep"),
        P("ep"),
        P("grp", None, None),
        P("grp", None, None),
        P("grp", None),
        P("grp", None),
    )
    return jax.shard_map(
        per_device,
        mesh=mesh,
        in_specs=placed,
        out_specs=(P("grp", "ep"), P("grp", None)),
        check_vma=False,
    )
```

profile of v0, /device:TPU:1, one launch (start us, length us, event | category | flops | bytes accessed | tf_op | source)
XLA Modules:
  0.0 435.2 jit_solution(1514925168340241131)
XLA Ops:
  7.2 4.2 collective-permute-start
  13.3 1.8 copy.96
  15.1 1.8 copy.104
  21.1 1.5 reshape.181
  22.6 1.4 slice_reduce_fusion
  24.0 1.4 reshape.199
  25.3 1.7 fusion.43
  27.0 1.5 copy.120
  28.5 1.3 bitcast_multiply_fusion.3
  31.1 1.4 convert_reduce_fusion
  32.5 1.4 reshape.186
  33.9 1.4 copy.112
  36.5 1.3 fusion.21
  37.9 1.4 reduce_window_sum.11
  39.3 1.4 select_reduce_fusion.1
  46.7 25.4 %all_gather.13 = f32[16,16,24]{2,1,0:T(8,128)S(1)} all-gather(f32[1,16,24]{2,1,0:T(8,128)S(1)} %copy.103), channel_id=1, replica_groups=mesh['grp'=32,'ep'=16] {'ep'}, dimensions={0}, use_global_device_ids=true | all-gather | bytes 26112 | tf_op jit(solution)/shard_map/all_gather | solution.py:29
  72.1 22.3 %all_gather.12 = f32[16,16,24]{2,1,0:T(8,128)S(1)} all-gather(f32[1,16,24]{2,1,0:T(8,128)S(1)} %copy.100), channel_id=1, replica_groups=mesh['grp'=32,'ep'=16] {'ep'}, dimensions={0}, use_global_device_ids=true | all-gather | bytes 26112 | tf_op jit(solution)/shard_map/all_gather | solution.py:29
  96.0 28.2 %while.19 = (s32[]{:T(128)}, f32[16,24]{1,0:T(8,128)S(1)}, f32[16,24]{1,0:T(8,128)S(1)}, f32[16,24,64]{2,1,0:T(8,128)S(1)}, f32[16,16,24]{2,1,0:T(8,128)}, /*ind...) while((s32[]{:T(128)}, f32[16,24]{1,0:T(8,128)S(1)}, ...), condition=%wide.region_3.4_spmd, body=%wide.region_2.3_spmd.sunk | while | flops 76037 | bytes 310423 | solution.py:34
  124.3 3.6 collective-permute-start.1
  128.7 1.9 collective-permute-start.3
  132.6 3.4 collective-permute-start.2
  136.8 1.7 collective-permute-done.2
  138.8 55.3 %all_gather.15 = bf16[256,1536]{1,0:T(8,128)(2,1)S(1)} all-gather(bf16[8,1536]{1,0:T(8,128)(2,1)S(1)} %convert_element_type.62), channel_id=1, replica_groups=mesh['grp'=32,'ep'=16] {'grp'}, dimensions={0}, use_global_device_ids=true | all-gather | bytes 811008 | tf_op jit(solution)/shard_map/all_gather | solution.py:139
  194.3 91.1 %all-reduce = bf16[256,96]{1,0:T(8,128)(2,1)S(1)} all-reduce(bf16[256,96]{1,0:T(8,128)(2,1)S(1)} %convolution_convert_fusion.1), channel_id=2, replica_groups=mesh['grp'=32,'ep'=16] {'grp'}, use_global_device_ids=true, to_apply=%region_4.5.clone | all-reduce | flops 24576 | bytes 98304
  286.3 75.5 %psum.7 = f32[8]{0:T(128)S(1)} all-reduce(f32[8]{0:T(128)S(1)} %multiply_reduce_fusion), channel_id=1, replica_groups=mesh['grp'=32,'ep'=16] {'ep'}, use_global_device_ids=true, to_apply=%region_9.10 | all-reduce | flops 8 | bytes 64 | tf_op jit(solution)/shard_map/psum | solution.py:150
  362.9 21.1 %all_to_all.45 = bf16[32,4,96]{2,1,0:T(4,128)(2,1)} all-to-all(bf16[32,4,96]{2,1,0:T(4,128)(2,1)S(1)} %bitcast.92), channel_id=1, replica_groups=mesh['grp'=32,'ep'=16] {'grp'}, dimensions={0} | all-to-all | bytes 49152 | tf_op jit(solution)/shard_map/all_to_all | solution.py:170
  384.0 5.4 %all-to-all-start.1 = ((bf16[16,8,96]{2,1,0:T(8,128)(2,1)}), bf16[16,8,96]{2,1,0:T(8,128)(2,1)S(1)}, u32[]{:S(2)}, u32[]{:S(2)}) async-start(bf16[16,8,96]{2,1,0:T(8,128)(2,1)} %bitcast.18), calls=%async_computation.1 | async-start | bytes 65536 | tf_op jit(solution)/shard_map/all_to_all | solution.py:171
  389.4 7.3 %all-to-all-done.1 = bf16[16,8,96]{2,1,0:T(8,128)(2,1)S(1)} async-done(((bf16[16,8,96]{2,1,0:T(8,128)(2,1)}), bf16[16,8,96]{2,1,0:T(8,128)(2,1)S(1)}, u32[]{:S(2)}, u32[]{:S(2)}) %all-to-all-start.1) | async-done | bytes 24608 | tf_op jit(solution)/shard_map/all_to_all | solution.py:171
  399.3 4.2 all-to-all-start.2
  403.5 7.4 %all-to-all-done.2 = bf16[8,16,96]{2,0,1:T(8,128)(2,1)} async-done(((bf16[8,16,96]{2,0,1:T(8,128)(2,1)}), bf16[8,16,96]{2,0,1:T(8,128)(2,1)}, u32[]{:S(2)}, u32[]{:S(2)}) %all-to-all-start.2) | async-done | bytes 24608 | tf_op jit(solution)/shard_map/all_to_all | solution.py:181
  411.0 3.9 all-to-all-start.3
  414.8 12.2 %all-to-all-done.3 = bf16[32,4,96]{2,1,0:T(4,128)(2,1)S(1)} async-done(((bf16[32,4,96]{2,1,0:T(4,128)(2,1)}), bf16[32,4,96]{2,1,0:T(4,128)(2,1)S(1)}, u32[]{:S(2)}, u32[]{:S(2)}) %all-to-all-start.3) | async-done | bytes 24608 | tf_op jit(solution)/shard_map/all_to_all | solution.py:184
  (127 shorter events, 53.5 us)
Async XLA Ops:
  7.2 389.6 %copy-start = (bf16[1,1536,1024]{2,1,0:T(8,128)(2,1)S(1)}, bf16[1,1536,1024]{2,1,0:T(8,128)(2,1)}, u32[]{:S(2)}) copy-start(bf16[1,1536,1024]{2,1,0:T(8,128)(2,1)} %param.24) | copy-start | bytes 9437188
  7.2 87.8 %all-gather.2.cloned.1.call-start = ((), (), s32[]{:S(2)}) async-start(), calls=%async_computation.4 | async-start | bytes 3342336 | tf_op jit(solution)/shard_map/all_gather | solution.py:29
  7.2 9.6 %collective-permute-start = (bf16[8,1536]{1,0:T(8,128)(2,1)}, bf16[8,1536]{1,0:T(8,128)(2,1)S(1)}, u32[]{:S(2)}, u32[]{:S(2)}) collective-permute-start(bf16[8,1536]{1,0:T(8,128)(2,1)} %param.16), channel_id=1, source_target_pairs={{0,16},{16,0},{32,48},{48,32},{64,80},{80,64},{96,112},{112,96},{1... | collective-permute-start | bytes 73736 | tf_op jit(solution)/shard_map/ppermute | solution.py:25
  44.8 91.2 %copy-start.5 = (f32[8,24]{0,1:T(8,128)S(1)}, f32[8,24]{0,1:T(8,128)}, u32[]{:S(2)}) copy-start(f32[8,24]{0,1:T(8,128)} %mul.194) | copy-start | bytes 2308
  44.8 93.6 %copy-start.3 = (f32[8,8,64]{2,0,1:T(8,128)S(1)}, f32[8,8,64]{2,0,1:T(8,128)}, u32[]{:S(2)}) copy-start(f32[8,8,64]{2,0,1:T(8,128)} %copy.112) | copy-start | bytes 49156
  72.1 122.0 %copy-start.8 = (bf16[48,96]{1,0:T(8,128)(2,1)S(1)}, bf16[48,96]{1,0:T(8,128)(2,1)}, u32[]{:S(2)}) copy-start(bf16[48,96]{1,0:T(8,128)(2,1)} %param.22) | copy-start | bytes 27652
  94.4 0.6 copy-start.2
  95.0 191.1 %copy-start.6 = (s32[8,8]{1,0:T(8,128)S(1)}, s32[8,8]{1,0:T(8,128)}, u32[]{:S(2)}) copy-start(s32[8,8]{1,0:T(8,128)} %get-tuple-element.221) | copy-start | bytes 772
  96.0 293.4 %copy-start.7 = (s32[8,8]{1,0:T(8,128)S(1)}, s32[8,8]{1,0:T(8,128)}, u32[]{:S(2)}) copy-start(s32[8,8]{1,0:T(8,128)} %get-tuple-element.220) | copy-start | bytes 772
  124.3 11.7 %collective-permute-start.1 = (f32[8,24]{0,1:T(8,128)S(1)}, f32[8,24]{0,1:T(8,128)}, u32[]{:S(2)}, u32[]{:S(2)}) collective-permute-start(f32[8,24]{0,1:T(8,128)S(1)} %slice.47), channel_id=1, source_target_pairs={{0,16},{16,0},{32,48},{48,32},{64,80},{80,64},{96,112},{112,96},{1... | collective-permute-start | bytes 2312 | tf_op jit(solution)/shard_map/ppermute | solution.py:25
  128.7 7.3 %collective-permute-start.3 = (f32[8,24]{0,1:T(8,128)}, f32[8,24]{0,1:T(8,128)}, u32[]{:S(2)}, u32[]{:S(2)}) collective-permute-start(f32[8,24]{0,1:T(8,128)} %slice.50), channel_id=1, source_target_pairs={{0,16},{16,0},{32,48},{48,32},{64,80},{80,64},{96,112},{112,96},{1... | collective-permute-start | bytes 2312 | tf_op jit(solution)/shard_map/ppermute | solution.py:25
  132.6 5.8 %collective-permute-start.2 = (f32[8,24,64]{2,0,1:T(8,128)S(1)}, f32[8,24,64]{2,0,1:T(8,128)S(1)}, u32[]{:S(2)}, u32[]{:S(2)}) collective-permute-start(f32[8,24,64]{2,0,1:T(8,128)S(1)} %slice.48), channel_id=1, source_target_pairs={{0,16},{16,0},{32,48},{48,32},{64,80},{80,64},{96,112},{112,96},{1... | collective-permute-start | bytes 147464 | tf_op jit(solution)/shard_map/ppermute | solution.py:25
  138.8 259.8 %copy-start.4 = (bf16[8,1536]{1,0:T(8,128)(2,1)}, bf16[8,1536]{1,0:T(8,128)(2,1)S(1)}, u32[]{:S(2)}) copy-start(bf16[8,1536]{1,0:T(8,128)(2,1)S(1)} %convert_element_type.62) | copy-start | bytes 73732
  138.8 264.7 %copy-start.10 = (s32[64]{0:T(128)S(1)}, s32[64]{0:T(128)}, u32[]{:S(2)}) copy-start(s32[64]{0:T(128)} %select_reduce_fusion.1) | copy-start | bytes 772
  138.8 264.7 %copy-start.11 = (bf16[8,8]{1,0:T(8,128)(2,1)S(1)}, bf16[8,8]{1,0:T(8,128)(2,1)}, u32[]{:S(2)}) copy-start(bf16[8,8]{1,0:T(8,128)(2,1)} %param.27) | copy-start | bytes 388
  194.1 233.7 %copy-start.9 = (bf16[8,96]{1,0:T(8,128)(2,1)S(1)}, bf16[8,96]{1,0:T(8,128)(2,1)}, u32[]{:S(2)}) copy-start(bf16[8,96]{1,0:T(8,128)(2,1)} %param.15) | copy-start | bytes 4612
  384.0 12.7 %all-to-all-start.1 = ((bf16[16,8,96]{2,1,0:T(8,128)(2,1)}), bf16[16,8,96]{2,1,0:T(8,128)(2,1)S(1)}, u32[]{:S(2)}, u32[]{:S(2)}) async-start(bf16[16,8,96]{2,1,0:T(8,128)(2,1)} %bitcast.18), calls=%async_computation.1 | async-start | bytes 65536 | tf_op jit(solution)/shard_map/all_to_all | solution.py:171
  396.8 1.4 copy-start.1
  399.3 11.7 %all-to-all-start.2 = ((bf16[8,16,96]{2,0,1:T(8,128)(2,1)}), bf16[8,16,96]{2,0,1:T(8,128)(2,1)}, u32[]{:S(2)}, u32[]{:S(2)}) async-start(bf16[8,16,96]{2,0,1:T(8,128)(2,1)} %copy.118), calls=%async_computation.2 | async-start | bytes 65536 | tf_op jit(solution)/shard_map/all_to_all | solution.py:181
  411.0 16.1 %all-to-all-start.3 = ((bf16[32,4,96]{2,1,0:T(4,128)(2,1)}), bf16[32,4,96]{2,1,0:T(4,128)(2,1)S(1)}, u32[]{:S(2)}, u32[]{:S(2)}) async-start(bf16[32,4,96]{2,1,0:T(4,128)(2,1)} %bitcast.23), calls=%async_computation.3 | async-start | bytes 65536 | tf_op jit(solution)/shard_map/all_to_all | solution.py:184
Sparse Core Ops, SparseCore 0:
  21.2 71.9 all-gather.1
where the time goes:
time: 438 us; the launch traced here: 435 us
  blocking collectives  291 us (66%)
  other arithmetic  40.8 us (9%)
  waiting for transfers between devices  28.6 us (7%)
  local copies, waits for them, and re-layouts  27.1 us (6%)
  starting transfers between devices  26.6 us (6%)
  between operations  15 us (3%)
  matrix products  6.08 us (1%)
    unnamed x1, blocking collectives  91.1 us
    psum x1, blocking collectives, per_device(): squares = lax.psum(jnp.sum(mixed * mixed, -1), 'ep')  75.5 us
    all_gather x1, blocking collectives, per_device(): every_head = lax.all_gather(attn_out, 'grp', axis=0, tiled=True)  55.3 us
    all_gather x2, blocking collectives, combined_all(): gathered = jax.tree.map(lambda a: lax.all_gather(a, axis), part)  47.7 us
    all_to_all x1, blocking collectives, per_device(): lax.all_to_all(sender, 'grp', split_axis=0, concat_axis=0, tiled=True)  21.1 us
    add x15, other arithmetic, merge_parts(): accum_one * factor_one[..., None] + accum_two * factor_two[..., None]  17 us
    ppermute x4, starting transfers between devices, from_partner(): return lax.ppermute(block, axis, route)  13.1 us
    all_to_all x1, waiting for transfers between devices, per_device(): lax.all_to_all(served, 'grp', split_axis=0, concat_axis=0, tiled=True)  12.2 us
  transfers between devices with their start and end apart: 8, of which 4 were waited for; matrix products, arithmetic and copies ran while one was open for 8% of the time, Pallas kernels for 0%

commit v1 on v0

--- a/solution.py
+++ b/solution.py
@@ -33,6 +33,17 @@
 
     return lax.fori_loop(
         1, lax.axis_size(axis), lambda source, state: combine(state, take(source)), take(0)
+    )
+
+
+def merge_stack(parts):
+    maxes, totals, accums = parts
+    highest = jnp.max(maxes, 0)
+    factors = jnp.exp(maxes - highest[None])
+    return (
+        highest,
+        jnp.sum(totals * factors, 0),
+        jnp.sum(accums * factors[..., None], 0),
     )
 
 
@@ -106,7 +117,8 @@
         .transpose(1, 0, 2, 3)
         .reshape(both_rows, HEADS, HD)
     )
-    merged = combined_all((part_max, part_total, part_accum), "ep", merge_parts)
+    gathered = lax.all_gather((part_max, part_total, part_accum), "ep")
+    merged = merge_stack(gathered)
     returned = from_partner(
         (merged[0][row_count:], merged[1][row_count:], merged[2][row_count:]), "grp", 0
     )
@@ -134,18 +146,9 @@
     attn_out = (
         (numerator / denominator[..., None]).reshape(row_count, HEADS * HD).astype(jnp.bfloat16)
     )
-    head_share = out_weight.shape[0]
+    weight_columns = lax.all_gather(out_weight, "grp", axis=0, tiled=True)
+    projected = jnp.dot(attn_out, weight_columns, preferred_element_type=jnp.float32)
     feature_share = hidden.shape[1]
-    every_head = lax.all_gather(attn_out, "grp", axis=0, tiled=True)
-    head_columns = lax.dynamic_slice_in_dim(
-        every_head, lax.axis_index("grp") * head_share, head_share, 1
-    )
-    projected = lax.psum_scatter(
-        jnp.dot(head_columns, out_weight, preferred_element_type=jnp.float32).astype(jnp.bfloat16),
-        "grp",
-        scatter_dimension=0,
-        tiled=True,
-    ).astype(jnp.float32)
     mixed = hidden.astype(jnp.float32) + projected
     squares = lax.psum(jnp.sum(mixed * mixed, -1), "ep")
     normed = (mixed * lax.rsqrt(squares / D + norm_epsilon)[:, None] * norm_gain).astype(

time: 438 us -> 307 us (0.70)
  blocking collectives: 291 us -> 175 us
  other arithmetic: 40.8 us -> 18.3 us
  local copies, waits for them, and re-layouts: 27.1 us -> 35.2 us
    unnamed x1 -> x0, blocking collectives: 91.1 us -> none
    psum x1, blocking collectives: 75.5 us -> 34.4 us  [per_device(): squares = lax.psum(jnp.sum(mixed * mixed, -1), 'ep')]
    add x30 -> x0, other arithmetic: 27.8 us -> none  [the longest x15 17 us: merge_parts(): accum_one * factor_one[..., None] + accum_two * factor_two[..., None]]
    all_gather x3, blocking collectives: 103 us -> 122 us  [the longest x1 61.6 us: per_device(): weight_columns = lax.all_gather(out_weight, 'grp', axis=0, tiled=True)]
  transfers between devices with their start and end apart: 8 -> 8, of which waited for: 4 -> 4; matrix products, arithmetic and copies ran while one was open for 8% -> 16% of each run, Pallas kernels for 0% -> 0%
where the time goes in v1:
time: 307 us; the launch traced here: 305 us
  blocking collectives  175 us (57%)
  local copies, waits for them, and re-layouts  35.2 us (11%)
  waiting for transfers between devices  29 us (9%)
  starting transfers between devices  26.3 us (9%)
  other arithmetic  18.3 us (6%)
  between operations  14.3 us (5%)
  matrix products  6.86 us (2%)
    all_gather x1, blocking collectives, per_device(): weight_columns = lax.all_gather(out_weight, 'grp', axis=0, tiled=True)  61.6 us
    all_gather x2, blocking collectives, per_device(): gathered = lax.all_gather((part_max, part_total, part_accum), 'ep')  60.9 us
    psum x1, blocking collectives, per_device(): squares = lax.psum(jnp.sum(mixed * mixed, -1), 'ep')  34.4 us
    all_to_all x1, blocking collectives, per_device(): lax.all_to_all(sender, 'grp', split_axis=0, concat_axis=0, tiled=True)  18.4 us
    all_to_all x1, waiting for transfers between devices, per_device(): lax.all_to_all(served, 'grp', split_axis=0, concat_axis=0, tiled=True)  12.2 us
    ppermute x4, starting transfers between devices, from_partner(): return lax.ppermute(block, axis, route)  11.4 us
    all_to_all x1, waiting for transfers between devices, per_device(): lax.all_to_all(result, 'ep', split_axis=1, concat_axis=0, tiled=True)  7.43 us
    all_to_all x1, starting transfers between devices, per_device(): lax.all_to_all(arrived.reshape(group_count * capacity, feature_share), 'e...  6.75 us
  transfers between devices with their start and end apart: 8, of which 4 were waited for; matrix products, arithmetic and copies ran while one was open for 16% of the time, Pallas kernels for 0%

profile of v1, /device:TPU:1, one launch (start us, length us, event | category | flops | bytes accessed | tf_op | source)
XLA Modules:
  0.0 305.3 jit_solution(13315299732806420359)
XLA Ops:
  7.2 4.2 %collective-permute-start = (bf16[8,1536]{1,0:T(8,128)(2,1)}, bf16[8,1536]{1,0:T(8,128)(2,1)S(1)}, u32[]{:S(2)}, u32[]{:S(2)}) collective-permute-start(bf16[8,1536]{1,0:T(8,128)(2,1)} %param.14), channel_id=1, source_target_pairs={{0,16},{16,0},{32,48},{48,32},{64,80},{80,64},{96,112},{112,96},{1... | collective-permute-start | bytes 73736 | tf_op jit(solution)/shard_map/ppermute | solution.py:25
  13.3 1.8 copy.85
  15.1 1.8 copy.87
  21.1 1.5 reshape.181
  23.9 1.4 reshape.199
  25.3 1.7 fusion.35
  27.0 1.5 copy.105
  32.5 1.4 convert_reduce_fusion
  33.8 1.4 reshape.186
  35.2 1.4 copy.96
  39.2 1.4 reduce_window_sum.11
  40.6 1.5 select_reduce_fusion.1
  45.4 61.6 %all_gather.15 = bf16[1536,96]{1,0:T(8,128)(2,1)} all-gather(bf16[48,96]{1,0:T(8,128)(2,1)} %param.20), channel_id=1, replica_groups=mesh['grp'=32,'ep'=16] {'grp'}, dimensions={0}, use_global_device_ids=true | all-gather | bytes 304128 | tf_op jit(solution)/shard_map/all_gather | solution.py:149
  108.5 1.4 copy.98
  112.7 1.4 copy.100
  117.6 40.9 %all_gather.13 = f32[16,16,24]{2,1,0:T(8,128)} all-gather(f32[1,16,24]{2,1,0:T(8,128)S(1)} %copy.93), channel_id=1, replica_groups=mesh['grp'=32,'ep'=16] {'ep'}, dimensions={0}, use_global_device_ids=true | all-gather | bytes 26112 | tf_op jit(solution)/shard_map/all_gather | solution.py:120
  160.1 20.0 %all_gather.14 = f32[16,16,24]{2,1,0:T(8,128)S(1)} all-gather(f32[1,16,24]{2,1,0:T(8,128)} %copy.100), channel_id=1, replica_groups=mesh['grp'=32,'ep'=16] {'ep'}, dimensions={0}, use_global_device_ids=true | all-gather | bytes 26112 | tf_op jit(solution)/shard_map/all_gather | solution.py:120
  180.1 1.6 multiply_reduce_fusion.1
  182.3 1.9 collective-permute-start.3
  184.2 3.4 %collective-permute-start.1 = (f32[8,24]{1,0:T(8,128)}, f32[8,24]{1,0:T(8,128)}, u32[]{:S(2)}, u32[]{:S(2)}) collective-permute-start(f32[8,24]{1,0:T(8,128)} %slice.44), channel_id=1, source_target_pairs={{0,16},{16,0},{32,48},{48,32},{64,80},{80,64},{96,112},{112,96},{1... | collective-permute-start | bytes 2312 | tf_op jit(solution)/shard_map/ppermute | solution.py:25
  187.6 2.4 multiply_reduce_fusion
  190.0 1.9 collective-permute-start.2
  192.7 2.7 collective-permute-done.2
  196.3 1.5 convert_element_type.56
  198.8 34.4 %psum.7 = f32[8]{0:T(128)S(1)} all-reduce(f32[8]{0:T(128)S(1)} %get-tuple-element.13), channel_id=1, replica_groups=mesh['grp'=32,'ep'=16] {'ep'}, use_global_device_ids=true, to_apply=%region_9.10 | all-reduce | flops 8 | bytes 64 | tf_op jit(solution)/shard_map/psum | solution.py:153
  234.3 18.4 %all_to_all.45 = bf16[32,4,96]{2,1,0:T(4,128)(2,1)} all-to-all(bf16[32,4,96]{2,1,0:T(4,128)(2,1)S(1)} %bitcast.63), channel_id=1, replica_groups=mesh['grp'=32,'ep'=16] {'grp'}, dimensions={0} | all-to-all | bytes 49152 | tf_op jit(solution)/shard_map/all_to_all | solution.py:173
  252.7 6.8 %all-to-all-start.1 = ((bf16[16,8,96]{2,1,0:T(8,128)(2,1)}), bf16[16,8,96]{2,1,0:T(8,128)(2,1)S(1)}, u32[]{:S(2)}, u32[]{:S(2)}) async-start(bf16[16,8,96]{2,1,0:T(8,128)(2,1)} %bitcast.12), calls=%async_computation.1 | async-start | bytes 65536 | tf_op jit(solution)/shard_map/all_to_all | solution.py:174
  260.2 6.6 %all-to-all-done.1 = bf16[16,8,96]{2,1,0:T(8,128)(2,1)S(1)} async-done(((bf16[16,8,96]{2,1,0:T(8,128)(2,1)}), bf16[16,8,96]{2,1,0:T(8,128)(2,1)S(1)}, u32[]{:S(2)}, u32[]{:S(2)}) %all-to-all-start.1) | async-done | bytes 24608 | tf_op jit(solution)/shard_map/all_to_all | solution.py:174
  269.4 4.2 %all-to-all-start.2 = ((bf16[8,16,96]{2,0,1:T(8,128)(2,1)}), bf16[8,16,96]{2,0,1:T(8,128)(2,1)}, u32[]{:S(2)}, u32[]{:S(2)}) async-start(bf16[8,16,96]{2,0,1:T(8,128)(2,1)} %copy.103), calls=%async_computation.2 | async-start | bytes 65536 | tf_op jit(solution)/shard_map/all_to_all | solution.py:184
  273.6 7.4 %all-to-all-done.2 = bf16[8,16,96]{2,0,1:T(8,128)(2,1)} async-done(((bf16[8,16,96]{2,0,1:T(8,128)(2,1)}), bf16[8,16,96]{2,0,1:T(8,128)(2,1)}, u32[]{:S(2)}, u32[]{:S(2)}) %all-to-all-start.2) | async-done | bytes 24608 | tf_op jit(solution)/shard_map/all_to_all | solution.py:184
  281.1 3.9 %all-to-all-start.3 = ((bf16[32,4,96]{2,1,0:T(4,128)(2,1)}), bf16[32,4,96]{2,1,0:T(4,128)(2,1)S(1)}, u32[]{:S(2)}, u32[]{:S(2)}) async-start(bf16[32,4,96]{2,1,0:T(4,128)(2,1)} %bitcast.17), calls=%async_computation.3 | async-start | bytes 65536 | tf_op jit(solution)/shard_map/all_to_all | solution.py:187
  284.9 12.2 %all-to-all-done.3 = bf16[32,4,96]{2,1,0:T(4,128)(2,1)S(1)} async-done(((bf16[32,4,96]{2,1,0:T(4,128)(2,1)}), bf16[32,4,96]{2,1,0:T(4,128)(2,1)S(1)}, u32[]{:S(2)}, u32[]{:S(2)}) %all-to-all-start.3) | async-done | bytes 24608 | tf_op jit(solution)/shard_map/all_to_all | solution.py:187
  (81 shorter events, 35.6 us)
Async XLA Ops:
  7.2 259.7 %copy-start = (bf16[1,1536,1024]{2,1,0:T(8,128)(2,1)S(1)}, bf16[1,1536,1024]{2,1,0:T(8,128)(2,1)}, u32[]{:S(2)}) copy-start(bf16[1,1536,1024]{2,1,0:T(8,128)(2,1)} %param.22) | copy-start | bytes 9437188
  7.2 180.4 %all-gather.2.cloned.1.call-start = ((), (), s32[]{:S(2)}) async-start(), calls=%async_computation.4 | async-start | bytes 3342336 | tf_op jit(solution)/shard_map/all_gather | solution.py:120
  7.2 9.6 %collective-permute-start = (bf16[8,1536]{1,0:T(8,128)(2,1)}, bf16[8,1536]{1,0:T(8,128)(2,1)S(1)}, u32[]{:S(2)}, u32[]{:S(2)}) collective-permute-start(bf16[8,1536]{1,0:T(8,128)(2,1)} %param.14), channel_id=1, source_target_pairs={{0,16},{16,0},{32,48},{48,32},{64,80},{80,64},{96,112},{112,96},{1... | collective-permute-start | bytes 73736 | tf_op jit(solution)/shard_map/ppermute | solution.py:25
  108.5 89.3 %copy-start.2 = (bf16[1536,96]{1,0:T(8,128)(2,1)S(1)}, bf16[1536,96]{1,0:T(8,128)(2,1)}, u32[]{:S(2)}) copy-start(bf16[1536,96]{1,0:T(8,128)(2,1)} %all_gather.15) | copy-start | bytes 884740
  182.3 9.7 %collective-permute-start.3 = (f32[8,24]{1,0:T(8,128)}, f32[8,24]{1,0:T(8,128)}, u32[]{:S(2)}, u32[]{:S(2)}) collective-permute-start(f32[8,24]{1,0:T(8,128)} %slice.47), channel_id=1, source_target_pairs={{0,16},{16,0},{32,48},{48,32},{64,80},{80,64},{96,112},{112,96},{1... | collective-permute-start | bytes 2312 | tf_op jit(solution)/shard_map/ppermute | solution.py:25
  184.2 7.8 %collective-permute-start.1 = (f32[8,24]{1,0:T(8,128)}, f32[8,24]{1,0:T(8,128)}, u32[]{:S(2)}, u32[]{:S(2)}) collective-permute-start(f32[8,24]{1,0:T(8,128)} %slice.44), channel_id=1, source_target_pairs={{0,16},{16,0},{32,48},{48,32},{64,80},{80,64},{96,112},{112,96},{1... | collective-permute-start | bytes 2312 | tf_op jit(solution)/shard_map/ppermute | solution.py:25
  187.6 4.4 %copy-start.4 = (f32[8,24]{1,0:T(8,128)S(1)}, f32[8,24]{1,0:T(8,128)}, u32[]{:S(2)}) copy-start(f32[8,24]{1,0:T(8,128)} %copy.94) | copy-start | bytes 2308
  187.6 7.8 %copy-start.3 = (f32[8,8,64]{2,0,1:T(8,128)S(1)}, f32[8,8,64]{2,0,1:T(8,128)}, u32[]{:S(2)}) copy-start(f32[8,8,64]{2,0,1:T(8,128)} %copy.96) | copy-start | bytes 49156
  190.0 5.4 %collective-permute-start.2 = (f32[8,24,64]{2,1,0:T(8,128)S(1)}, f32[8,24,64]{2,1,0:T(8,128)S(1)}, u32[]{:S(2)}, u32[]{:S(2)}) collective-permute-start(f32[8,24,64]{2,1,0:T(8,128)S(1)} %slice.45), channel_id=1, source_target_pairs={{0,16},{16,0},{32,48},{48,32},{64,80},{80,64},{96,112},{112,96},{1... | collective-permute-start | bytes 147464 | tf_op jit(solution)/shard_map/ppermute | solution.py:25
  195.4 78.2 %copy-start.5 = (s32[64]{0:T(128)S(1)}, s32[64]{0:T(128)}, u32[]{:S(2)}) copy-start(s32[64]{0:T(128)} %select_reduce_fusion.1) | copy-start | bytes 772
  195.4 78.2 %copy-start.6 = (bf16[8,8]{1,0:T(8,128)(2,1)S(1)}, bf16[8,8]{1,0:T(8,128)(2,1)}, u32[]{:S(2)}) copy-start(bf16[8,8]{1,0:T(8,128)(2,1)} %param.25) | copy-start | bytes 388
  252.7 14.1 %all-to-all-start.1 = ((bf16[16,8,96]{2,1,0:T(8,128)(2,1)}), bf16[16,8,96]{2,1,0:T(8,128)(2,1)S(1)}, u32[]{:S(2)}, u32[]{:S(2)}) async-start(bf16[16,8,96]{2,1,0:T(8,128)(2,1)} %bitcast.12), calls=%async_computation.1 | async-start | bytes 65536 | tf_op jit(solution)/shard_map/all_to_all | solution.py:174
  266.9 1.4 copy-start.1
  269.4 11.7 %all-to-all-start.2 = ((bf16[8,16,96]{2,0,1:T(8,128)(2,1)}), bf16[8,16,96]{2,0,1:T(8,128)(2,1)}, u32[]{:S(2)}, u32[]{:S(2)}) async-start(bf16[8,16,96]{2,0,1:T(8,128)(2,1)} %copy.103), calls=%async_computation.2 | async-start | bytes 65536 | tf_op jit(solution)/shard_map/all_to_all | solution.py:184
  281.1 16.1 %all-to-all-start.3 = ((bf16[32,4,96]{2,1,0:T(4,128)(2,1)}), bf16[32,4,96]{2,1,0:T(4,128)(2,1)S(1)}, u32[]{:S(2)}, u32[]{:S(2)}) async-start(bf16[32,4,96]{2,1,0:T(4,128)(2,1)} %bitcast.17), calls=%async_computation.3 | async-start | bytes 65536 | tf_op jit(solution)/shard_map/all_to_all | solution.py:187
Sparse Core Ops, SparseCore 0:
  21.2 72.1 all-gather.1

commit v2 on v1

--- a/solution.py
+++ b/solution.py
@@ -1,7 +1,10 @@
 import jax
 import jax.numpy as jnp
 from jax import lax
+from jax.experimental import pallas as pl
+from jax.experimental.pallas import tpu as pltpu
 from jax.sharding import PartitionSpec as P
+import functools
 
 D = 1536
 HEADS = 24
@@ -12,6 +15,125 @@
 
 
 masked_score = -1e30
+
+MESH = pl.DeviceIdType.MESH
+
+
+def merge_kernel(rows, n_ep, part_ref, own_ref, out_ref, got, final, s1, r1, s2, r2):
+    g = lax.axis_index("grp")
+    e = lax.axis_index("ep")
+    mate = g + 1 - 2 * (g % 2)
+    barrier = pltpu.get_barrier_semaphore()
+    for peer in range(n_ep):
+        @pl.when(e != peer)
+        def _():
+            pl.semaphore_signal(barrier, inc=1, device_id=(g, peer), device_id_type=MESH)
+        pl.semaphore_signal(barrier, inc=1, device_id=(mate, peer), device_id_type=MESH)
+    pl.semaphore_wait(barrier, 2 * n_ep - 1)
+
+    def first(row):
+        if row < rows:
+            target = (g, row)
+            slot = e
+        else:
+            target = (mate, row - rows)
+            slot = n_ep + e
+        return pltpu.make_async_remote_copy(
+            src_ref=part_ref.at[row], dst_ref=got.at[slot], send_sem=s1.at[row],
+            recv_sem=r1.at[slot], device_id=target, device_id_type=MESH)
+
+    for row in range(2 * rows):
+        if row < rows:
+            @pl.when(e != row)
+            def _():
+                first(row).start()
+
+            @pl.when(e == row)
+            def _():
+                got[e] = part_ref[row]
+        else:
+            first(row).start()
+
+    def incoming(slot):
+        return pltpu.make_async_remote_copy(
+            src_ref=part_ref.at[0], dst_ref=got.at[slot], send_sem=s1.at[0],
+            recv_sem=r1.at[slot], device_id=(g, 0), device_id_type=MESH)
+
+    def second(target):
+        return pltpu.make_async_remote_copy(
+            src_ref=final.at[e], dst_ref=final.at[e], send_sem=s2.at[target],
+            recv_sem=r2.at[e], device_id=(g, target), device_id_type=MESH)
+
+    @pl.when(e < rows)
+    def _():
+        for slot in range(2 * n_ep):
+            if slot < n_ep:
+                @pl.when(e != slot)
+                def _():
+                    incoming(slot).wait_recv()
+            else:
+                incoming(slot).wait_recv()
+        stack = got[...]
+        own = own_ref[e]
+        maxes = jnp.maximum(jnp.max(stack[:, :, HD:HD + 1], 0), own[:, HD:HD + 1])
+        factors = jnp.exp(stack[:, :, HD:HD + 1] - maxes[None])
+        own_factor = jnp.exp(own[:, HD:HD + 1] - maxes)
+        total = jnp.sum(stack[:, :, HD + 1:HD + 2] * factors, 0) + own_factor
+        accum = jnp.sum(stack[:, :, :HD] * factors, 0) + own[:, :HD] * own_factor
+        final[e] = (accum / total).astype(final.dtype)
+        for target in range(n_ep):
+            @pl.when(e != target)
+            def _():
+                second(target).start()
+
+    for row in range(2 * rows):
+        if row < rows:
+            @pl.when(e != row)
+            def _():
+                first(row).wait_send()
+        else:
+            first(row).wait_send()
+
+    def arriving(row):
+        return pltpu.make_async_remote_copy(
+            src_ref=final.at[row], dst_ref=final.at[row], send_sem=s2.at[0],
+            recv_sem=r2.at[row], device_id=(g, row), device_id_type=MESH)
+
+    for row in range(rows):
+        @pl.when(e != row)
+        def _():
+            arriving(row).wait_recv()
+
+    @pl.when(e < rows)
+    def _():
+        for target in range(n_ep):
+            @pl.when(e != target)
+            def _():
+                second(target).wait_send()
+
+    out_ref[...] = final[...]
+
+
+def merge_call(part, own):
+    rows = own.shape[0]
+    heads = own.shape[1]
+    n_ep = lax.axis_size("ep")
+    return pl.pallas_call(
+        functools.partial(merge_kernel, rows, n_ep),
+        out_shape=jax.ShapeDtypeStruct((rows, heads, HD), jnp.bfloat16),
+        in_specs=[pl.BlockSpec(memory_space=pltpu.VMEM)] * 2,
+        out_specs=pl.BlockSpec(memory_space=pltpu.VMEM),
+        scratch_shapes=[
+            pltpu.VMEM((2 * n_ep, heads, 128), jnp.float32),
+            pltpu.VMEM((rows, heads, HD), jnp.bfloat16),
+            pltpu.SemaphoreType.DMA((2 * rows,)),
+            pltpu.SemaphoreType.DMA((2 * n_ep,)),
+            pltpu.SemaphoreType.DMA((n_ep,)),
+            pltpu.SemaphoreType.DMA((rows,)),
+        ],
+        compiler_params=pltpu.CompilerParams(collective_id=0, has_side_effects=True),
+    )(part, own)
+
 norm_epsilon = 1e-05
 
 
@@ -23,41 +145,6 @@
         if high != low and high < count:
             route += [(low, high), (high, low)]
     return lax.ppermute(block, axis, route)
-
-
-def combined_all(part, axis, combine):
-    gathered = jax.tree.map(lambda a: lax.all_gather(a, axis), part)
-
-    def take(source):
-        return jax.tree.map(lambda a: lax.dynamic_index_in_dim(a, source, 0, False), gathered)
-
-    return lax.fori_loop(
-        1, lax.axis_size(axis), lambda source, state: combine(state, take(source)), take(0)
-    )
-
-
-def merge_stack(parts):
-    maxes, totals, accums = parts
-    highest = jnp.max(maxes, 0)
-    factors = jnp.exp(maxes - highest[None])
-    return (
-        highest,
-        jnp.sum(totals * factors, 0),
-        jnp.sum(accums * factors[..., None], 0),
-    )
-
-
-def merge_parts(earlier, later):
-    max_one, total_one, accum_one = earlier
-    max_two, total_two, accum_two = later
-    highest = jnp.maximum(max_one, max_two)
-    factor_one = jnp.exp(max_one - highest)
-    factor_two = jnp.exp(max_two - highest)
-    return (
-        highest,
-        total_one * factor_one + total_two * factor_two,
-        accum_one * factor_one[..., None] + accum_two * factor_two[..., None],
-    )
 
 
 def per_device(
@@ -117,14 +204,6 @@
         .transpose(1, 0, 2, 3)
         .reshape(both_rows, HEADS, HD)
     )
-    gathered = lax.all_gather((part_max, part_total, part_accum), "ep")
-    merged = merge_stack(gathered)
-    returned = from_partner(
-        (merged[0][row_count:], merged[1][row_count:], merged[2][row_count:]), "grp", 0
-    )
-    combined = merge_parts(
-        (merged[0][:row_count], merged[1][:row_count], merged[2][:row_count]), returned
-    )
     own_query = query.reshape(row_count, KV_HEADS, head_group, HD)
     fresh_key = new_kv[:, 0].reshape(row_count, KV_HEADS, HD)
     fresh_value = new_kv[:, 1].astype(jnp.float32).reshape(row_count, KV_HEADS, HD)
@@ -134,18 +213,17 @@
         ).reshape(row_count, HEADS)
         * scale
     )
-    cache_max, cache_total, cache_accum = combined
-    highest = jnp.maximum(cache_max, own_score)
-    cache_factor = jnp.exp(cache_max - highest)
-    own_weight = jnp.exp(own_score - highest)
     value_rows = jnp.broadcast_to(
         fresh_value[:, :, None, :], (row_count, KV_HEADS, head_group, HD)
     ).reshape(row_count, HEADS, HD)
-    numerator = cache_accum * cache_factor[..., None] + own_weight[..., None] * value_rows
-    denominator = cache_total * cache_factor + own_weight
-    attn_out = (
-        (numerator / denominator[..., None]).reshape(row_count, HEADS * HD).astype(jnp.bfloat16)
-    )
+    pad = jnp.zeros((both_rows, HEADS, 128 - HD - 2), jnp.float32)
+    packed = jnp.concatenate(
+        [part_accum, part_max[..., None], part_total[..., None], pad], -1
+    )
+    own_packed = jnp.concatenate(
+        [value_rows, own_score[..., None], jnp.ones_like(own_score)[..., None], pad[:row_count]], -1
+    )
+    attn_out = merge_call(packed, own_packed).reshape(row_count, HEADS * HD)
     weight_columns = lax.all_gather(out_weight, "grp", axis=0, tiled=True)
     projected = jnp.dot(attn_out, weight_columns, preferred_element_type=jnp.float32)
     feature_share = hidden.shape[1]

time: 307 us -> 228 us (0.74)
  blocking collectives: 175 us -> 113 us
  Pallas kernels: 0 us -> 32.2 us
  local copies, waits for them, and re-layouts: 35.2 us -> 18.6 us
  between operations: 14.3 us -> 0.92 us
  other arithmetic: 18.3 us -> 8.51 us
  starting transfers between devices: 26.3 us -> 22.1 us
    all_gather x2 -> x0, blocking collectives: 60.9 us -> none  [per_device(): gathered = lax.all_gather((part_max, part_total, part_accum), 'ep')]
    pallas_call x0 -> x1, Pallas kernels: none -> 32.2 us  [merge_call(): pl.pallas_call(functools.partial(merge_kernel, rows, n_ep), out_shape=jax...]
    ppermute x4 -> x1, starting transfers between devices: 11.4 us -> 4.21 us  [from_partner(): return lax.ppermute(block, axis, route)]
    reduce_sum x2 -> x0, other arithmetic: 4.01 us -> none  [the longest x1 2.41 us: merge_stack(): jnp.sum(accums * factors[..., None], 0)]
  transfers between devices with their start and end apart: 8 -> 4, of which waited for: 4 -> 3; matrix products, arithmetic and copies ran while one was open for 16% -> 6% of each run, Pallas kernels for 0% -> 0%
where the time goes in v2:
time: 228 us; the launch traced here: 227 us
  blocking collectives  113 us (50%)
  Pallas kernels  32.2 us (14%)
  waiting for transfers between devices  26.2 us (11%)
  starting transfers between devices  22.1 us (10%)
  local copies, waits for them, and re-layouts  18.6 us (8%)
  other arithmetic  8.51 us (4%)
  matrix products  5.67 us (2%)
    all_gather x1, blocking collectives, per_device(): weight_columns = lax.all_gather(out_weight, 'grp', axis=0, tiled=True)  61 us
    psum x1, blocking collectives, per_device(): squares = lax.psum(jnp.sum(mixed * mixed, -1), 'ep')  33.1 us
    pallas_call x1, Pallas kernels, merge_call(): pl.pallas_call(functools.partial(merge_kernel, rows, n_ep), out_shape=jax...  32.2 us
    all_to_all x1, blocking collectives, per_device(): lax.all_to_all(sender, 'grp', split_axis=0, concat_axis=0, tiled=True)  18.9 us
    all_to_all x1, waiting for transfers between devices, per_device(): lax.all_to_all(served, 'grp', split_axis=0, concat_axis=0, tiled=True)  12.2 us
    all_to_all x1, starting transfers between devices, per_device(): lax.all_to_all(arrived.reshape(group_count * capacity, feature_share), 'e...  9.8 us
    all_to_all x1, waiting for transfers between devices, per_device(): lax.all_to_all(result, 'ep', split_axis=1, concat_axis=0, tiled=True)  7.43 us
    all_to_all x1, waiting for transfers between devices, per_device(): lax.all_to_all(arrived.reshape(group_count * capacity, feature_share), 'e...  6.6 us
  transfers between devices with their start and end apart: 4, of which 3 were waited for; matrix products, arithmetic and copies ran while one was open for 6% of the time, Pallas kernels for 0%

profile of v2, /device:TPU:1, one launch (start us, length us, event | category | flops | bytes accessed | tf_op | source)
XLA Modules:
  0.0 227.3 jit_solution(7646470424980892187)
XLA Ops:
  0.6 4.2 %collective-permute-start = (bf16[8,1536]{1,0:T(8,128)(2,1)}, bf16[8,1536]{1,0:T(8,128)(2,1)S(1)}, u32[]{:S(2)}, u32[]{:S(2)}) collective-permute-start(bf16[8,1536]{1,0:T(8,128)(2,1)} %param.14), channel_id=1, source_target_pairs={{0,16},{16,0},{32,48},{48,32},{64,80},{80,64},{96,112},{112,96},{1... | collective-permute-start | bytes 73736 | tf_op jit(solution)/shard_map/ppermute | solution.py:147
  4.9 0.9 reshape.190
  5.7 0.8 slice_reduce_fusion
  6.5 0.8 convert_reduce_fusion
  8.2 0.7 broadcast_reduce_fusion
  10.1 61.0 %all_gather.3 = bf16[1536,96]{1,0:T(8,128)(2,1)} all-gather(bf16[48,96]{1,0:T(8,128)(2,1)} %param.20), channel_id=1, replica_groups=mesh['grp'=32,'ep'=16] {'grp'}, dimensions={0}, use_global_device_ids=true | all-gather | bytes 304128 | tf_op jit(solution)/shard_map/all_gather | solution.py:227
  71.1 0.8 eq.49
  72.3 1.3 broadcast_multiply_fusion
  73.6 0.7 maximum_maximum_fusion.1.own_ref
  75.1 1.8 copy.57
  76.8 1.8 copy.59
  79.5 1.2 select_reduce_fusion
  81.5 0.8 fusion.3
  82.3 1.2 fusion.5
  84.8 1.4 reduce_max.12
  86.1 0.8 copy.63
  87.6 1.6 copy.67
  89.2 1.8 maximum_maximum_fusion.part_ref
  90.9 32.2 %shard_map.140 = bf16[8,24,64]{2,1,0:T(8,128)(2,1)} custom-call(f32[16,24,128]{2,1,0:T(8,128)} %maximum_maximum_fusion.part_ref, f32[8,24,128]{2,1,0:T(8,128)} %maximum_maximum_fusion.1.own_ref), custom_call_target="tpu_custom_call" | custom-call | tf_op jit(solution)/shard_map/pallas_call | solution.py:121
  123.1 0.9 reshape.191
  124.1 1.3 multiply_reduce_fusion
  125.3 33.1 %psum.7 = f32[8]{0:T(128)S(1)} all-reduce(f32[8]{0:T(128)S(1)} %get-tuple-element.6), channel_id=1, replica_groups=mesh['grp'=32,'ep'=16] {'ep'}, use_global_device_ids=true, to_apply=%region_6.7 | all-reduce | flops 8 | bytes 64 | tf_op jit(solution)/shard_map/psum | solution.py:231
  158.5 1.0 convolution_convert_fusion.1
  159.6 18.9 %all_to_all.45 = bf16[32,4,96]{2,1,0:T(4,128)(2,1)} all-to-all(bf16[32,4,96]{2,1,0:T(4,128)(2,1)S(1)} %bitcast.64), channel_id=1, replica_groups=mesh['grp'=32,'ep'=16] {'grp'}, dimensions={0} | all-to-all | bytes 49152 | tf_op jit(solution)/shard_map/all_to_all | solution.py:251
  178.4 9.8 %all-to-all-start.1 = ((bf16[16,8,96]{2,1,0:T(8,128)(2,1)}), bf16[16,8,96]{2,1,0:T(8,128)(2,1)S(1)}, u32[]{:S(2)}, u32[]{:S(2)}) async-start(bf16[16,8,96]{2,1,0:T(8,128)(2,1)} %bitcast.12), calls=%async_computation.1 | async-start | bytes 65536 | tf_op jit(solution)/shard_map/all_to_all | solution.py:252
  188.2 0.8 mul.93
  189.0 6.6 %all-to-all-done.1 = bf16[16,8,96]{2,1,0:T(8,128)(2,1)S(1)} async-done(((bf16[16,8,96]{2,1,0:T(8,128)(2,1)}), bf16[16,8,96]{2,1,0:T(8,128)(2,1)S(1)}, u32[]{:S(2)}, u32[]{:S(2)}) %all-to-all-start.1) | async-done | bytes 24608 | tf_op jit(solution)/shard_map/all_to_all | solution.py:252
  196.2 0.9 copy-done.1
  198.2 4.2 %all-to-all-start.2 = ((bf16[8,16,96]{2,0,1:T(8,128)(2,1)}), bf16[8,16,96]{2,0,1:T(8,128)(2,1)}, u32[]{:S(2)}, u32[]{:S(2)}) async-start(bf16[8,16,96]{2,0,1:T(8,128)(2,1)} %copy.74), calls=%async_computation.2 | async-start | bytes 65536 | tf_op jit(solution)/shard_map/all_to_all | solution.py:262
  202.4 7.4 %all-to-all-done.2 = bf16[8,16,96]{2,0,1:T(8,128)(2,1)} async-done(((bf16[8,16,96]{2,0,1:T(8,128)(2,1)}), bf16[8,16,96]{2,0,1:T(8,128)(2,1)}, u32[]{:S(2)}, u32[]{:S(2)}) %all-to-all-start.2) | async-done | bytes 24608 | tf_op jit(solution)/shard_map/all_to_all | solution.py:262
  209.9 3.9 %all-to-all-start.3 = ((bf16[32,4,96]{2,1,0:T(4,128)(2,1)}), bf16[32,4,96]{2,1,0:T(4,128)(2,1)S(1)}, u32[]{:S(2)}, u32[]{:S(2)}) async-start(bf16[32,4,96]{2,1,0:T(4,128)(2,1)} %bitcast.17), calls=%async_computation.3 | async-start | bytes 65536 | tf_op jit(solution)/shard_map/all_to_all | solution.py:265
  213.7 12.2 %all-to-all-done.3 = bf16[32,4,96]{2,1,0:T(4,128)(2,1)S(1)} async-done(((bf16[32,4,96]{2,1,0:T(4,128)(2,1)}), bf16[32,4,96]{2,1,0:T(4,128)(2,1)S(1)}, u32[]{:S(2)}, u32[]{:S(2)}) %all-to-all-start.3) | async-done | bytes 24608 | tf_op jit(solution)/shard_map/all_to_all | solution.py:265
  (69 shorter events, 9.7 us)
Async XLA Ops:
  0.6 195.1 %copy-start = (bf16[1,1536,1024]{2,1,0:T(8,128)(2,1)S(1)}, bf16[1,1536,1024]{2,1,0:T(8,128)(2,1)}, u32[]{:S(2)}) copy-start(bf16[1,1536,1024]{2,1,0:T(8,128)(2,1)} %param.22) | copy-start | bytes 9437188
  0.6 77.9 %collective-permute-start = (bf16[8,1536]{1,0:T(8,128)(2,1)}, bf16[8,1536]{1,0:T(8,128)(2,1)S(1)}, u32[]{:S(2)}, u32[]{:S(2)}) collective-permute-start(bf16[8,1536]{1,0:T(8,128)(2,1)} %param.14), channel_id=1, source_target_pairs={{0,16},{16,0},{32,48},{48,32},{64,80},{80,64},{96,112},{112,96},{1... | collective-permute-start | bytes 73736 | tf_op jit(solution)/shard_map/ppermute | solution.py:147
  10.0 69.5 %copy-start.6 = (f32[128]{0:T(128)}, f32[128]{0:T(128)S(1)}, u32[]{:S(2)}) copy-start(f32[128]{0:T(128)S(1)} %pad.7.clone) | copy-start | bytes 1540
  72.2 7.3 %copy-start.3 = (s32[64]{0:T(128)}, s32[64]{0:T(128)S(1)}, u32[]{:S(2)}) copy-start(s32[64]{0:T(128)S(1)} %select_reduce_fusion.1) | copy-start | bytes 772
  90.9 111.5 %copy-start.4 = (s32[64]{0:T(128)S(1)}, s32[64]{0:T(128)}, u32[]{:S(2)}) copy-start(s32[64]{0:T(128)} %copy-done.3) | copy-start | bytes 772
  90.9 111.5 %copy-start.5 = (bf16[8,8]{1,0:T(8,128)(2,1)S(1)}, bf16[8,8]{1,0:T(8,128)(2,1)}, u32[]{:S(2)}) copy-start(bf16[8,8]{1,0:T(8,128)(2,1)} %param.25) | copy-start | bytes 388
  124.1 103.2 %copy-start.2 = (bf16[8,1536]{1,0:T(8,128)(2,1)}, bf16[8,1536]{1,0:T(8,128)(2,1)S(1)}, u32[]{:S(2)}) copy-start(bf16[8,1536]{1,0:T(8,128)(2,1)S(1)} %reshape.191) | copy-start | bytes 73732
  178.4 17.2 %all-to-all-start.1 = ((bf16[16,8,96]{2,1,0:T(8,128)(2,1)}), bf16[16,8,96]{2,1,0:T(8,128)(2,1)S(1)}, u32[]{:S(2)}, u32[]{:S(2)}) async-start(bf16[16,8,96]{2,1,0:T(8,128)(2,1)} %bitcast.12), calls=%async_computation.1 | async-start | bytes 65536 | tf_op jit(solution)/shard_map/all_to_all | solution.py:252
  195.7 1.4 copy-start.1
  198.2 11.7 %all-to-all-start.2 = ((bf16[8,16,96]{2,0,1:T(8,128)(2,1)}), bf16[8,16,96]{2,0,1:T(8,128)(2,1)}, u32[]{:S(2)}, u32[]{:S(2)}) async-start(bf16[8,16,96]{2,0,1:T(8,128)(2,1)} %copy.74), calls=%async_computation.2 | async-start | bytes 65536 | tf_op jit(solution)/shard_map/all_to_all | solution.py:262
  209.9 16.1 %all-to-all-start.3 = ((bf16[32,4,96]{2,1,0:T(4,128)(2,1)}), bf16[32,4,96]{2,1,0:T(4,128)(2,1)S(1)}, u32[]{:S(2)}, u32[]{:S(2)}) async-start(bf16[32,4,96]{2,1,0:T(4,128)(2,1)} %bitcast.17), calls=%async_computation.3 | async-start | bytes 65536 | tf_op jit(solution)/shard_map/all_to_all | solution.py:265

commit v3 on v2

--- a/solution.py
+++ b/solution.py
@@ -19,7 +19,10 @@
 MESH = pl.DeviceIdType.MESH
 
 
-def merge_kernel(rows, n_ep, part_ref, own_ref, out_ref, got, final, s1, r1, s2, r2):
+def merge_kernel(
+    rows, n_ep, n_grp, part_ref, own_ref, block_ref, out_ref, columns_ref,
+    got, final, blocks, s1, r1, s2, r2, s3, r3,
+):
     g = lax.axis_index("grp")
     e = lax.axis_index("ep")
     mate = g + 1 - 2 * (g % 2)
@@ -29,7 +32,11 @@
         def _():
             pl.semaphore_signal(barrier, inc=1, device_id=(g, peer), device_id_type=MESH)
         pl.semaphore_signal(barrier, inc=1, device_id=(mate, peer), device_id_type=MESH)
-    pl.semaphore_wait(barrier, 2 * n_ep - 1)
+    for step in range(1, n_grp):
+        pl.semaphore_signal(
+            barrier, inc=1, device_id=(lax.rem(g + step, n_grp), e), device_id_type=MESH
+        )
+    pl.semaphore_wait(barrier, 2 * n_ep - 1 + n_grp - 1)
 
     def first(row):
         if row < rows:
@@ -53,6 +60,21 @@
                 got[e] = part_ref[row]
         else:
             first(row).start()
+
+    def spread(step):
+        return pltpu.make_async_remote_copy(
+            src_ref=block_ref, dst_ref=blocks.at[g], send_sem=s3.at[step],
+            recv_sem=r3.at[g], device_id=(lax.rem(g + step, n_grp), e), device_id_type=MESH)
+
+    def gathered(step):
+        source = lax.rem(g + n_grp - step, n_grp)
+        return pltpu.make_async_remote_copy(
+            src_ref=block_ref, dst_ref=blocks.at[source], send_sem=s3.at[step],
+            recv_sem=r3.at[source], device_id=(source, e), device_id_type=MESH)
+
+    for step in range(1, n_grp):
+        spread(step).start()
+    blocks[g] = block_ref[...]
 
     def incoming(slot):
         return pltpu.make_async_remote_copy(
@@ -111,28 +133,40 @@
             def _():
                 second(target).wait_send()
 
+    for step in range(1, n_grp):
+        spread(step).wait_send()
+        gathered(step).wait_recv()
     out_ref[...] = final[...]
-
-
-def merge_call(part, own):
+    columns_ref[...] = blocks[...]
+
+
+def merge_call(part, own, block):
     rows = own.shape[0]
     heads = own.shape[1]
     n_ep = lax.axis_size("ep")
+    n_grp = lax.axis_size("grp")
+    gathered_shape = (n_grp,) + block.shape
     return pl.pallas_call(
-        functools.partial(merge_kernel, rows, n_ep),
-        out_shape=jax.ShapeDtypeStruct((rows, heads, HD), jnp.bfloat16),
-        in_specs=[pl.BlockSpec(memory_space=pltpu.VMEM)] * 2,
-        out_specs=pl.BlockSpec(memory_space=pltpu.VMEM),
+        functools.partial(merge_kernel, rows, n_ep, n_grp),
+        out_shape=(
+            jax.ShapeDtypeStruct((rows, heads, HD), jnp.bfloat16),
+            jax.ShapeDtypeStruct(gathered_shape, block.dtype),
+        ),
+        in_specs=[pl.BlockSpec(memory_space=pltpu.VMEM)] * 3,
+        out_specs=(pl.BlockSpec(memory_space=pltpu.VMEM),) * 2,
         scratch_shapes=[
             pltpu.VMEM((2 * n_ep, heads, 128), jnp.float32),
             pltpu.VMEM((rows, heads, HD), jnp.bfloat16),
+            pltpu.VMEM(gathered_shape, block.dtype),
             pltpu.SemaphoreType.DMA((2 * rows,)),
             pltpu.SemaphoreType.DMA((2 * n_ep,)),
             pltpu.SemaphoreType.DMA((n_ep,)),
             pltpu.SemaphoreType.DMA((rows,)),
+            pltpu.SemaphoreType.DMA((n_grp,)),
+            pltpu.SemaphoreType.DMA((n_grp,)),
         ],
         compiler_params=pltpu.CompilerParams(collective_id=0, has_side_effects=True),
-    )(part, own)
+    )(part, own, block)
 
 norm_epsilon = 1e-05
 
@@ -223,8 +257,9 @@
     own_packed = jnp.concatenate(
         [value_rows, own_score[..., None], jnp.ones_like(own_score)[..., None], pad[:row_count]], -1
     )
-    attn_out = merge_call(packed, own_packed).reshape(row_count, HEADS * HD)
-    weight_columns = lax.all_gather(out_weight, "grp", axis=0, tiled=True)
+    merged, weight_blocks = merge_call(packed, own_packed, out_weight)
+    attn_out = merged.reshape(row_count, HEADS * HD)
+    weight_columns = weight_blocks.reshape(-1, out_weight.shape[1])
     projected = jnp.dot(attn_out, weight_columns, preferred_element_type=jnp.float32)
     feature_share = hidden.shape[1]
     mixed = hidden.astype(jnp.float32) + projected

time: 228 us -> 173 us (0.76)
  blocking collectives: 113 us -> 53.1 us
  Pallas kernels: 32.2 us -> 40.2 us
  starting transfers between devices: 22.1 us -> 18.4 us
    all_gather x1 -> x0, blocking collectives: 61 us -> none  [per_device(): weight_columns = lax.all_gather(out_weight, 'grp', axis=0, tiled=True)]
    pallas_call x1, Pallas kernels: 32.2 us -> 40.2 us  [merge_call(): pl.pallas_call(functools.partial(merge_kernel, rows, n_ep, n_grp), out_sh...]
    all_to_all x1, starting transfers between devices: 9.8 us -> 6.04 us  [per_device(): lax.all_to_all(arrived.reshape(group_count * capacity, feature_share), 'e...]
  transfers between devices with their start and end apart: 4 -> 4, of which waited for: 3 -> 3; matrix products, arithmetic and copies ran while one was open for 6% -> 8% of each run, Pallas kernels for 0% -> 0%
where the time goes in v3:
time: 173 us; the launch traced here: 172 us
  blocking collectives  53.1 us (31%)
  Pallas kernels  40.2 us (23%)
  waiting for transfers between devices  26.2 us (15%)
  local copies, waits for them, and re-layouts  18.6 us (11%)
  starting transfers between devices  18.4 us (11%)
  other arithmetic  8.51 us (5%)
  matrix products  5.68 us (3%)
    pallas_call x1, Pallas kernels, merge_call(): pl.pallas_call(functools.partial(merge_kernel, rows, n_ep, n_grp), out_sh...  40.2 us
    psum x1, blocking collectives, per_device(): squares = lax.psum(jnp.sum(mixed * mixed, -1), 'ep')  33.6 us
    all_to_all x1, blocking collectives, per_device(): lax.all_to_all(sender, 'grp', split_axis=0, concat_axis=0, tiled=True)  19.5 us
    all_to_all x1, waiting for transfers between devices, per_device(): lax.all_to_all(served, 'grp', split_axis=0, concat_axis=0, tiled=True)  12.2 us
    all_to_all x1, waiting for transfers between devices, per_device(): lax.all_to_all(result, 'ep', split_axis=1, concat_axis=0, tiled=True)  7.43 us
    all_to_all x1, waiting for transfers between devices, per_device(): lax.all_to_all(arrived.reshape(group_count * capacity, feature_share), 'e...  6.6 us
    all_to_all x1, starting transfers between devices, per_device(): lax.all_to_all(arrived.reshape(group_count * capacity, feature_share), 'e...  6.04 us
    unnamed x16, local copies, waits for them, and re-layouts  4.44 us
  transfers between devices with their start and end apart: 4, of which 3 were waited for; matrix products, arithmetic and copies ran while one was open for 8% of the time, Pallas kernels for 0%

profile of v3, /device:TPU:1, one launch (start us, length us, event | category | flops | bytes accessed | tf_op | source)
XLA Modules:
  0.0 171.5 jit_solution(350138727276178993)
XLA Ops:
  0.6 4.2 %collective-permute-start = (bf16[8,1536]{1,0:T(8,128)(2,1)}, bf16[8,1536]{1,0:T(8,128)(2,1)S(1)}, u32[]{:S(2)}, u32[]{:S(2)}) collective-permute-start(bf16[8,1536]{1,0:T(8,128)(2,1)} %param.14), channel_id=1, source_target_pairs={{0,16},{16,0},{32,48},{48,32},{64,80},{80,64},{96,112},{112,96},{1... | collective-permute-start | bytes 73736 | tf_op jit(solution)/shard_map/ppermute | solution.py:181
  4.9 0.9 reshape.193
  5.7 0.8 slice_reduce_fusion
  6.5 0.8 convert_reduce_fusion
  8.2 0.7 broadcast_reduce_fusion
  10.1 0.8 eq.49
  11.3 1.3 broadcast_multiply_fusion
  14.0 1.8 %copy.57 = bf16[192,512]{0,1:T(8,128)(2,1)} copy(bf16[192,512]{1,0:T(8,128)(2,1)} %param.16) | data formatting | bytes 393216 | tf_op args[3]
  15.8 1.8 %copy.59 = bf16[192,512]{0,1:T(8,128)(2,1)} copy(bf16[192,512]{1,0:T(8,128)(2,1)} %param.17) | data formatting | bytes 393216 | tf_op args[4]
  17.6 0.7 pad_maximum_fusion
  18.5 1.2 select_reduce_fusion
  20.4 0.8 fusion.3
  21.2 1.2 fusion.5
  22.6 0.7 copy.64
  23.7 1.4 reduce_max.12
  25.1 0.8 copy.63
  26.5 1.6 copy.67
  28.1 1.8 %maximum_maximum_fusion.part_ref = f32[16,24,128]{2,1,0:T(8,128)} fusion(f32[16,24,1]{2,1,0:T(8,128)S(1)} %copy.68, f32[16,24,1]{2,1,0:T(8,128)} %copy.67, f32[16,24,64]{2,1,0:T(8,128)S(1)} %copy.66, f32[128]{0:T(128)} %copy-done.6), kind=kLoop, calls=%fused_computation.13 | loop fusion | flops 147456 | bytes 298496 | tf_op jit(solution)/shard_map/concatenate | solution.py:254
  29.9 40.2 %shard_map.140 = (bf16[8,24,64]{2,1,0:T(8,128)(2,1)}, bf16[32,48,96]{2,1,0:T(8,128)(2,1)}) custom-call(f32[16,24,128]{2,1,0:T(8,128)} %maximum_maximum_fusion.part_ref, f32[8,24,128]{2,1,0:T(8,128)} %maximum_maximum_fusion.1.own_ref, bf16[48,96]{1,0:T(8,128)(2,1)} %block_ref.1), custom_call_target="tpu_custom_call" | custom-call | tf_op jit(solution)/shard_map/pallas_call | solution.py:149
  70.1 0.9 reshape.194
  71.0 1.3 multiply_reduce_fusion
  72.3 33.6 %psum.7 = f32[8]{0:T(128)S(1)} all-reduce(f32[8]{0:T(128)S(1)} %get-tuple-element.10), channel_id=1, replica_groups=mesh['grp'=32,'ep'=16] {'ep'}, use_global_device_ids=true, to_apply=%region_6.7 | all-reduce | flops 8 | bytes 64 | tf_op jit(solution)/shard_map/psum | solution.py:266
  105.9 1.0 convolution_convert_fusion.1
  107.0 19.5 %all_to_all.45 = bf16[32,4,96]{2,1,0:T(4,128)(2,1)} all-to-all(bf16[32,4,96]{2,1,0:T(4,128)(2,1)S(1)} %bitcast.66), channel_id=1, replica_groups=mesh['grp'=32,'ep'=16] {'grp'}, dimensions={0} | all-to-all | bytes 49152 | tf_op jit(solution)/shard_map/all_to_all | solution.py:286
  126.4 6.0 %all-to-all-start.1 = ((bf16[16,8,96]{2,1,0:T(8,128)(2,1)}), bf16[16,8,96]{2,1,0:T(8,128)(2,1)S(1)}, u32[]{:S(2)}, u32[]{:S(2)}) async-start(bf16[16,8,96]{2,1,0:T(8,128)(2,1)} %bitcast.13), calls=%async_computation.1 | async-start | bytes 65536 | tf_op jit(solution)/shard_map/all_to_all | solution.py:287
  132.5 0.8 mul.93
  133.2 6.6 %all-to-all-done.1 = bf16[16,8,96]{2,1,0:T(8,128)(2,1)S(1)} async-done(((bf16[16,8,96]{2,1,0:T(8,128)(2,1)}), bf16[16,8,96]{2,1,0:T(8,128)(2,1)S(1)}, u32[]{:S(2)}, u32[]{:S(2)}) %all-to-all-start.1) | async-done | bytes 24608 | tf_op jit(solution)/shard_map/all_to_all | solution.py:287
  140.5 0.9 copy-done.1
  142.4 4.2 %all-to-all-start.2 = ((bf16[8,16,96]{2,0,1:T(8,128)(2,1)}), bf16[8,16,96]{2,0,1:T(8,128)(2,1)}, u32[]{:S(2)}, u32[]{:S(2)}) async-start(bf16[8,16,96]{2,0,1:T(8,128)(2,1)} %copy.74), calls=%async_computation.2 | async-start | bytes 65536 | tf_op jit(solution)/shard_map/all_to_all | solution.py:297
  146.7 7.4 %all-to-all-done.2 = bf16[8,16,96]{2,0,1:T(8,128)(2,1)} async-done(((bf16[8,16,96]{2,0,1:T(8,128)(2,1)}), bf16[8,16,96]{2,0,1:T(8,128)(2,1)}, u32[]{:S(2)}, u32[]{:S(2)}) %all-to-all-start.2) | async-done | bytes 24608 | tf_op jit(solution)/shard_map/all_to_all | solution.py:297
  154.1 3.9 %all-to-all-start.3 = ((bf16[32,4,96]{2,1,0:T(4,128)(2,1)}), bf16[32,4,96]{2,1,0:T(4,128)(2,1)S(1)}, u32[]{:S(2)}, u32[]{:S(2)}) async-start(bf16[32,4,96]{2,1,0:T(4,128)(2,1)} %bitcast.18), calls=%async_computation.3 | async-start | bytes 65536 | tf_op jit(solution)/shard_map/all_to_all | solution.py:300
  158.0 12.2 %all-to-all-done.3 = bf16[32,4,96]{2,1,0:T(4,128)(2,1)S(1)} async-done(((bf16[32,4,96]{2,1,0:T(4,128)(2,1)}), bf16[32,4,96]{2,1,0:T(4,128)(2,1)S(1)}, u32[]{:S(2)}, u32[]{:S(2)}) %all-to-all-start.3) | async-done | bytes 24608 | tf_op jit(solution)/shard_map/all_to_all | solution.py:300
  (68 shorter events, 9.0 us)
Async XLA Ops:
  0.6 139.3 %copy-start = (bf16[1,1536,1024]{2,1,0:T(8,128)(2,1)S(1)}, bf16[1,1536,1024]{2,1,0:T(8,128)(2,1)}, u32[]{:S(2)}) copy-start(bf16[1,1536,1024]{2,1,0:T(8,128)(2,1)} %param.22) | copy-start | bytes 9437188
  0.6 16.9 %collective-permute-start = (bf16[8,1536]{1,0:T(8,128)(2,1)}, bf16[8,1536]{1,0:T(8,128)(2,1)S(1)}, u32[]{:S(2)}, u32[]{:S(2)}) collective-permute-start(bf16[8,1536]{1,0:T(8,128)(2,1)} %param.14), channel_id=1, source_target_pairs={{0,16},{16,0},{32,48},{48,32},{64,80},{80,64},{96,112},{112,96},{1... | collective-permute-start | bytes 73736 | tf_op jit(solution)/shard_map/ppermute | solution.py:181
  10.0 8.5 %copy-start.6 = (f32[128]{0:T(128)}, f32[128]{0:T(128)S(1)}, u32[]{:S(2)}) copy-start(f32[128]{0:T(128)S(1)} %pad.7.clone) | copy-start | bytes 1540
  11.2 7.3 %copy-start.3 = (s32[64]{0:T(128)}, s32[64]{0:T(128)S(1)}, u32[]{:S(2)}) copy-start(s32[64]{0:T(128)S(1)} %select_reduce_fusion.1) | copy-start | bytes 772
  29.9 116.8 %copy-start.4 = (s32[64]{0:T(128)S(1)}, s32[64]{0:T(128)}, u32[]{:S(2)}) copy-start(s32[64]{0:T(128)} %copy-done.3) | copy-start | bytes 772
  29.9 116.8 %copy-start.5 = (bf16[8,8]{1,0:T(8,128)(2,1)S(1)}, bf16[8,8]{1,0:T(8,128)(2,1)}, u32[]{:S(2)}) copy-start(bf16[8,8]{1,0:T(8,128)(2,1)} %param.25) | copy-start | bytes 388
  71.0 100.5 %copy-start.2 = (bf16[8,1536]{1,0:T(8,128)(2,1)}, bf16[8,1536]{1,0:T(8,128)(2,1)S(1)}, u32[]{:S(2)}) copy-start(bf16[8,1536]{1,0:T(8,128)(2,1)S(1)} %reshape.194) | copy-start | bytes 73732
  126.4 13.4 %all-to-all-start.1 = ((bf16[16,8,96]{2,1,0:T(8,128)(2,1)}), bf16[16,8,96]{2,1,0:T(8,128)(2,1)S(1)}, u32[]{:S(2)}, u32[]{:S(2)}) async-start(bf16[16,8,96]{2,1,0:T(8,128)(2,1)} %bitcast.13), calls=%async_computation.1 | async-start | bytes 65536 | tf_op jit(solution)/shard_map/all_to_all | solution.py:287
  140.0 1.4 copy-start.1
  142.4 11.7 %all-to-all-start.2 = ((bf16[8,16,96]{2,0,1:T(8,128)(2,1)}), bf16[8,16,96]{2,0,1:T(8,128)(2,1)}, u32[]{:S(2)}, u32[]{:S(2)}) async-start(bf16[8,16,96]{2,0,1:T(8,128)(2,1)} %copy.74), calls=%async_computation.2 | async-start | bytes 65536 | tf_op jit(solution)/shard_map/all_to_all | solution.py:297
  154.1 16.1 %all-to-all-start.3 = ((bf16[32,4,96]{2,1,0:T(4,128)(2,1)}), bf16[32,4,96]{2,1,0:T(4,128)(2,1)S(1)}, u32[]{:S(2)}, u32[]{:S(2)}) async-start(bf16[32,4,96]{2,1,0:T(4,128)(2,1)} %bitcast.18), calls=%async_computation.3 | async-start | bytes 65536 | tf_op jit(solution)/shard_map/all_to_all | solution.py:300

commit v4 on v3

--- a/solution.py
+++ b/solution.py
@@ -179,6 +179,178 @@
         if high != low and high < count:
             route += [(low, high), (high, low)]
     return lax.ppermute(block, axis, route)
+
+
+def expert_kernel(
+    n_ep, n_grp, width, mixed_ref, gain_ref, picker_ref, combine_ref, up_ref, down_ref,
+    out_ref, squares, outgoing, incoming, results, returned,
+    s_sq, r_sq, s_out, r_in, s_res, r_ret,
+):
+    g = lax.axis_index("grp")
+    e = lax.axis_index("ep")
+    home = g // 2
+    serving = home == e
+    barrier = pltpu.get_barrier_semaphore()
+    for peer in range(n_ep):
+        @pl.when(e != peer)
+        def _():
+            pl.semaphore_signal(barrier, inc=1, device_id=(g, peer), device_id_type=MESH)
+    for expert in range(n_grp):
+        @pl.when(jnp.logical_not(serving & (g == expert)))
+        def _():
+            pl.semaphore_signal(barrier, inc=1, device_id=(expert, home), device_id_type=MESH)
+    for half in range(2):
+        for peer in range(n_ep):
+            @pl.when(jnp.logical_not(serving & (g == 2 * e + half) & (e == peer)))
+            def _():
+                pl.semaphore_signal(
+                    barrier, inc=1, device_id=(2 * e + half, peer), device_id_type=MESH
+                )
+
+    @pl.when(serving)
+    def _():
+        pl.semaphore_wait(barrier, n_ep - 1 + 2 * (2 * n_ep - 1))
+
+    @pl.when(jnp.logical_not(serving))
+    def _():
+        pl.semaphore_wait(barrier, n_ep - 1 + 2 * 2 * n_ep)
+
+    mixed = mixed_ref[...]
+    own_sum = jnp.sum(mixed * mixed, axis=1, keepdims=True)
+    squares[e] = jnp.broadcast_to(own_sum, squares.shape[1:])
+
+    def sq_copy(peer):
+        return pltpu.make_async_remote_copy(
+            src_ref=squares.at[e], dst_ref=squares.at[e], send_sem=s_sq.at[peer],
+            recv_sem=r_sq.at[e], device_id=(g, peer), device_id_type=MESH)
+
+    def sq_arrival(peer):
+        return pltpu.make_async_remote_copy(
+            src_ref=squares.at[peer], dst_ref=squares.at[peer], send_sem=s_sq.at[peer],
+            recv_sem=r_sq.at[peer], device_id=(g, peer), device_id_type=MESH)
+
+    for peer in range(n_ep):
+        @pl.when(e != peer)
+        def _():
+            sq_copy(peer).start()
+    for peer in range(n_ep):
+        @pl.when(e != peer)
+        def _():
+            sq_arrival(peer).wait_recv()
+    total = jnp.sum(squares[...][:, :, 0:1], axis=0)
+    normed = (mixed * lax.rsqrt(total / width + norm_epsilon) * gain_ref[...]).astype(jnp.bfloat16)
+    slots = outgoing.shape[1]
+    picked = jnp.dot(picker_ref[...], normed, preferred_element_type=jnp.float32)
+    outgoing[...] = picked.reshape(outgoing.shape)
+
+    def dispatch(expert):
+        return pltpu.make_async_remote_copy(
+            src_ref=outgoing.at[expert], dst_ref=incoming.at[e, g % 2], send_sem=s_out.at[expert],
+            recv_sem=r_in.at[g % 2, e], device_id=(expert, home), device_id_type=MESH)
+
+    for expert in range(n_grp):
+        @pl.when(jnp.logical_not(serving & (g == expert)))
+        def _():
+            dispatch(expert).start()
+
+    @pl.when(serving)
+    def _():
+        incoming[e, g % 2] = outgoing[g]
+
+    def gathered(half, peer):
+        return pltpu.make_async_remote_copy(
+            src_ref=outgoing.at[0], dst_ref=incoming.at[peer, half], send_sem=s_out.at[0],
+            recv_sem=r_in.at[half, peer], device_id=(2 * e + half, peer), device_id_type=MESH)
+
+    for half in range(2):
+        for peer in range(n_ep):
+            @pl.when(jnp.logical_not(serving & (g == 2 * e + half) & (e == peer)))
+            def _():
+                gathered(half, peer).wait_recv()
+
+    pre = jnp.zeros((2 * slots, up_ref.shape[1]), jnp.float32)
+    for peer in range(n_ep):
+        lhs = incoming[peer].reshape(2 * slots, width // n_ep).astype(jnp.bfloat16)
+        pre = pre + jnp.dot(
+            lhs, up_ref[peer * (width // n_ep):(peer + 1) * (width // n_ep), :],
+            preferred_element_type=jnp.float32)
+    hidden_units = up_ref.shape[1] // 2
+    gate = pre[:, :hidden_units]
+    act = (gate / (1.0 + jnp.exp(-gate)) * pre[:, hidden_units:]).astype(jnp.bfloat16)
+    for peer in range(n_ep):
+        piece = jnp.dot(act, down_ref[peer], preferred_element_type=jnp.float32)
+        results[peer] = piece.astype(jnp.bfloat16).astype(jnp.float32).reshape(results.shape[1:])
+
+    def give_back(half, peer):
+        return pltpu.make_async_remote_copy(
+            src_ref=results.at[peer, half], dst_ref=returned.at[g], send_sem=s_res.at[half, peer],
+            recv_sem=r_ret.at[g], device_id=(2 * e + half, peer), device_id_type=MESH)
+
+    for half in range(2):
+        for peer in range(n_ep):
+            @pl.when(jnp.logical_not(serving & (g == 2 * e + half) & (e == peer)))
+            def _():
+                give_back(half, peer).start()
+
+    @pl.when(serving)
+    def _():
+        returned[g] = results[e, g % 2]
+
+    def coming_back(expert):
+        return pltpu.make_async_remote_copy(
+            src_ref=results.at[0, 0], dst_ref=returned.at[expert], send_sem=s_res.at[0, 0],
+            recv_sem=r_ret.at[expert], device_id=(expert, home), device_id_type=MESH)
+
+    for expert in range(n_grp):
+        @pl.when(jnp.logical_not(serving & (g == expert)))
+        def _():
+            coming_back(expert).wait_recv()
+
+    back = returned[...].reshape(n_grp * slots, width // n_ep).astype(jnp.bfloat16)
+    mix = jnp.dot(combine_ref[...], back, preferred_element_type=jnp.float32)
+    out_ref[...] = (mixed + mix).astype(out_ref.dtype)
+
+    for peer in range(n_ep):
+        @pl.when(e != peer)
+        def _():
+            sq_copy(peer).wait_send()
+    for expert in range(n_grp):
+        @pl.when(jnp.logical_not(serving & (g == expert)))
+        def _():
+            dispatch(expert).wait_send()
+    for half in range(2):
+        for peer in range(n_ep):
+            @pl.when(jnp.logical_not(serving & (g == 2 * e + half) & (e == peer)))
+            def _():
+                give_back(half, peer).wait_send()
+
+
+def expert_call(mixed, gain, picker, combine, up, down_parts):
+    n_ep = lax.axis_size("ep")
+    n_grp = lax.axis_size("grp")
+    rows, share = mixed.shape
+    slots = picker.shape[0] // n_grp
+    width = share * n_ep
+    return pl.pallas_call(
+        functools.partial(expert_kernel, n_ep, n_grp, width),
+        out_shape=jax.ShapeDtypeStruct((rows, share), jnp.bfloat16),
+        in_specs=[pl.BlockSpec(memory_space=pltpu.VMEM)] * 6,
+        out_specs=pl.BlockSpec(memory_space=pltpu.VMEM),
+        scratch_shapes=[
+            pltpu.VMEM((n_ep, rows, 128), jnp.float32),
+            pltpu.VMEM((n_grp, slots, share), jnp.float32),
+            pltpu.VMEM((n_ep, 2, slots, share), jnp.float32),
+            pltpu.VMEM((n_ep, 2, slots, share), jnp.float32),
+            pltpu.VMEM((n_grp, slots, share), jnp.float32),
+            pltpu.SemaphoreType.DMA((n_ep,)),
+            pltpu.SemaphoreType.DMA((n_ep,)),
+            pltpu.SemaphoreType.DMA((n_grp,)),
+            pltpu.SemaphoreType.DMA((2, n_ep)),
+            pltpu.SemaphoreType.DMA((2, n_ep)),
+            pltpu.SemaphoreType.DMA((n_grp,)),
+        ],
+        compiler_params=pltpu.CompilerParams(collective_id=1, has_side_effects=True),
+    )(mixed, gain, picker, combine, up, down_parts)
 
 
 def per_device(
@@ -263,48 +435,29 @@
     projected = jnp.dot(attn_out, weight_columns, preferred_element_type=jnp.float32)
     feature_share = hidden.shape[1]
     mixed = hidden.astype(jnp.float32) + projected
-    squares = lax.psum(jnp.sum(mixed * mixed, -1), "ep")
-    normed = (mixed * lax.rsqrt(squares / D + norm_epsilon)[:, None] * norm_gain).astype(
-        jnp.bfloat16
-    )
-    capacity = min(row_count, 2 * row_count * TOP // group_count)
     expert_ids = jnp.arange(group_count, dtype=jnp.int32)
-    flat_routes = routes.reshape(-1)
-    hits = (flat_routes[:, None] == expert_ids[None, :]).astype(jnp.int32)
-    earlier_hits = jnp.cumsum(hits, 0) - hits
-    position = jnp.sum(earlier_hits * hits, 1)
-    slot_index = flat_routes * capacity + position
-    slots_all = jnp.arange(group_count * capacity, dtype=jnp.int32)
-    picker = jnp.any(
-        slot_index.reshape(row_count, TOP)[None, :, :] == slots_all[:, None, None], 2
-    ).astype(jnp.bfloat16)
-    sender = (
-        jnp.dot(picker, normed, preferred_element_type=jnp.float32)
+    named = routes[:, :, None] == expert_ids[None, None, :]
+    chosen = jnp.any(named, 1).astype(jnp.int32)
+    weight_at = jnp.sum(
+        jnp.where(named, route_weight.astype(jnp.float32)[:, :, None], 0.0), 1
+    )
+    position = jnp.cumsum(chosen, 0) - chosen
+    slot_ids = jnp.arange(row_count, dtype=jnp.int32)
+    placed = (chosen[:, :, None] == 1) & (position[:, :, None] == slot_ids[None, None, :])
+    picker = (
+        placed.transpose(1, 2, 0).reshape(group_count * row_count, row_count).astype(jnp.bfloat16)
+    )
+    combine = (
+        jnp.where(placed, weight_at[:, :, None], 0.0)
+        .reshape(row_count, group_count * row_count)
         .astype(jnp.bfloat16)
-        .reshape(group_count, capacity, feature_share)
-    )
-    arrived = lax.all_to_all(sender, "grp", split_axis=0, concat_axis=0, tiled=True)
-    whole_rows = lax.all_to_all(
-        arrived.reshape(group_count * capacity, feature_share),
-        "ep",
-        split_axis=0,
-        concat_axis=1,
-        tiled=True,
-    )
-    pre_sum = jnp.dot(whole_rows, gate_up[0], preferred_element_type=jnp.float32)
-    activated = (jax.nn.silu(pre_sum[:, :FF]) * pre_sum[:, FF:]).astype(jnp.bfloat16)
-    result = jnp.dot(activated, down[0], preferred_element_type=jnp.float32).astype(jnp.bfloat16)
-    served = lax.all_to_all(result, "ep", split_axis=1, concat_axis=0, tiled=True).reshape(
-        group_count, capacity, feature_share
-    )
-    returned_rows = lax.all_to_all(served, "grp", split_axis=0, concat_axis=0, tiled=True)
-    gathered_rows = returned_rows.reshape(group_count * capacity, feature_share)[
-        slot_index
-    ].reshape(row_count, TOP, feature_share)
-    expert_mix = jnp.sum(
-        route_weight.astype(jnp.float32)[:, :, None] * gathered_rows.astype(jnp.float32), 1
-    )
-    layer_out = (mixed + expert_mix).astype(jnp.bfloat16)
+    )
+    down_parts = (
+        down[0].reshape(FF, lax.axis_size("ep"), feature_share).transpose(1, 0, 2)
+    )
+    layer_out = expert_call(
+        mixed, norm_gain.reshape(1, feature_share), picker, combine, gate_up[0], down_parts
+    )
     return (layer_out, attn_out)
 
 

time: 173 us -> 119 us (0.69)
  the two profiles are of different devices: /device:TPU:1 before, /device:TPU:31 now
where the time goes in v4:
time: 119 us; the launch traced here: 118 us
  Pallas kernels  93.8 us (79%)
  local copies, waits for them, and re-layouts  11.3 us (9%)
  other arithmetic  6.88 us (6%)
  starting transfers between devices  2.59 us (2%)
  matrix products  2.47 us (2%)
    pallas_call x1, Pallas kernels, expert_call(): pl.pallas_call(functools.partial(expert_kernel, n_ep, n_grp, width), out_...  57.8 us
    pallas_call x1, Pallas kernels, merge_call(): pl.pallas_call(functools.partial(merge_kernel, rows, n_ep, n_grp), out_sh...  36 us
    unnamed x20, local copies, waits for them, and re-layouts  3 us
    ppermute x1, starting transfers between devices, from_partner(): return lax.ppermute(block, axis, route)  2.59 us
    another operation x1, local copies, waits for them, and re-layouts, per_device(): down[0].reshape(FF, lax.axis_size('ep'), feature_share).transpose(1, 0, 2)  2.45 us
  transfers between devices with their start and end apart: 1, of which 0 were waited for; matrix products, arithmetic and copies ran while one was open for 12% of the time, Pallas kernels for 0%

profile of v4, /device:TPU:31, one launch (start us, length us, event | category | flops | bytes accessed | tf_op | source)
XLA Modules:
  0.0 118.0 jit_solution(4206987084353771744)
XLA Ops:
  0.7 2.6 %collective-permute-start = (bf16[8,1536]{1,0:T(8,128)(2,1)}, bf16[8,1536]{1,0:T(8,128)(2,1)S(1)}, u32[]{:S(2)}, u32[]{:S(2)}) collective-permute-start(bf16[8,1536]{1,0:T(8,128)(2,1)} %param.14), channel_id=1, source_target_pairs={{0,16},{16,0},{32,48},{48,32},{64,80},{80,64},{96,112},{112,96},{1... | collective-permute-start | bytes 73736 | tf_op jit(solution)/shard_map/ppermute | solution.py:181
  3.3 0.8 slice_reduce_fusion
  4.0 0.8 convert_reduce_fusion
  4.8 0.9 reshape.164
  5.8 0.8 fusion.10
  6.6 0.7 iota_compare_fusion.1
  7.3 0.7 convert_element_type.49
  8.0 0.8 select_reduce_fusion.1
  9.8 0.1 and.46
  10.1 0.1 broadcast_in_dim.79
  10.2 0.2 fusion.13
  10.4 0.1 copy.81
  10.6 0.2 copy.75
  11.1 0.7 fusion.8.picker_ref
  11.8 0.6 select_convert_fusion.combine_ref
  12.4 0.7 maximum_maximum_fusion.1.own_ref
  13.2 0.1 copy.61
  13.3 0.9 copy.63
  14.2 0.7 copy.78
  14.9 2.4 %copy.79 = bf16[512,16,96]{2,0,1:T(8,128)(2,1)} copy(bf16[512,16,96]{0,2,1:T(8,128)(2,1)S(1)} %bitcast.47) | data formatting | bytes 3145728 | tf_op jit(solution)/shard_map/reshape;squeeze | solution.py:456
  17.4 0.2 reshape.157
  17.6 0.3 select_reduce_fusion
  18.0 0.2 fusion
  18.5 0.2 copy.71
  18.7 0.2 copy.72
  19.0 0.3 fusion.2
  19.4 0.8 maximum_maximum_fusion.part_ref
  20.3 36.0 %shard_map.140 = (bf16[8,24,64]{2,1,0:T(8,128)(2,1)}, bf16[32,48,96]{2,1,0:T(8,128)(2,1)}) custom-call(f32[16,24,128]{2,1,0:T(8,128)} %maximum_maximum_fusion.part_ref, f32[8,24,128]{2,1,0:T(8,128)} %maximum_maximum_fusion.1.own_ref, bf16[48,96]{1,0:T(8,128)(2,1)} %block_ref.1), custom_call_target="tpu_custom_call" | custom-call | tf_op jit(solution)/shard_map/pallas_call | solution.py:149
  56.3 0.9 reshape.165
  57.2 1.8 %convolution_add_fusion.mixed_ref = f32[8,96]{1,0:T(8,128)} fusion(bf16[8,1536]{1,0:T(8,128)(2,1)S(1)} %reshape.165, bf16[1536,96]{1,0:T(8,128)(2,1)} %bitcast.55, bf16[8,96]{1,0:T(8,128)(2,1)S(1)} %copy-done.7), kind=kOutput, calls=%fused_computation.1 | convolution fusion | flops 2360832 | bytes 324096 | tf_op jit(solution)/shard_map/dot_general | solution.py:435
  58.9 57.8 %shard_map.141 = bf16[8,96]{1,0:T(8,128)(2,1)} custom-call(f32[8,96]{1,0:T(8,128)} %convolution_add_fusion.mixed_ref, f32[1,96]{1,0:T(1,128)} %bitcast.60, bf16[256,8]{1,0:T(8,128)(2,1)} %fusion.8.picker_ref, bf16[8,256]{1,0:T(8,128)(2,1)} %select_convert_fusion.combine_ref, bf16[1536,1024]{1,0:T(8,128)(2,1)} %bitcast.48, bf16[16,512,96]{2,1,0:T(8,128)(2,1)} %bitcast.46), custom_call_target="tpu_custom_call" | custom-call | tf_op jit(solution)/shard_map/pallas_call | solution.py:334
  116.8 1.3 %copy.87 = bf16[8,96]{1,0:T(8,128)(2,1)} copy(bf16[8,96]{1,0:T(8,128)(2,1)} %shard_map.141) | data formatting | bytes 3072
  (61 shorter events, 2.2 us)
Async XLA Ops:
  0.6 8.3 %copy-start = (s32[12]{0:T(128)S(1)}, s32[12]{0:T(128)}, u32[]{:S(2)}) copy-start(s32[12]{0:T(128)} %param.19) | copy-start | bytes 148
  0.6 12.5 %copy-start.3 = (bf16[192,512]{1,0:T(8,128)(2,1)S(1)}, bf16[192,512]{1,0:T(8,128)(2,1)}, u32[]{:S(2)}) copy-start(bf16[192,512]{1,0:T(8,128)(2,1)} %param.16) | copy-start | bytes 589828
  0.7 12.7 %copy-start.4 = (bf16[192,512]{1,0:T(8,128)(2,1)S(1)}, bf16[192,512]{1,0:T(8,128)(2,1)}, u32[]{:S(2)}) copy-start(bf16[192,512]{1,0:T(8,128)(2,1)} %param.17) | copy-start | bytes 589828
  0.7 13.5 %copy-start.1 = (bf16[1,512,1536]{2,1,0:T(8,128)(2,1)S(1)}, bf16[1,512,1536]{2,1,0:T(8,128)(2,1)}, u32[]{:S(2)}) copy-start(bf16[1,512,1536]{2,1,0:T(8,128)(2,1)} %param.23) | copy-start | bytes 4718596
  0.7 16.7 %collective-permute-start = (bf16[8,1536]{1,0:T(8,128)(2,1)}, bf16[8,1536]{1,0:T(8,128)(2,1)S(1)}, u32[]{:S(2)}, u32[]{:S(2)}) collective-permute-start(bf16[8,1536]{1,0:T(8,128)(2,1)} %param.14), channel_id=1, source_target_pairs={{0,16},{16,0},{32,48},{48,32},{64,80},{80,64},{96,112},{112,96},{1... | collective-permute-start | bytes 73736 | tf_op jit(solution)/shard_map/ppermute | solution.py:181
  14.9 2.5 %copy-start.6 = (bf16[8,1536]{1,0:T(8,128)(2,1)S(1)}, bf16[8,1536]{1,0:T(8,128)(2,1)}, u32[]{:S(2)}) copy-start(bf16[8,1536]{1,0:T(8,128)(2,1)} %param.14) | copy-start | bytes 73732
  17.4 1.6 %copy-start.2 = (bf16[192,512]{0,1:T(8,128)(2,1)S(1)}, bf16[192,512]{0,1:T(8,128)(2,1)}, u32[]{:S(2)}) copy-start(bf16[192,512]{0,1:T(8,128)(2,1)} %copy.63) | copy-start | bytes 589828
  18.0 39.2 %copy-start.7 = (bf16[8,96]{1,0:T(8,128)(2,1)S(1)}, bf16[8,96]{1,0:T(8,128)(2,1)}, u32[]{:S(2)}) copy-start(bf16[8,96]{1,0:T(8,128)(2,1)} %param.13) | copy-start | bytes 4612
  57.2 59.6 %copy-start.5 = (bf16[8,1536]{1,0:T(8,128)(2,1)}, bf16[8,1536]{1,0:T(8,128)(2,1)S(1)}, u32[]{:S(2)}) copy-start(bf16[8,1536]{1,0:T(8,128)(2,1)S(1)} %reshape.165) | copy-start | bytes 73732

commit v5 on v4

v5 whole, which is shorter than its diff:
```python
import jax
import jax.numpy as jnp
from jax import lax
from jax.experimental import pallas as pl
from jax.experimental.pallas import tpu as pltpu
from jax.sharding import PartitionSpec as P
import functools

D = 1536
HEADS = 24
KV_HEADS = 8
HD = 64
FF = 512
TOP = 8


masked_score = -1e30
norm_epsilon = 1e-05

MESH = pl.DeviceIdType.MESH


def layer_kernel(
    rows, n_ep, n_grp, width,
    part_ref, own_ref, block_ref, hidden_ref, gain_ref, picker_ref, combine_ref, up_ref, down_ref,
    out_ref, attn_ref,
    got, final, blocks, squares, outgoing, incoming, results, returned,
    s1, r1, s2, r2, s3, r3, s_sq, r_sq, s_out, r_in, s_res, r_ret,
):
    g = lax.axis_index("grp")
    e = lax.axis_index("ep")
    mate = g + 1 - 2 * (g % 2)
    home = g // 2
    serving = home == e
    share = width // n_ep
    barrier = pltpu.get_barrier_semaphore()
    for peer in range(n_ep):
        @pl.when(e != peer)
        def _():
            pl.semaphore_signal(barrier, inc=1, device_id=(g, peer), device_id_type=MESH)
            pl.semaphore_signal(barrier, inc=1, device_id=(g, peer), device_id_type=MESH)
        pl.semaphore_signal(barrier, inc=1, device_id=(mate, peer), device_id_type=MESH)
    for step in range(1, n_grp):
        pl.semaphore_signal(
            barrier, inc=1, device_id=(lax.rem(g + step, n_grp), e), device_id_type=MESH
        )
    for expert in range(n_grp):
        @pl.when(jnp.logical_not(serving & (g == expert)))
        def _():
            pl.semaphore_signal(barrier, inc=1, device_id=(expert, home), device_id_type=MESH)
    for half in range(2):
        for peer in range(n_ep):
            @pl.when(jnp.logical_not(serving & (g == 2 * e + half) & (e == peer)))
            def _():
                pl.semaphore_signal(
                    barrier, inc=1, device_id=(2 * e + half, peer), device_id_type=MESH
                )
    common = 2 * (n_ep - 1) + n_ep + n_grp - 1

    @pl.when(serving)
    def _():
        pl.semaphore_wait(barrier, common + n_grp - 1 + 2 * n_ep - 1)

    @pl.when(jnp.logical_not(serving))
    def _():
        pl.semaphore_wait(barrier, common + n_grp + 2 * n_ep)

    def first(row):
        if row < rows:
            target = (g, row)
            slot = e
        else:
            target = (mate, row - rows)
            slot = n_ep + e
        return pltpu.make_async_remote_copy(
            src_ref=part_ref.at[row], dst_ref=got.at[slot], send_sem=s1.at[row],
            recv_sem=r1.at[slot], device_id=target, device_id_type=MESH)

    for row in range(2 * rows):
        if row < rows:
            @pl.when(e != row)
            def _():
                first(row).start()

            @pl.when(e == row)
            def _():
                got[e] = part_ref[row]
        else:
            first(row).start()

    def spread(step):
        return pltpu.make_async_remote_copy(
            src_ref=block_ref, dst_ref=blocks.at[g], send_sem=s3.at[step],
            recv_sem=r3.at[g], device_id=(lax.rem(g + step, n_grp), e), device_id_type=MESH)

    def gathered_block(step):
        source = lax.rem(g + n_grp - step, n_grp)
        return pltpu.make_async_remote_copy(
            src_ref=block_ref, dst_ref=blocks.at[source], send_sem=s3.at[step],
            recv_sem=r3.at[source], device_id=(source, e), device_id_type=MESH)

    for step in range(1, n_grp):
        spread(step).start()
    blocks[g] = block_ref[...]

    def incoming_part(slot):
        return pltpu.make_async_remote_copy(
            src_ref=part_ref.at[0], dst_ref=got.at[slot], send_sem=s1.at[0],
            recv_sem=r1.at[slot], device_id=(g, 0), device_id_type=MESH)

    def second(target):
        return pltpu.make_async_remote_copy(
            src_ref=final.at[e], dst_ref=final.at[e], send_sem=s2.at[target],
            recv_sem=r2.at[e], device_id=(g, target), device_id_type=MESH)

    @pl.when(e < rows)
    def _():
        for slot in range(2 * n_ep):
            if slot < n_ep:
                @pl.when(e != slot)
                def _():
                    incoming_part(slot).wait_recv()
            else:
                incoming_part(slot).wait_recv()
        stack = got[...]
        own = own_ref[e]
        maxes = jnp.maximum(jnp.max(stack[:, 1:2, :], 0), own[1:2, :])
        factors = jnp.exp(stack[:, 1:2, :] - maxes[None])
        own_factor = jnp.exp(own[1:2, :] - maxes)
        total = jnp.sum(stack[:, 2:3, :] * factors, 0) + own_factor
        accum = jnp.sum(stack[:, 0:1, :] * factors, 0) + own[0:1, :] * own_factor
        final[e] = (accum / total).astype(jnp.bfloat16).astype(jnp.float32)
        for target in range(n_ep):
            @pl.when(e != target)
            def _():
                second(target).start()

    def arriving(row):
        return pltpu.make_async_remote_copy(
            src_ref=final.at[row], dst_ref=final.at[row], send_sem=s2.at[0],
            recv_sem=r2.at[row], device_id=(g, row), device_id_type=MESH)

    for row in range(rows):
        @pl.when(e != row)
        def _():
            arriving(row).wait_recv()

    row_ids = lax.broadcasted_iota(jnp.int32, (rows, width), 0)
    attn = jnp.zeros((rows, width), jnp.float32)
    for row in range(rows):
        attn = jnp.where(row_ids == row, jnp.broadcast_to(final[row], (rows, width)), attn)
    attn = attn.astype(jnp.bfloat16)
    attn_ref[...] = attn

    for step in range(1, n_grp):
        gathered_block(step).wait_recv()
    columns = blocks[...].reshape(n_grp * blocks.shape[1], share)
    projected = jnp.dot(attn, columns, preferred_element_type=jnp.float32)
    mixed = hidden_ref[...].astype(jnp.float32) + projected

    own_sum = jnp.sum(mixed * mixed, axis=1, keepdims=True)
    squares[e] = jnp.broadcast_to(own_sum, squares.shape[1:])

    def sq_copy(peer):
        return pltpu.make_async_remote_copy(
            src_ref=squares.at[e], dst_ref=squares.at[e], send_sem=s_sq.at[peer],
            recv_sem=r_sq.at[e], device_id=(g, peer), device_id_type=MESH)

    def sq_arrival(peer):
        return pltpu.make_async_remote_copy(
            src_ref=squares.at[peer], dst_ref=squares.at[peer], send_sem=s_sq.at[peer],
            recv_sem=r_sq.at[peer], device_id=(g, peer), device_id_type=MESH)

    for peer in range(n_ep):
        @pl.when(e != peer)
        def _():
            sq_copy(peer).start()
    for peer in range(n_ep):
        @pl.when(e != peer)
        def _():
            sq_arrival(peer).wait_recv()
    total_sq = jnp.sum(squares[...][:, :, 0:1], axis=0)
    normed = (mixed * lax.rsqrt(total_sq / width + norm_epsilon) * gain_ref[...]).astype(jnp.bfloat16)
    slots = outgoing.shape[1]
    picked = jnp.dot(picker_ref[...], normed, preferred_element_type=jnp.float32)
    outgoing[...] = picked.reshape(outgoing.shape)

    def dispatch(expert):
        return pltpu.make_async_remote_copy(
            src_ref=outgoing.at[expert], dst_ref=incoming.at[e, g % 2], send_sem=s_out.at[expert],
            recv_sem=r_in.at[g % 2, e], device_id=(expert, home), device_id_type=MESH)

    for expert in range(n_grp):
        @pl.when(jnp.logical_not(serving & (g == expert)))
        def _():
            dispatch(expert).start()

    @pl.when(serving)
    def _():
        incoming[e, g % 2] = outgoing[g]

    def gathered(half, peer):
        return pltpu.make_async_remote_copy(
            src_ref=outgoing.at[0], dst_ref=incoming.at[peer, half], send_sem=s_out.at[0],
            recv_sem=r_in.at[half, peer], device_id=(2 * e + half, peer), device_id_type=MESH)

    for half in range(2):
        for peer in range(n_ep):
            @pl.when(jnp.logical_not(serving & (g == 2 * e + half) & (e == peer)))
            def _():
                gathered(half, peer).wait_recv()

    pre = jnp.zeros((2 * slots, up_ref.shape[1]), jnp.float32)
    for peer in range(n_ep):
        lhs = incoming[peer].reshape(2 * slots, share).astype(jnp.bfloat16)
        pre = pre + jnp.dot(
            lhs, up_ref[peer * share:(peer + 1) * share, :], preferred_element_type=jnp.float32)
    hidden_units = up_ref.shape[1] // 2
    gate = pre[:, :hidden_units]
    act = (gate / (1.0 + jnp.exp(-gate)) * pre[:, hidden_units:]).astype(jnp.bfloat16)
    for peer in range(n_ep):
        piece = jnp.dot(act, down_ref[peer], preferred_element_type=jnp.float32)
        results[peer] = piece.astype(jnp.bfloat16).astype(jnp.float32).reshape(results.shape[1:])

    def give_back(half, peer):
        return pltpu.make_async_remote_copy(
            src_ref=results.at[peer, half], dst_ref=returned.at[g], send_sem=s_res.at[half, peer],
            recv_sem=r_ret.at[g], device_id=(2 * e + half, peer), device_id_type=MESH)

    for half in range(2):
        for peer in range(n_ep):
            @pl.when(jnp.logical_not(serving & (g == 2 * e + half) & (e == peer)))
            def _():
                give_back(half, peer).start()

    @pl.when(serving)
    def _():
        returned[g] = results[e, g % 2]

    def coming_back(expert):
        return pltpu.make_async_remote_copy(
            src_ref=results.at[0, 0], dst_ref=returned.at[expert], send_sem=s_res.at[0, 0],
            recv_sem=r_ret.at[expert], device_id=(expert, home), device_id_type=MESH)

    for expert in range(n_grp):
        @pl.when(jnp.logical_not(serving & (g == expert)))
        def _():
            coming_back(expert).wait_recv()

    back = returned[...].reshape(n_grp * slots, share).astype(jnp.bfloat16)
    mix = jnp.dot(combine_ref[...], back, preferred_element_type=jnp.float32)
    out_ref[...] = (mixed + mix).astype(out_ref.dtype)

    for row in range(2 * rows):
        if row < rows:
            @pl.when(e != row)
            def _():
                first(row).wait_send()
        else:
            first(row).wait_send()

    @pl.when(e < rows)
    def _():
        for target in range(n_ep):
            @pl.when(e != target)
            def _():
                second(target).wait_send()

    for step in range(1, n_grp):
        spread(step).wait_send()
    for peer in range(n_ep):
        @pl.when(e != peer)
        def _():
            sq_copy(peer).wait_send()
    for expert in range(n_grp):
        @pl.when(jnp.logical_not(serving & (g == expert)))
        def _():
            dispatch(expert).wait_send()
    for half in range(2):
        for peer in range(n_ep):
            @pl.when(jnp.logical_not(serving & (g == 2 * e + half) & (e == peer)))
            def _():
                give_back(half, peer).wait_send()


def layer_call(part, own, block, hidden, gain, picker, combine, up, down_parts):
    n_ep = lax.axis_size("ep")
    n_grp = lax.axis_size("grp")
    rows, share = hidden.shape
    width = share * n_ep
    slots = picker.shape[0] // n_grp
    return pl.pallas_call(
        functools.partial(layer_kernel, rows, n_ep, n_grp, width),
        out_shape=(
            jax.ShapeDtypeStruct((rows, share), jnp.bfloat16),
            jax.ShapeDtypeStruct((rows, width), jnp.bfloat16),
        ),
        in_specs=[pl.BlockSpec(memory_space=pltpu.VMEM)] * 9,
        out_specs=(pl.BlockSpec(memory_space=pltpu.VMEM),) * 2,
        scratch_shapes=[
            pltpu.VMEM((2 * n_ep,) + part.shape[1:], jnp.float32),
            pltpu.VMEM((rows, 1, width), jnp.float32),
            pltpu.VMEM((n_grp,) + block.shape, block.dtype),
            pltpu.VMEM((n_ep, rows, 128), jnp.float32),
            pltpu.VMEM((n_grp, slots, share), jnp.float32),
            pltpu.VMEM((n_ep, 2, slots, share), jnp.float32),
            pltpu.VMEM((n_ep, 2, slots, share), jnp.float32),
            pltpu.VMEM((n_grp, slots, share), jnp.float32),
            pltpu.SemaphoreType.DMA((2 * rows,)),
            pltpu.SemaphoreType.DMA((2 * n_ep,)),
            pltpu.SemaphoreType.DMA((n_ep,)),
            pltpu.SemaphoreType.DMA((rows,)),
            pltpu.SemaphoreType.DMA((n_grp,)),
            pltpu.SemaphoreType.DMA((n_grp,)),
            pltpu.SemaphoreType.DMA((n_ep,)),
            pltpu.SemaphoreType.DMA((n_ep,)),
            pltpu.SemaphoreType.DMA((n_grp,)),
            pltpu.SemaphoreType.DMA((2, n_ep)),
            pltpu.SemaphoreType.DMA((2, n_ep)),
            pltpu.SemaphoreType.DMA((n_grp,)),
        ],
        compiler_params=pltpu.CompilerParams(collective_id=0, has_side_effects=True),
    )(part, own, block, hidden, gain, picker, combine, up, down_parts)


def from_partner(block, axis, apart):
    count = lax.axis_size(axis)
    route = []
    for low in range(count):
        high = low | 1 << apart
        if high != low and high < count:
            route += [(low, high), (high, low)]
    return lax.ppermute(block, axis, route)


def per_device(
    hidden,
    query,
    new_kv,
    key_cache,
    value_cache,
    page_owner,
    page_fill,
    out_weight,
    norm_gain,
    gate_up,
    down,
    routes,
    route_weight,
):
    row_count = query.shape[0]
    group_count = lax.axis_size("grp")
    head_group = HEADS // KV_HEADS
    page_count = page_owner.shape[0]
    token_count = key_cache.shape[0]
    page_length = token_count // page_count
    both_rows = 2 * row_count
    scale = HD ** (-0.5)
    partner_query = from_partner(query, "grp", 0)
    all_queries = jnp.concatenate([query, partner_query], 0)
    query_heads = (
        all_queries.reshape(both_rows, KV_HEADS, head_group, HD)
        .transpose(1, 0, 2, 3)
        .reshape(KV_HEADS, both_rows * head_group, HD)
    )
    key_heads = key_cache.reshape(token_count, KV_HEADS, HD)
    value_heads = value_cache.reshape(token_count, KV_HEADS, HD)
    scores = (
        jnp.einsum("kqd,tkd->kqt", query_heads, key_heads, preferred_element_type=jnp.float32)
        * scale
    )
    scores = scores.reshape(KV_HEADS, both_rows, head_group, token_count)
    row_index = jnp.arange(both_rows, dtype=jnp.int32)
    in_page = jnp.arange(page_length, dtype=jnp.int32)
    usable = (page_owner[None, :, None] == row_index[:, None, None]) & (
        in_page[None, None, :] < page_fill[None, :, None]
    )
    usable = usable.reshape(both_rows, token_count)[None, :, None, :]
    local_top = jnp.max(jnp.where(usable, scores, masked_score), -1)
    weights = jnp.where(usable, jnp.exp(scores - local_top[..., None]), 0.0)
    local_total = jnp.sum(weights, -1)
    rounded = weights.astype(jnp.bfloat16).reshape(KV_HEADS, both_rows * head_group, token_count)
    local_accum = jnp.einsum(
        "kqt,tkd->kqd", rounded, value_heads, preferred_element_type=jnp.float32
    )
    part_max = local_top.transpose(1, 0, 2).reshape(both_rows, HEADS)
    part_total = local_total.transpose(1, 0, 2).reshape(both_rows, HEADS)
    part_accum = (
        local_accum.reshape(KV_HEADS, both_rows, head_group, HD)
        .transpose(1, 0, 2, 3)
        .reshape(both_rows, HEADS, HD)
    )
    own_query = query.reshape(row_count, KV_HEADS, head_group, HD)
    fresh_key = new_kv[:, 0].reshape(row_count, KV_HEADS, HD)
    fresh_value = new_kv[:, 1].astype(jnp.float32).reshape(row_count, KV_HEADS, HD)
    own_score = (
        jnp.einsum(
            "rkgd,rkd->rkg", own_query, fresh_key, preferred_element_type=jnp.float32
        ).reshape(row_count, HEADS)
        * scale
    )
    value_rows = jnp.broadcast_to(
        fresh_value[:, :, None, :], (row_count, KV_HEADS, head_group, HD)
    ).reshape(row_count, HEADS, HD)
    width = HEADS * HD
    packed = jnp.stack(
        [
            part_accum.reshape(both_rows, width),
            jnp.broadcast_to(part_max[..., None], part_accum.shape).reshape(both_rows, width),
            jnp.broadcast_to(part_total[..., None], part_accum.shape).reshape(both_rows, width),
        ],
        1,
    )
    own_packed = jnp.stack(
        [
            value_rows.reshape(row_count, width),
            jnp.broadcast_to(own_score[..., None], value_rows.shape).reshape(row_count, width),
            jnp.ones((row_count, width), jnp.float32),
        ],
        1,
    )
    feature_share = hidden.shape[1]
    expert_ids = jnp.arange(group_count, dtype=jnp.int32)
    named = routes[:, :, None] == expert_ids[None, None, :]
    chosen = jnp.any(named, 1).astype(jnp.int32)
    weight_at = jnp.sum(
        jnp.where(named, route_weight.astype(jnp.float32)[:, :, None], 0.0), 1
    )
    position = jnp.cumsum(chosen, 0) - chosen
    slot_ids = jnp.arange(row_count, dtype=jnp.int32)
    placed = (chosen[:, :, None] == 1) & (position[:, :, None] == slot_ids[None, None, :])
    picker = (
        placed.transpose(1, 2, 0).reshape(group_count * row_count, row_count).astype(jnp.bfloat16)
    )
    combine = (
        jnp.where(placed, weight_at[:, :, None], 0.0)
        .reshape(row_count, group_count * row_count)
        .astype(jnp.bfloat16)
    )
    down_parts = (
        down[0].reshape(FF, lax.axis_size("ep"), feature_share).transpose(1, 0, 2)
    )
    layer_out, attn_out = layer_call(
        packed, own_packed, out_weight, hidden, norm_gain.reshape(1, feature_share),
        picker, combine, gate_up[0], down_parts,
    )
    return (layer_out, attn_out)


def solution(mesh):
    placed = (
        P("grp", "ep"),
        P("grp", None),
        P("grp", None, None),
        P(("grp", "ep"), None),
        P(("grp", "ep"), None),
        P(("grp", "ep")),
        P(("grp", "ep")),
        P("grp", "ep"),
        P("ep"),
        P("grp", None, None),
        P("grp", None, None),
        P("grp", None),
        P("grp", None),
    )
    return jax.shard_map(
        per_device,
        mesh=mesh,
        in_specs=placed,
        out_specs=(P("grp", "ep"), P("grp", None)),
        check_vma=False,
    )
```

time: 119 us -> 107 us (0.90)
  Pallas kernels: 93.8 us -> 83 us
  matrix products: 2.47 us -> 0.72 us
    pallas_call x2 -> x1, Pallas kernels: 93.8 us -> 83 us  [layer_call(): pl.pallas_call(functools.partial(layer_kernel, rows, n_ep, n_grp, width),...]
    another operation x0 -> x2, other arithmetic: none -> 1.79 us  [the longest x1 1.02 us: per_device(): jnp.stack([part_accum.reshape(both_rows, width), jnp.broadcast_to(part_ma...]
    dot_general x1 -> x0, matrix products: 1.75 us -> none  [per_device(): jnp.dot(attn_out, weight_columns, preferred_element_type=jnp.float32)]
    concatenate x2 -> x0, other arithmetic: 1.57 us -> none  [the longest x1 0.85 us: per_device(): jnp.concatenate([part_accum, part_max[..., None], part_total[..., None],...]
    unnamed x20 -> x17, local copies, waits for them, and re-layouts: 3 us -> 4.34 us
  transfers between devices with their start and end apart: 1 -> 1, of which waited for: 0 -> 0; matrix products, arithmetic and copies ran while one was open for 12% -> 13% of each run, Pallas kernels for 0% -> 0%
where the time goes in v5:
time: 107 us
  Pallas kernels  83 us (78%)
  local copies, waits for them, and re-layouts  12.2 us (11%)
  other arithmetic  7.1 us (7%)
  starting transfers between devices  2.59 us (2%)
    pallas_call x1, Pallas kernels, layer_call(): pl.pallas_call(functools.partial(layer_kernel, rows, n_ep, n_grp, width),...  83 us
    unnamed x17, local copies, waits for them, and re-layouts  4.34 us
    ppermute x1, starting transfers between devices, from_partner(): return lax.ppermute(block, axis, route)  2.59 us
    another operation x1, local copies, waits for them, and re-layouts, per_device(): down[0].reshape(FF, lax.axis_size('ep'), feature_share).transpose(1, 0, 2)  2.45 us
  transfers between devices with their start and end apart: 1, of which 0 were waited for; matrix products, arithmetic and copies ran while one was open for 13% of the time, Pallas kernels for 0%

profile of v5, /device:TPU:31, one launch (start us, length us, event | category | flops | bytes accessed | tf_op | source)
XLA Modules:
  0.0 106.6 jit_solution(14490686356717302603)
XLA Ops:
  0.7 2.6 %collective-permute-start = (bf16[8,1536]{1,0:T(8,128)(2,1)}, bf16[8,1536]{1,0:T(8,128)(2,1)S(1)}, u32[]{:S(2)}, u32[]{:S(2)}) collective-permute-start(bf16[8,1536]{1,0:T(8,128)(2,1)} %param.14), channel_id=1, source_target_pairs={{0,16},{16,0},{32,48},{48,32},{64,80},{80,64},{96,112},{112,96},{1... | collective-permute-start | bytes 73736 | tf_op jit(solution)/shard_map/ppermute | solution.py:333
  3.3 0.9 reshape.147
  4.1 0.8 slice_reduce_fusion
  4.9 0.8 convert_reduce_fusion
  5.7 0.7 iota_compare_fusion.1
  6.8 0.8 fusion.10
  7.8 0.1 eq.96
  8.0 0.1 and.46
  8.2 0.7 convert_element_type.45
  8.9 0.8 select_reduce_fusion.1
  9.8 0.1 broadcast_in_dim.99
  10.2 0.2 fusion.13
  10.4 0.1 copy.79
  10.9 0.1 stack_reshape_reshape.9
  11.2 0.7 fusion.8.picker_ref
  11.9 0.6 select_convert_fusion.combine_ref
  12.5 0.8 maximum_maximum_fusion.own_ref
  13.3 0.1 copy.60
  13.5 0.9 copy.62
  14.4 0.7 copy.76
  15.1 2.4 %copy.77 = bf16[512,16,96]{2,0,1:T(8,128)(2,1)} copy(bf16[512,16,96]{0,2,1:T(8,128)(2,1)S(1)} %bitcast.42) | data formatting | bytes 3145728 | tf_op jit(solution)/shard_map/reshape;squeeze | solution.py:441
  17.5 0.2 reshape.142
  17.7 0.3 select_reduce_fusion
  18.1 0.2 fusion
  18.3 0.3 fusion.2
  18.8 0.2 stack_reshape_reshape.8
  19.4 0.2 stack_reshape.10
  19.8 0.2 stack_reshape.9
  20.0 1.0 pad_maximum_fusion.part_ref
  21.0 83.0 %shard_map.140 = (bf16[8,96]{1,0:T(8,128)(2,1)}, bf16[8,1536]{1,0:T(8,128)(2,1)}) custom-call(f32[16,3,1536]{2,1,0:T(4,128)} %pad_maximum_fusion.part_ref, f32[8,3,1536]{2,1,0:T(4,128)} %maximum_maximum_fusion.own_ref, bf16[48,96]{1,0:T(8,128)(2,1)} %block_ref.1, bf16[8,96]{1,0:T(8,128)(2,1)} %hidden_ref.1, f32[1,96]{1,0:T(1,128)} %bitcast.52, ...), custom_call_target="tpu_custom_call" | custom-call | tf_op jit(solution)/shard_map/pallas_call | solution.py:292
  104.0 1.3 %copy.86 = bf16[8,96]{1,0:T(8,128)(2,1)} copy(bf16[8,96]{1,0:T(8,128)(2,1)} %get-tuple-element.9) | data formatting | bytes 3072
  105.3 1.3 %copy.87 = bf16[8,1536]{1,0:T(8,128)(2,1)} copy(bf16[8,1536]{1,0:T(8,128)(2,1)} %get-tuple-element.10) | data formatting | bytes 49152
  (58 shorter events, 2.6 us)
Async XLA Ops:
  0.6 6.0 %copy-start = (s32[12]{0:T(128)S(1)}, s32[12]{0:T(128)}, u32[]{:S(2)}) copy-start(s32[12]{0:T(128)} %param.19) | copy-start | bytes 148
  0.6 12.7 %copy-start.3 = (bf16[192,512]{1,0:T(8,128)(2,1)S(1)}, bf16[192,512]{1,0:T(8,128)(2,1)}, u32[]{:S(2)}) copy-start(bf16[192,512]{1,0:T(8,128)(2,1)} %param.16) | copy-start | bytes 589828
  0.7 12.8 %copy-start.4 = (bf16[192,512]{1,0:T(8,128)(2,1)S(1)}, bf16[192,512]{1,0:T(8,128)(2,1)}, u32[]{:S(2)}) copy-start(bf16[192,512]{1,0:T(8,128)(2,1)} %param.17) | copy-start | bytes 589828
  0.7 13.7 %copy-start.1 = (bf16[1,512,1536]{2,1,0:T(8,128)(2,1)S(1)}, bf16[1,512,1536]{2,1,0:T(8,128)(2,1)}, u32[]{:S(2)}) copy-start(bf16[1,512,1536]{2,1,0:T(8,128)(2,1)} %param.23) | copy-start | bytes 4718596
  0.7 16.9 %collective-permute-start = (bf16[8,1536]{1,0:T(8,128)(2,1)}, bf16[8,1536]{1,0:T(8,128)(2,1)S(1)}, u32[]{:S(2)}, u32[]{:S(2)}) collective-permute-start(bf16[8,1536]{1,0:T(8,128)(2,1)} %param.14), channel_id=1, source_target_pairs={{0,16},{16,0},{32,48},{48,32},{64,80},{80,64},{96,112},{112,96},{1... | collective-permute-start | bytes 73736 | tf_op jit(solution)/shard_map/ppermute | solution.py:333
  15.1 2.5 %copy-start.5 = (bf16[8,1536]{1,0:T(8,128)(2,1)S(1)}, bf16[8,1536]{1,0:T(8,128)(2,1)}, u32[]{:S(2)}) copy-start(bf16[8,1536]{1,0:T(8,128)(2,1)} %param.14) | copy-start | bytes 73732
  15.1 3.3 %copy-start.2 = (bf16[192,512]{0,1:T(8,128)(2,1)S(1)}, bf16[192,512]{0,1:T(8,128)(2,1)}, u32[]{:S(2)}) copy-start(bf16[192,512]{0,1:T(8,128)(2,1)} %copy.62) | copy-start | bytes 589828

commit v6 on v5

--- a/solution.py
+++ b/solution.py
@@ -22,9 +22,10 @@
 
 def layer_kernel(
     rows, n_ep, n_grp, width,
-    part_ref, own_ref, block_ref, hidden_ref, gain_ref, picker_ref, combine_ref, up_ref, down_ref,
+    query_ref, mate_query_ref, key_ref, value_ref, owner_ref, fill_ref,
+    own_ref, block_ref, hidden_ref, gain_ref, picker_ref, combine_ref, up_ref, down_ref,
     out_ref, attn_ref,
-    got, final, blocks, squares, outgoing, incoming, results, returned,
+    part_ref, got, final, blocks, squares, outgoing, incoming, results, returned,
     s1, r1, s2, r2, s3, r3, s_sq, r_sq, s_out, r_in, s_res, r_ret,
 ):
     g = lax.axis_index("grp")
@@ -56,6 +57,50 @@
                     barrier, inc=1, device_id=(2 * e + half, peer), device_id_type=MESH
                 )
     common = 2 * (n_ep - 1) + n_ep + n_grp - 1
+
+    heads = width // HD
+    both = 2 * rows
+    pages = owner_ref.shape[1]
+    tokens = key_ref.shape[0]
+    page_length = tokens // pages
+    queries = jnp.concatenate([query_ref[...], mate_query_ref[...]], 0)
+    lane_head = lax.broadcasted_iota(jnp.int32, (both, width), 1) // HD
+    stacked = jnp.concatenate(
+        [jnp.where(lane_head == h, queries, jnp.zeros_like(queries)) for h in range(heads)], 0
+    )
+    row_of = lax.broadcasted_iota(jnp.int32, (both, pages), 0)
+    owns = (owner_ref[...] == row_of).astype(jnp.float32)
+    token_of = lax.broadcasted_iota(jnp.int32, (tokens, pages), 0)
+    page_of = lax.broadcasted_iota(jnp.int32, (tokens, pages), 1)
+    filled = (
+        (token_of // page_length == page_of) & (token_of % page_length < fill_ref[...])
+    ).astype(jnp.float32)
+    usable = lax.dot_general(
+        owns, filled, (((1,), (1,)), ((), ())), preferred_element_type=jnp.float32
+    ) > 0.5
+    usable = jnp.concatenate([usable] * heads, 0)
+    scores = lax.dot_general(
+        stacked, key_ref[...], (((1,), (1,)), ((), ())), preferred_element_type=jnp.float32
+    ) * (HD ** -0.5)
+    local_top = jnp.max(jnp.where(usable, scores, masked_score), 1, keepdims=True)
+    weights = jnp.where(usable, jnp.exp(scores - local_top), 0.0)
+    local_total = jnp.sum(weights, 1, keepdims=True)
+    local_accum = jnp.dot(
+        weights.astype(jnp.bfloat16), value_ref[...], preferred_element_type=jnp.float32
+    )
+    accum_rows = jnp.zeros((both, width), jnp.float32)
+    top_rows = jnp.zeros((both, width), jnp.float32)
+    total_rows = jnp.zeros((both, width), jnp.float32)
+    for h in range(heads):
+        mine = lane_head == h
+        block = slice(h * both, (h + 1) * both)
+        accum_rows = jnp.where(mine, local_accum[block], accum_rows)
+        top_rows = jnp.where(mine, jnp.broadcast_to(local_top[block], (both, width)), top_rows)
+        total_rows = jnp.where(mine, jnp.broadcast_to(local_total[block], (both, width)), total_rows)
+    for row in range(both):
+        part_ref[row, 0:1, :] = accum_rows[row:row + 1]
+        part_ref[row, 1:2, :] = top_rows[row:row + 1]
+        part_ref[row, 2:3, :] = total_rows[row:row + 1]
 
     @pl.when(serving)
     def _():
@@ -283,7 +328,7 @@
                 give_back(half, peer).wait_send()
 
 
-def layer_call(part, own, block, hidden, gain, picker, combine, up, down_parts):
+def layer_call(query, mate_query, keys, values, owner, fill, own, block, hidden, gain, picker, combine, up, down_parts):
     n_ep = lax.axis_size("ep")
     n_grp = lax.axis_size("grp")
     rows, share = hidden.shape
@@ -295,10 +340,11 @@
             jax.ShapeDtypeStruct((rows, share), jnp.bfloat16),
             jax.ShapeDtypeStruct((rows, width), jnp.bfloat16),
         ),
-        in_specs=[pl.BlockSpec(memory_space=pltpu.VMEM)] * 9,
+        in_specs=[pl.BlockSpec(memory_space=pltpu.VMEM)] * 14,
         out_specs=(pl.BlockSpec(memory_space=pltpu.VMEM),) * 2,
         scratch_shapes=[
-            pltpu.VMEM((2 * n_ep,) + part.shape[1:], jnp.float32),
+            pltpu.VMEM((2 * rows, 3, width), jnp.float32),
+            pltpu.VMEM((2 * n_ep, 3, width), jnp.float32),
             pltpu.VMEM((rows, 1, width), jnp.float32),
             pltpu.VMEM((n_grp,) + block.shape, block.dtype),
             pltpu.VMEM((n_ep, rows, 128), jnp.float32),
@@ -320,7 +366,7 @@
             pltpu.SemaphoreType.DMA((n_grp,)),
         ],
         compiler_params=pltpu.CompilerParams(collective_id=0, has_side_effects=True),
-    )(part, own, block, hidden, gain, picker, combine, up, down_parts)
+    )(query, mate_query, keys, values, owner, fill, own, block, hidden, gain, picker, combine, up, down_parts)
 
 
 def from_partner(block, axis, apart):
@@ -357,39 +403,13 @@
     both_rows = 2 * row_count
     scale = HD ** (-0.5)
     partner_query = from_partner(query, "grp", 0)
-    all_queries = jnp.concatenate([query, partner_query], 0)
-    query_heads = (
-        all_queries.reshape(both_rows, KV_HEADS, head_group, HD)
-        .transpose(1, 0, 2, 3)
-        .reshape(KV_HEADS, both_rows * head_group, HD)
-    )
-    key_heads = key_cache.reshape(token_count, KV_HEADS, HD)
-    value_heads = value_cache.reshape(token_count, KV_HEADS, HD)
-    scores = (
-        jnp.einsum("kqd,tkd->kqt", query_heads, key_heads, preferred_element_type=jnp.float32)
-        * scale
-    )
-    scores = scores.reshape(KV_HEADS, both_rows, head_group, token_count)
-    row_index = jnp.arange(both_rows, dtype=jnp.int32)
-    in_page = jnp.arange(page_length, dtype=jnp.int32)
-    usable = (page_owner[None, :, None] == row_index[:, None, None]) & (
-        in_page[None, None, :] < page_fill[None, :, None]
-    )
-    usable = usable.reshape(both_rows, token_count)[None, :, None, :]
-    local_top = jnp.max(jnp.where(usable, scores, masked_score), -1)
-    weights = jnp.where(usable, jnp.exp(scores - local_top[..., None]), 0.0)
-    local_total = jnp.sum(weights, -1)
-    rounded = weights.astype(jnp.bfloat16).reshape(KV_HEADS, both_rows * head_group, token_count)
-    local_accum = jnp.einsum(
-        "kqt,tkd->kqd", rounded, value_heads, preferred_element_type=jnp.float32
-    )
-    part_max = local_top.transpose(1, 0, 2).reshape(both_rows, HEADS)
-    part_total = local_total.transpose(1, 0, 2).reshape(both_rows, HEADS)
-    part_accum = (
-        local_accum.reshape(KV_HEADS, both_rows, head_group, HD)
-        .transpose(1, 0, 2, 3)
-        .reshape(both_rows, HEADS, HD)
-    )
+    expanded = (token_count, KV_HEADS, head_group, HD)
+    keys = jnp.broadcast_to(
+        key_cache.reshape(token_count, KV_HEADS, 1, HD), expanded
+    ).reshape(token_count, HEADS * HD)
+    values = jnp.broadcast_to(
+        value_cache.reshape(token_count, KV_HEADS, 1, HD), expanded
+    ).reshape(token_count, HEADS * HD)
     own_query = query.reshape(row_count, KV_HEADS, head_group, HD)
     fresh_key = new_kv[:, 0].reshape(row_count, KV_HEADS, HD)
     fresh_value = new_kv[:, 1].astype(jnp.float32).reshape(row_count, KV_HEADS, HD)
@@ -403,14 +423,6 @@
         fresh_value[:, :, None, :], (row_count, KV_HEADS, head_group, HD)
     ).reshape(row_count, HEADS, HD)
     width = HEADS * HD
-    packed = jnp.stack(
-        [
-            part_accum.reshape(both_rows, width),
-            jnp.broadcast_to(part_max[..., None], part_accum.shape).reshape(both_rows, width),
-            jnp.broadcast_to(part_total[..., None], part_accum.shape).reshape(both_rows, width),
-        ],
-        1,
-    )
     own_packed = jnp.stack(
         [
             value_rows.reshape(row_count, width),
@@ -441,7 +453,8 @@
         down[0].reshape(FF, lax.axis_size("ep"), feature_share).transpose(1, 0, 2)
     )
     layer_out, attn_out = layer_call(
-        packed, own_packed, out_weight, hidden, norm_gain.reshape(1, feature_share),
+        query, partner_query, keys, values, page_owner.reshape(1, -1), page_fill.reshape(1, -1),
+        own_packed, out_weight, hidden, norm_gain.reshape(1, feature_share),
         picker, combine, gate_up[0], down_parts,
     )
     return (layer_out, attn_out)

time: 107 us -> 105 us (0.981)
  other arithmetic: 7.1 us -> 5.15 us
    reshape x1 -> x2, local copies, waits for them, and re-layouts: 0.16 us -> 2.16 us  [the longest x1 1.09 us: per_device(): values = jnp.broadcast_to(value_cache.reshape(token_count, KV_HEADS, 1, H...]
    unnamed x17 -> x13, local copies, waits for them, and re-layouts: 4.34 us -> 4.19 us
  transfers between devices with their start and end apart: 1 -> 1, of which waited for: 0 -> 0; matrix products, arithmetic and copies ran while one was open for 13% -> 14% of each run, Pallas kernels for 0% -> 0%
where the time goes in v6:
time: 105 us
  Pallas kernels  83.6 us (80%)
  local copies, waits for them, and re-layouts  12.3 us (12%)
  other arithmetic  5.15 us (5%)
  starting transfers between devices  2.59 us (2%)
    pallas_call x1, Pallas kernels, layer_call(): pl.pallas_call(functools.partial(layer_kernel, rows, n_ep, n_grp, width),...  83.6 us
    unnamed x13, local copies, waits for them, and re-layouts  4.19 us
    ppermute x1, starting transfers between devices, from_partner(): return lax.ppermute(block, axis, route)  2.59 us
    another operation x1, local copies, waits for them, and re-layouts, per_device(): down[0].reshape(FF, lax.axis_size('ep'), feature_share).transpose(1, 0, 2)  2.45 us
  transfers between devices with their start and end apart: 1, of which 0 were waited for; matrix products, arithmetic and copies ran while one was open for 14% of the time, Pallas kernels for 0%

profile of v6, /device:TPU:31, one launch (start us, length us, event | category | flops | bytes accessed | tf_op | source)
XLA Modules:
  0.0 104.6 jit_solution(17607590553011710394)
XLA Ops:
  0.6 2.6 %collective-permute-start = (bf16[8,1536]{1,0:T(8,128)(2,1)}, bf16[8,1536]{1,0:T(8,128)(2,1)S(1)}, u32[]{:S(2)}, u32[]{:S(2)}) collective-permute-start(bf16[8,1536]{1,0:T(8,128)(2,1)} %query_ref.1), channel_id=1, source_target_pairs={{0,16},{16,0},{32,48},{48,32},{64,80},{80,64},{96,112},{112,96},{1... | collective-permute-start | bytes 73736 | tf_op jit(solution)/shard_map/ppermute | solution.py:379
  3.2 0.9 reshape.73
  4.1 0.8 slice_reduce_fusion
  4.9 0.8 convert_reduce_fusion
  5.7 0.8 fusion.2
  6.5 0.1 eq.74
  6.6 0.1 eq.75
  6.7 0.1 and.22
  6.8 0.1 and.23
  7.0 0.7 convert_element_type.40
  7.7 0.8 select_reduce_fusion
  8.5 0.1 broadcast_in_dim.66
  8.6 0.1 broadcast_in_dim.67
  8.8 0.1 copy.31
  9.0 0.2 fusion.4
  9.2 0.1 copy.38
  9.4 0.1 broadcast_in_dim.63
  9.5 0.1 stack_reshape.3
  9.8 0.1 stack_reshape_reshape.4
  10.0 0.7 fusion.1.picker_ref
  10.7 0.8 maximum_maximum_fusion.own_ref
  11.5 0.6 select_convert_fusion.combine_ref
  12.1 0.7 copy.33
  12.8 2.4 %copy.34 = bf16[512,16,96]{2,0,1:T(8,128)(2,1)} copy(bf16[512,16,96]{0,2,1:T(8,128)(2,1)S(1)} %bitcast.29) | data formatting | bytes 3145728 | tf_op jit(solution)/shard_map/reshape;squeeze | solution.py:453
  15.2 0.1 copy.27
  15.4 1.1 %copy.35.key_ref = bf16[192,1536]{1,0:T(8,128)(2,1)} copy(bf16[192,1536]{0,1:T(8,128)(2,1)S(1)} %bitcast.31) | data formatting | bytes 1179648 | tf_op jit(solution)/shard_map/reshape | solution.py:409
  16.5 0.1 copy.28
  16.7 1.1 %copy.36.value_ref = bf16[192,1536]{1,0:T(8,128)(2,1)} copy(bf16[192,1536]{0,1:T(8,128)(2,1)S(1)} %bitcast.32) | data formatting | bytes 1179648 | tf_op jit(solution)/shard_map/reshape | solution.py:412
  17.8 0.6 copy-done.3
  18.4 83.6 %shard_map.140 = (bf16[8,96]{1,0:T(8,128)(2,1)}, bf16[8,1536]{1,0:T(8,128)(2,1)}) custom-call(bf16[8,1536]{1,0:T(8,128)(2,1)} %query_ref.1, bf16[8,1536]{1,0:T(8,128)(2,1)} %copy-done.3, bf16[192,1536]{1,0:T(8,128)(2,1)} %copy.35.key_ref, bf16[192,1536]{1,0:T(8,128)(2,1)} %copy.36.value_ref, s32[1,12]{1,0:T(1,128)} %bitcast.36, s32[1,12]{1,0:T(1,128)} %bitcast.37, ...), custom_call_target="tpu_custom_call" | custom-call | tf_op jit(solution)/shard_map/pallas_call | solution.py:337
  102.0 1.3 %copy.41 = bf16[8,96]{1,0:T(8,128)(2,1)} copy(bf16[8,96]{1,0:T(8,128)(2,1)} %get-tuple-element.7) | data formatting | bytes 3072
  103.3 1.3 %copy.42 = bf16[8,1536]{1,0:T(8,128)(2,1)} copy(bf16[8,1536]{1,0:T(8,128)(2,1)} %get-tuple-element.8) | data formatting | bytes 49152
  (23 shorter events, 0.7 us)
Async XLA Ops:
  0.6 11.4 %copy-start = (bf16[1,512,1536]{2,1,0:T(8,128)(2,1)S(1)}, bf16[1,512,1536]{2,1,0:T(8,128)(2,1)}, u32[]{:S(2)}) copy-start(bf16[1,512,1536]{2,1,0:T(8,128)(2,1)} %param.23) | copy-start | bytes 4718596
  0.6 17.2 %collective-permute-start = (bf16[8,1536]{1,0:T(8,128)(2,1)}, bf16[8,1536]{1,0:T(8,128)(2,1)S(1)}, u32[]{:S(2)}, u32[]{:S(2)}) collective-permute-start(bf16[8,1536]{1,0:T(8,128)(2,1)} %query_ref.1), channel_id=1, source_target_pairs={{0,16},{16,0},{32,48},{48,32},{64,80},{80,64},{96,112},{112,96},{1... | collective-permute-start | bytes 73736 | tf_op jit(solution)/shard_map/ppermute | solution.py:379
  12.8 2.5 %copy-start.1 = (bf16[192,512]{1,0:T(8,128)(2,1)S(1)}, bf16[192,512]{1,0:T(8,128)(2,1)}, u32[]{:S(2)}) copy-start(bf16[192,512]{1,0:T(8,128)(2,1)} %param.16) | copy-start | bytes 589828
  15.2 1.3 %copy-start.2 = (bf16[192,512]{1,0:T(8,128)(2,1)S(1)}, bf16[192,512]{1,0:T(8,128)(2,1)}, u32[]{:S(2)}) copy-start(bf16[192,512]{1,0:T(8,128)(2,1)} %param.17) | copy-start | bytes 589828
  17.8 0.6 copy-start.3

commit v7 on v6

--- a/solution.py
+++ b/solution.py
@@ -23,7 +23,7 @@
 def layer_kernel(
     rows, n_ep, n_grp, width,
     query_ref, mate_query_ref, key_ref, value_ref, owner_ref, fill_ref,
-    own_ref, block_ref, hidden_ref, gain_ref, picker_ref, combine_ref, up_ref, down_ref,
+    own_ref, block_ref, hidden_ref, gain_ref, routes_ref, route_weight_ref, up_ref, down_ref,
     out_ref, attn_ref,
     part_ref, got, final, blocks, squares, outgoing, incoming, results, returned,
     s1, r1, s2, r2, s3, r3, s_sq, r_sq, s_out, r_in, s_res, r_ret,
@@ -102,6 +102,33 @@
         part_ref[row, 1:2, :] = top_rows[row:row + 1]
         part_ref[row, 2:3, :] = total_rows[row:row + 1]
 
+    choices = routes_ref.shape[1]
+    expert_of = lax.broadcasted_iota(jnp.int32, (rows, n_grp), 1)
+    chosen = jnp.zeros((rows, n_grp), jnp.float32)
+    weight_at = jnp.zeros((rows, n_grp), jnp.float32)
+    for choice in range(choices):
+        hit = routes_ref[:, choice:choice + 1] == expert_of
+        chosen = chosen + hit.astype(jnp.float32)
+        weight_at = weight_at + jnp.where(
+            hit, route_weight_ref[:, choice:choice + 1].astype(jnp.float32), 0.0)
+    earlier = (
+        lax.broadcasted_iota(jnp.int32, (rows, rows), 1)
+        < lax.broadcasted_iota(jnp.int32, (rows, rows), 0)
+    ).astype(jnp.float32)
+    position = jnp.dot(earlier, chosen, preferred_element_type=jnp.float32)
+    slot_count = rows * n_grp
+    spread_out = (
+        lax.broadcasted_iota(jnp.int32, (n_grp, slot_count), 1) // rows
+        == lax.broadcasted_iota(jnp.int32, (n_grp, slot_count), 0)
+    ).astype(jnp.bfloat16)
+    chosen_wide = jnp.dot(chosen.astype(jnp.bfloat16), spread_out, preferred_element_type=jnp.float32)
+    position_wide = jnp.dot(position.astype(jnp.bfloat16), spread_out, preferred_element_type=jnp.float32)
+    weight_wide = jnp.dot(weight_at.astype(jnp.bfloat16), spread_out, preferred_element_type=jnp.float32)
+    slot_of = (lax.broadcasted_iota(jnp.int32, (rows, slot_count), 1) % rows).astype(jnp.float32)
+    placed = (chosen_wide > 0.5) & (position_wide == slot_of)
+    combine = jnp.where(placed, weight_wide, 0.0).astype(jnp.bfloat16)
+    picker = jnp.transpose(placed.astype(jnp.float32)).astype(jnp.bfloat16)
+
     @pl.when(serving)
     def _():
         pl.semaphore_wait(barrier, common + n_grp - 1 + 2 * n_ep - 1)
@@ -227,7 +254,7 @@
     total_sq = jnp.sum(squares[...][:, :, 0:1], axis=0)
     normed = (mixed * lax.rsqrt(total_sq / width + norm_epsilon) * gain_ref[...]).astype(jnp.bfloat16)
     slots = outgoing.shape[1]
-    picked = jnp.dot(picker_ref[...], normed, preferred_element_type=jnp.float32)
+    picked = jnp.dot(picker, normed, preferred_element_type=jnp.float32)
     outgoing[...] = picked.reshape(outgoing.shape)
 
     def dispatch(expert):
@@ -264,7 +291,8 @@
     gate = pre[:, :hidden_units]
     act = (gate / (1.0 + jnp.exp(-gate)) * pre[:, hidden_units:]).astype(jnp.bfloat16)
     for peer in range(n_ep):
-        piece = jnp.dot(act, down_ref[peer], preferred_element_type=jnp.float32)
+        piece = jnp.dot(
+            act, down_ref[:, peer * share:(peer + 1) * share], preferred_element_type=jnp.float32)
         results[peer] = piece.astype(jnp.bfloat16).astype(jnp.float32).reshape(results.shape[1:])
 
     def give_back(half, peer):
@@ -293,7 +321,7 @@
             coming_back(expert).wait_recv()
 
     back = returned[...].reshape(n_grp * slots, share).astype(jnp.bfloat16)
-    mix = jnp.dot(combine_ref[...], back, preferred_element_type=jnp.float32)
+    mix = jnp.dot(combine, back, preferred_element_type=jnp.float32)
     out_ref[...] = (mixed + mix).astype(out_ref.dtype)
 
     for row in range(2 * rows):
@@ -328,12 +356,12 @@
                 give_back(half, peer).wait_send()
 
 
-def layer_call(query, mate_query, keys, values, owner, fill, own, block, hidden, gain, picker, combine, up, down_parts):
+def layer_call(query, mate_query, keys, values, owner, fill, own, block, hidden, gain, routes, route_weight, up, down):
     n_ep = lax.axis_size("ep")
     n_grp = lax.axis_size("grp")
     rows, share = hidden.shape
     width = share * n_ep
-    slots = picker.shape[0] // n_grp
+    slots = rows
     return pl.pallas_call(
         functools.partial(layer_kernel, rows, n_ep, n_grp, width),
         out_shape=(
@@ -366,7 +394,7 @@
             pltpu.SemaphoreType.DMA((n_grp,)),
         ],
         compiler_params=pltpu.CompilerParams(collective_id=0, has_side_effects=True),
-    )(query, mate_query, keys, values, owner, fill, own, block, hidden, gain, picker, combine, up, down_parts)
+    )(query, mate_query, keys, values, owner, fill, own, block, hidden, gain, routes, route_weight, up, down)
 
 
 def from_partner(block, axis, apart):
@@ -432,30 +460,10 @@
         1,
     )
     feature_share = hidden.shape[1]
-    expert_ids = jnp.arange(group_count, dtype=jnp.int32)
-    named = routes[:, :, None] == expert_ids[None, None, :]
-    chosen = jnp.any(named, 1).astype(jnp.int32)
-    weight_at = jnp.sum(
-        jnp.where(named, route_weight.astype(jnp.float32)[:, :, None], 0.0), 1
-    )
-    position = jnp.cumsum(chosen, 0) - chosen
-    slot_ids = jnp.arange(row_count, dtype=jnp.int32)
-    placed = (chosen[:, :, None] == 1) & (position[:, :, None] == slot_ids[None, None, :])
-    picker = (
-        placed.transpose(1, 2, 0).reshape(group_count * row_count, row_count).astype(jnp.bfloat16)
-    )
-    combine = (
-        jnp.where(placed, weight_at[:, :, None], 0.0)
-        .reshape(row_count, group_count * row_count)
-        .astype(jnp.bfloat16)
-    )
-    down_parts = (
-        down[0].reshape(FF, lax.axis_size("ep"), feature_share).transpose(1, 0, 2)
-    )
     layer_out, attn_out = layer_call(
         query, partner_query, keys, values, page_owner.reshape(1, -1), page_fill.reshape(1, -1),
         own_packed, out_weight, hidden, norm_gain.reshape(1, feature_share),
-        picker, combine, gate_up[0], down_parts,
+        routes, route_weight, gate_up[0], down[0],
     )
     return (layer_out, attn_out)
 

time: 105 us -> 97.7 us (0.930)
  other arithmetic: 5.15 us -> 1.55 us
  local copies, waits for them, and re-layouts: 12.3 us -> 9.15 us
    another operation x1 -> x0, local copies, waits for them, and re-layouts: 2.45 us -> none  [per_device(): down[0].reshape(FF, lax.axis_size('ep'), feature_share).transpose(1, 0, 2)]
    convert_element_type x3 -> x0, other arithmetic: 2 us -> none  [the longest x1 0.72 us: per_device(): placed.transpose(1, 2, 0).reshape(group_count * row_count, row_count)]
    unnamed x13 -> x8, local copies, waits for them, and re-layouts: 4.19 us -> 4.41 us
  transfers between devices with their start and end apart: 1 -> 1, of which waited for: 0 -> 0; matrix products, arithmetic and copies ran while one was open for 14% -> 8% of each run, Pallas kernels for 0% -> 0%
where the time goes in v7:
time: 97.7 us; the launch traced here: 97.2 us
  Pallas kernels  83 us (85%)
  local copies, waits for them, and re-layouts  9.15 us (9%)
  starting transfers between devices  2.59 us (3%)
  other arithmetic  1.55 us (2%)
    pallas_call x1, Pallas kernels, layer_call(): pl.pallas_call(functools.partial(layer_kernel, rows, n_ep, n_grp, width),...  83 us
    unnamed x8, local copies, waits for them, and re-layouts  4.41 us
    ppermute x1, starting transfers between devices, from_partner(): return lax.ppermute(block, axis, route)  2.59 us
  transfers between devices with their start and end apart: 1, of which 0 were waited for; matrix products, arithmetic and copies ran while one was open for 8% of the time, Pallas kernels for 0%

profile of v7, /device:TPU:31, one launch (start us, length us, event | category | flops | bytes accessed | tf_op | source)
XLA Modules:
  0.0 97.2 jit_solution(15647129637336388807)
XLA Ops:
  0.6 0.0 copy-start
  0.6 2.6 %collective-permute-start = (bf16[8,1536]{1,0:T(8,128)(2,1)}, bf16[8,1536]{1,0:T(8,128)(2,1)S(1)}, u32[]{:S(2)}, u32[]{:S(2)}) collective-permute-start(bf16[8,1536]{1,0:T(8,128)(2,1)} %query_ref.1), channel_id=1, source_target_pairs={{0,16},{16,0},{32,48},{48,32},{64,80},{80,64},{96,112},{112,96},{1... | collective-permute-start | bytes 73736 | tf_op jit(solution)/shard_map/ppermute | solution.py:407
  3.2 0.9 reshape.45
  4.1 0.8 slice_reduce_fusion
  4.9 0.8 convert_reduce_fusion
  5.7 0.1 reshape.51
  5.7 0.2 fusion
  5.9 0.1 copy.22
  6.1 0.1 copy.17
  6.2 0.1 broadcast_in_dim.30
  6.3 0.1 stack_reshape.3
  6.4 0.1 reshape.47
  6.5 0.1 stack_reshape_reshape.4
  6.6 0.1 pad.2.clone
  6.7 0.8 maximum_maximum_fusion.own_ref
  7.5 1.1 %copy.15 = bf16[192,512]{0,1:T(8,128)(2,1)S(1)} copy(bf16[192,512]{1,0:T(8,128)(2,1)} %param.16) | data formatting | bytes 393216 | tf_op args[3]
  8.5 0.1 broadcast_in_dim.26
  8.6 1.1 %copy.19.key_ref = bf16[192,1536]{1,0:T(8,128)(2,1)} copy(bf16[192,1536]{0,1:T(8,128)(2,1)S(1)} %bitcast.17) | data formatting | bytes 1179648 | tf_op jit(solution)/shard_map/reshape | solution.py:437
  9.7 0.0 copy-done
  9.7 0.1 copy.16
  9.8 0.1 broadcast_in_dim.28
  9.9 1.1 %copy.20.value_ref = bf16[192,1536]{1,0:T(8,128)(2,1)} copy(bf16[192,1536]{0,1:T(8,128)(2,1)S(1)} %bitcast.18) | data formatting | bytes 1179648 | tf_op jit(solution)/shard_map/reshape | solution.py:440
  11.0 0.0 collective-permute-done.mate_query_ref
  11.0 0.0 copy-start.1
  11.0 0.6 copy-done.1
  11.6 83.0 %shard_map.140 = (bf16[8,96]{1,0:T(8,128)(2,1)}, bf16[8,1536]{1,0:T(8,128)(2,1)}) custom-call(bf16[8,1536]{1,0:T(8,128)(2,1)} %query_ref.1, bf16[8,1536]{1,0:T(8,128)(2,1)} %copy-done.1, bf16[192,1536]{1,0:T(8,128)(2,1)} %copy.19.key_ref, bf16[192,1536]{1,0:T(8,128)(2,1)} %copy.20.value_ref, s32[1,12]{1,0:T(1,128)} %bitcast.22, s32[1,12]{1,0:T(1,128)} %bitcast.23, ...), custom_call_target="tpu_custom_call" | custom-call | tf_op jit(solution)/shard_map/pallas_call | solution.py:365
  94.6 1.3 %copy.25 = bf16[8,96]{1,0:T(8,128)(2,1)} copy(bf16[8,96]{1,0:T(8,128)(2,1)} %get-tuple-element.4) | data formatting | bytes 3072
  95.9 1.3 %copy.26 = bf16[8,1536]{1,0:T(8,128)(2,1)} copy(bf16[8,1536]{1,0:T(8,128)(2,1)} %get-tuple-element.5) | data formatting | bytes 49152
  (3 shorter events, 0.0 us)
Async XLA Ops:
  0.6 9.1 %copy-start = (bf16[192,512]{1,0:T(8,128)(2,1)S(1)}, bf16[192,512]{1,0:T(8,128)(2,1)}, u32[]{:S(2)}) copy-start(bf16[192,512]{1,0:T(8,128)(2,1)} %param.17) | copy-start | bytes 589828
  0.6 10.4 %collective-permute-start = (bf16[8,1536]{1,0:T(8,128)(2,1)}, bf16[8,1536]{1,0:T(8,128)(2,1)S(1)}, u32[]{:S(2)}, u32[]{:S(2)}) collective-permute-start(bf16[8,1536]{1,0:T(8,128)(2,1)} %query_ref.1), channel_id=1, source_target_pairs={{0,16},{16,0},{32,48},{48,32},{64,80},{80,64},{96,112},{112,96},{1... | collective-permute-start | bytes 73736 | tf_op jit(solution)/shard_map/ppermute | solution.py:407
  11.0 0.6 copy-start.1

commit v8 on v7

--- a/solution.py
+++ b/solution.py
@@ -23,9 +23,9 @@
 def layer_kernel(
     rows, n_ep, n_grp, width,
     query_ref, mate_query_ref, key_ref, value_ref, owner_ref, fill_ref,
-    own_ref, block_ref, hidden_ref, gain_ref, routes_ref, route_weight_ref, up_ref, down_ref,
+    fresh_ref, block_ref, hidden_ref, gain_ref, routes_ref, route_weight_ref, up_ref, down_ref,
     out_ref, attn_ref,
-    part_ref, got, final, blocks, squares, outgoing, incoming, results, returned,
+    part_ref, own_ref, got, final, blocks, squares, outgoing, incoming, results, returned,
     s1, r1, s2, r2, s3, r3, s_sq, r_sq, s_out, r_in, s_res, r_ret,
 ):
     g = lax.axis_index("grp")
@@ -62,6 +62,18 @@
     both = 2 * rows
     pages = owner_ref.shape[1]
     tokens = key_ref.shape[0]
+    kv_width = key_ref.shape[1]
+    group_size = heads // (kv_width // HD)
+    kv_lane = lax.broadcasted_iota(jnp.int32, (kv_width, width), 0)
+    head_lane = lax.broadcasted_iota(jnp.int32, (kv_width, width), 1)
+    widen = (
+        (kv_lane % HD == head_lane % HD) & (kv_lane // HD == head_lane // (HD * group_size))
+    ).astype(jnp.bfloat16)
+    wide_keys = jnp.dot(key_ref[...], widen, preferred_element_type=jnp.float32).astype(jnp.bfloat16)
+    wide_values = jnp.dot(value_ref[...], widen, preferred_element_type=jnp.float32).astype(jnp.bfloat16)
+    fresh_keys = jnp.dot(
+        fresh_ref[:, :kv_width], widen, preferred_element_type=jnp.float32).astype(jnp.bfloat16)
+    fresh_values = jnp.dot(fresh_ref[:, kv_width:], widen, preferred_element_type=jnp.float32)
     page_length = tokens // pages
     queries = jnp.concatenate([query_ref[...], mate_query_ref[...]], 0)
     lane_head = lax.broadcasted_iota(jnp.int32, (both, width), 1) // HD
@@ -80,27 +92,39 @@
     ) > 0.5
     usable = jnp.concatenate([usable] * heads, 0)
     scores = lax.dot_general(
-        stacked, key_ref[...], (((1,), (1,)), ((), ())), preferred_element_type=jnp.float32
+        stacked, wide_keys, (((1,), (1,)), ((), ())), preferred_element_type=jnp.float32
     ) * (HD ** -0.5)
+    own_scores = lax.dot_general(
+        stacked, fresh_keys, (((1,), (1,)), ((), ())), preferred_element_type=jnp.float32
+    ) * (HD ** -0.5)
+    own_column = lax.broadcasted_iota(jnp.int32, own_scores.shape, 1)
+    own_row = lax.broadcasted_iota(jnp.int32, own_scores.shape, 0) % both
+    own_top = jnp.sum(jnp.where(own_column == own_row, own_scores, 0.0), 1, keepdims=True)
     local_top = jnp.max(jnp.where(usable, scores, masked_score), 1, keepdims=True)
     weights = jnp.where(usable, jnp.exp(scores - local_top), 0.0)
     local_total = jnp.sum(weights, 1, keepdims=True)
     local_accum = jnp.dot(
-        weights.astype(jnp.bfloat16), value_ref[...], preferred_element_type=jnp.float32
+        weights.astype(jnp.bfloat16), wide_values, preferred_element_type=jnp.float32
     )
     accum_rows = jnp.zeros((both, width), jnp.float32)
     top_rows = jnp.zeros((both, width), jnp.float32)
     total_rows = jnp.zeros((both, width), jnp.float32)
+    own_rows = jnp.zeros((both, width), jnp.float32)
     for h in range(heads):
         mine = lane_head == h
         block = slice(h * both, (h + 1) * both)
         accum_rows = jnp.where(mine, local_accum[block], accum_rows)
         top_rows = jnp.where(mine, jnp.broadcast_to(local_top[block], (both, width)), top_rows)
         total_rows = jnp.where(mine, jnp.broadcast_to(local_total[block], (both, width)), total_rows)
+        own_rows = jnp.where(mine, jnp.broadcast_to(own_top[block], (both, width)), own_rows)
     for row in range(both):
         part_ref[row, 0:1, :] = accum_rows[row:row + 1]
         part_ref[row, 1:2, :] = top_rows[row:row + 1]
         part_ref[row, 2:3, :] = total_rows[row:row + 1]
+    for row in range(rows):
+        own_ref[row, 0:1, :] = fresh_values[row:row + 1]
+        own_ref[row, 1:2, :] = own_rows[row:row + 1]
+        own_ref[row, 2:3, :] = jnp.ones((1, width), jnp.float32)
 
     choices = routes_ref.shape[1]
     expert_of = lax.broadcasted_iota(jnp.int32, (rows, n_grp), 1)
@@ -356,7 +380,7 @@
                 give_back(half, peer).wait_send()
 
 
-def layer_call(query, mate_query, keys, values, owner, fill, own, block, hidden, gain, routes, route_weight, up, down):
+def layer_call(query, mate_query, keys, values, owner, fill, fresh, block, hidden, gain, routes, route_weight, up, down):
     n_ep = lax.axis_size("ep")
     n_grp = lax.axis_size("grp")
     rows, share = hidden.shape
@@ -372,6 +396,7 @@
         out_specs=(pl.BlockSpec(memory_space=pltpu.VMEM),) * 2,
         scratch_shapes=[
             pltpu.VMEM((2 * rows, 3, width), jnp.float32),
+            pltpu.VMEM((rows, 3, width), jnp.float32),
             pltpu.VMEM((2 * n_ep, 3, width), jnp.float32),
             pltpu.VMEM((rows, 1, width), jnp.float32),
             pltpu.VMEM((n_grp,) + block.shape, block.dtype),
@@ -394,7 +419,7 @@
             pltpu.SemaphoreType.DMA((n_grp,)),
         ],
         compiler_params=pltpu.CompilerParams(collective_id=0, has_side_effects=True),
-    )(query, mate_query, keys, values, owner, fill, own, block, hidden, gain, routes, route_weight, up, down)
+    )(query, mate_query, keys, values, owner, fill, fresh, block, hidden, gain, routes, route_weight, up, down)
 
 
 def from_partner(block, axis, apart):
@@ -431,38 +456,10 @@
     both_rows = 2 * row_count
     scale = HD ** (-0.5)
     partner_query = from_partner(query, "grp", 0)
-    expanded = (token_count, KV_HEADS, head_group, HD)
-    keys = jnp.broadcast_to(
-        key_cache.reshape(token_count, KV_HEADS, 1, HD), expanded
-    ).reshape(token_count, HEADS * HD)
-    values = jnp.broadcast_to(
-        value_cache.reshape(token_count, KV_HEADS, 1, HD), expanded
-    ).reshape(token_count, HEADS * HD)
-    own_query = query.reshape(row_count, KV_HEADS, head_group, HD)
-    fresh_key = new_kv[:, 0].reshape(row_count, KV_HEADS, HD)
-    fresh_value = new_kv[:, 1].astype(jnp.float32).reshape(row_count, KV_HEADS, HD)
-    own_score = (
-        jnp.einsum(
-            "rkgd,rkd->rkg", own_query, fresh_key, preferred_element_type=jnp.float32
-        ).reshape(row_count, HEADS)
-        * scale
-    )
-    value_rows = jnp.broadcast_to(
-        fresh_value[:, :, None, :], (row_count, KV_HEADS, head_group, HD)
-    ).reshape(row_count, HEADS, HD)
-    width = HEADS * HD
-    own_packed = jnp.stack(
-        [
-            value_rows.reshape(row_count, width),
-            jnp.broadcast_to(own_score[..., None], value_rows.shape).reshape(row_count, width),
-            jnp.ones((row_count, width), jnp.float32),
-        ],
-        1,
-    )
     feature_share = hidden.shape[1]
     layer_out, attn_out = layer_call(
-        query, partner_query, keys, values, page_owner.reshape(1, -1), page_fill.reshape(1, -1),
-        own_packed, out_weight, hidden, norm_gain.reshape(1, feature_share),
+        query, partner_query, key_cache, value_cache, page_owner.reshape(1, -1),
+        page_fill.reshape(1, -1), new_kv.reshape(row_count, -1), out_weight, hidden, norm_gain.reshape(1, feature_share),
         routes, route_weight, gate_up[0], down[0],
     )
     return (layer_out, attn_out)

time: 97.7 us -> 91.7 us (0.939)
  local copies, waits for them, and re-layouts: 9.15 us -> 4.53 us
  other arithmetic: 1.55 us -> 0 us
  waiting for transfers between devices: 0.01 us -> 1 us
    reshape x3 -> x0, local copies, waits for them, and re-layouts: 3 us -> none  [the longest x1 1.07 us: per_device(): values = jnp.broadcast_to(value_cache.reshape(token_count, KV_HEADS, 1, H...]
    ppermute x1, waiting for transfers between devices: 0.01 us -> 1 us  [from_partner(): return lax.ppermute(block, axis, route)]
    unnamed x8 -> x5, local copies, waits for them, and re-layouts: 4.41 us -> 4.53 us
  transfers between devices with their start and end apart: 1 -> 1, of which waited for: 0 -> 1; matrix products, arithmetic and copies ran while one was open for 8% -> 1% of each run, Pallas kernels for 0% -> 0%
where the time goes in v8:
time: 91.7 us; the launch traced here: 91.5 us
  Pallas kernels  82.8 us (90%)
  local copies, waits for them, and re-layouts  4.53 us (5%)
  starting transfers between devices  2.46 us (3%)
  waiting for transfers between devices  1 us (1%)
    pallas_call x1, Pallas kernels, layer_call(): pl.pallas_call(functools.partial(layer_kernel, rows, n_ep, n_grp, width),...  82.8 us
    unnamed x5, local copies, waits for them, and re-layouts  4.53 us
    ppermute x1, starting transfers between devices, from_partner(): return lax.ppermute(block, axis, route)  2.46 us
  transfers between devices with their start and end apart: 1, of which 1 were waited for; matrix products, arithmetic and copies ran while one was open for 1% of the time, Pallas kernels for 0%

profile of v8, /device:TPU:31, one launch (start us, length us, event | category | flops | bytes accessed | tf_op | source)
XLA Modules:
  0.0 91.5 jit_solution(6051529915252131476)
XLA Ops:
  0.6 2.5 %collective-permute-start = (bf16[8,1536]{1,0:T(8,128)(2,1)}, bf16[8,1536]{1,0:T(8,128)(2,1)S(1)}, u32[]{:S(2)}, u32[]{:S(2)}) collective-permute-start(bf16[8,1536]{1,0:T(8,128)(2,1)} %query_ref.1), channel_id=1, source_target_pairs={{0,16},{16,0},{32,48},{48,32},{64,80},{80,64},{96,112},{112,96},{1... | collective-permute-start | bytes 73736 | tf_op jit(solution)/shard_map/ppermute | solution.py:432
  3.1 1.3 %copy.15 = bf16[1,8,2,512]{3,1,2,0:T(8,128)(2,1)} copy(bf16[1,8,2,512]{3,2,1,0:T(2,128)(2,1)} %bitcast.10) | data formatting | bytes 32768
  4.4 1.0 %collective-permute-done.mate_query_ref = bf16[8,1536]{1,0:T(8,128)(2,1)S(1)} collective-permute-done((bf16[8,1536]{1,0:T(8,128)(2,1)}, bf16[8,1536]{1,0:T(8,128)(2,1)S(1)}, u32[]{:S(2)}, u32[]{:S(2)}) %collective-permute-start) | collective-permute-done | bytes 24608 | tf_op jit(solution)/shard_map/ppermute | solution.py:432
  5.4 0.0 copy-start
  5.4 0.6 copy-done
  6.0 82.8 %shard_map.140 = (bf16[8,96]{1,0:T(8,128)(2,1)}, bf16[8,1536]{1,0:T(8,128)(2,1)}) custom-call(bf16[8,1536]{1,0:T(8,128)(2,1)} %query_ref.1, bf16[8,1536]{1,0:T(8,128)(2,1)} %copy-done, bf16[192,512]{1,0:T(8,128)(2,1)} %key_ref.1, bf16[192,512]{1,0:T(8,128)(2,1)} %value_ref.1, s32[1,12]{1,0:T(1,128)} %bitcast.11, s32[1,12]{1,0:T(1,128)} %bitcast.12, ...), custom_call_target="tpu_custom_call" | custom-call | tf_op jit(solution)/shard_map/pallas_call | solution.py:389
  88.9 1.3 %copy.18 = bf16[8,96]{1,0:T(8,128)(2,1)} copy(bf16[8,96]{1,0:T(8,128)(2,1)} %get-tuple-element.4) | data formatting | bytes 3072
  90.1 1.3 %copy.19 = bf16[8,1536]{1,0:T(8,128)(2,1)} copy(bf16[8,1536]{1,0:T(8,128)(2,1)} %get-tuple-element.5) | data formatting | bytes 49152
Async XLA Ops:
  0.6 4.8 %collective-permute-start = (bf16[8,1536]{1,0:T(8,128)(2,1)}, bf16[8,1536]{1,0:T(8,128)(2,1)S(1)}, u32[]{:S(2)}, u32[]{:S(2)}) collective-permute-start(bf16[8,1536]{1,0:T(8,128)(2,1)} %query_ref.1), channel_id=1, source_target_pairs={{0,16},{16,0},{32,48},{48,32},{64,80},{80,64},{96,112},{112,96},{1... | collective-permute-start | bytes 73736 | tf_op jit(solution)/shard_map/ppermute | solution.py:432
  5.4 0.6 copy-start

commit v9 on v8

--- a/solution.py
+++ b/solution.py
@@ -254,31 +254,20 @@
     projected = jnp.dot(attn, columns, preferred_element_type=jnp.float32)
     mixed = hidden_ref[...].astype(jnp.float32) + projected
 
-    own_sum = jnp.sum(mixed * mixed, axis=1, keepdims=True)
-    squares[e] = jnp.broadcast_to(own_sum, squares.shape[1:])
-
-    def sq_copy(peer):
-        return pltpu.make_async_remote_copy(
-            src_ref=squares.at[e], dst_ref=squares.at[e], send_sem=s_sq.at[peer],
-            recv_sem=r_sq.at[e], device_id=(g, peer), device_id_type=MESH)
-
-    def sq_arrival(peer):
-        return pltpu.make_async_remote_copy(
-            src_ref=squares.at[peer], dst_ref=squares.at[peer], send_sem=s_sq.at[peer],
-            recv_sem=r_sq.at[peer], device_id=(g, peer), device_id_type=MESH)
-
-    for peer in range(n_ep):
-        @pl.when(e != peer)
-        def _():
-            sq_copy(peer).start()
-    for peer in range(n_ep):
-        @pl.when(e != peer)
-        def _():
-            sq_arrival(peer).wait_recv()
-    total_sq = jnp.sum(squares[...][:, :, 0:1], axis=0)
-    normed = (mixed * lax.rsqrt(total_sq / width + norm_epsilon) * gain_ref[...]).astype(jnp.bfloat16)
+    scaled = mixed * gain_ref[...]
+    lanes = outgoing.shape[2]
+    place = (
+        lax.broadcasted_iota(jnp.int32, (share, lanes), 0)
+        == lax.broadcasted_iota(jnp.int32, (share, lanes), 1)
+    ).astype(jnp.float32)
+    lane_of = lax.broadcasted_iota(jnp.int32, (rows, lanes), 1)
+    carried = jnp.dot(
+        scaled, place, precision=lax.Precision.HIGHEST, preferred_element_type=jnp.float32
+    ) + jnp.where(lane_of == share, jnp.sum(mixed * mixed, axis=1, keepdims=True), 0.0)
     slots = outgoing.shape[1]
-    picked = jnp.dot(picker, normed, preferred_element_type=jnp.float32)
+    picked = jnp.dot(
+        picker.astype(jnp.float32), carried, precision=lax.Precision.HIGHEST,
+        preferred_element_type=jnp.float32)
     outgoing[...] = picked.reshape(outgoing.shape)
 
     def dispatch(expert):
@@ -306,9 +295,12 @@
             def _():
                 gathered(half, peer).wait_recv()
 
+    arrived = incoming[...]
+    row_total = jnp.sum(arrived[:, :, :, share:share + 1], 0)
+    factor = lax.rsqrt(row_total / width + norm_epsilon)
     pre = jnp.zeros((2 * slots, up_ref.shape[1]), jnp.float32)
     for peer in range(n_ep):
-        lhs = incoming[peer].reshape(2 * slots, share).astype(jnp.bfloat16)
+        lhs = (arrived[peer][:, :, :share] * factor).astype(jnp.bfloat16).reshape(2 * slots, share)
         pre = pre + jnp.dot(
             lhs, up_ref[peer * share:(peer + 1) * share, :], preferred_element_type=jnp.float32)
     hidden_units = up_ref.shape[1] // 2
@@ -365,10 +357,6 @@
 
     for step in range(1, n_grp):
         spread(step).wait_send()
-    for peer in range(n_ep):
-        @pl.when(e != peer)
-        def _():
-            sq_copy(peer).wait_send()
     for expert in range(n_grp):
         @pl.when(jnp.logical_not(serving & (g == expert)))
         def _():
@@ -401,8 +389,8 @@
             pltpu.VMEM((rows, 1, width), jnp.float32),
             pltpu.VMEM((n_grp,) + block.shape, block.dtype),
             pltpu.VMEM((n_ep, rows, 128), jnp.float32),
-            pltpu.VMEM((n_grp, slots, share), jnp.float32),
-            pltpu.VMEM((n_ep, 2, slots, share), jnp.float32),
+            pltpu.VMEM((n_grp, slots, 128), jnp.float32),
+            pltpu.VMEM((n_ep, 2, slots, 128), jnp.float32),
             pltpu.VMEM((n_ep, 2, slots, share), jnp.float32),
             pltpu.VMEM((n_grp, slots, share), jnp.float32),
             pltpu.SemaphoreType.DMA((2 * rows,)),

time: 91.7 us -> 89.4 us (0.975)
  Pallas kernels: 82.8 us -> 80.4 us
    pallas_call x1, Pallas kernels: 82.8 us -> 80.4 us  [layer_call(): pl.pallas_call(functools.partial(layer_kernel, rows, n_ep, n_grp, width),...]
where the time goes in v9:
time: 89.4 us; the launch traced here: 89.1 us
  Pallas kernels  80.4 us (90%)
  local copies, waits for them, and re-layouts  4.53 us (5%)
  starting transfers between devices  2.46 us (3%)
  waiting for transfers between devices  1 us (1%)
    pallas_call x1, Pallas kernels, layer_call(): pl.pallas_call(functools.partial(layer_kernel, rows, n_ep, n_grp, width),...  80.4 us
    unnamed x5, local copies, waits for them, and re-layouts  4.53 us
    ppermute x1, starting transfers between devices, from_partner(): return lax.ppermute(block, axis, route)  2.46 us
  transfers between devices with their start and end apart: 1, of which 1 were waited for; matrix products, arithmetic and copies ran while one was open for 1% of the time, Pallas kernels for 0%

profile of v9, /device:TPU:31, one launch (start us, length us, event | category | flops | bytes accessed | tf_op | source)
XLA Modules:
  0.0 89.1 jit_solution(14548876551915726568)
XLA Ops:
  0.6 2.5 %collective-permute-start = (bf16[8,1536]{1,0:T(8,128)(2,1)}, bf16[8,1536]{1,0:T(8,128)(2,1)S(1)}, u32[]{:S(2)}, u32[]{:S(2)}) collective-permute-start(bf16[8,1536]{1,0:T(8,128)(2,1)} %query_ref.1), channel_id=1, source_target_pairs={{0,16},{16,0},{32,48},{48,32},{64,80},{80,64},{96,112},{112,96},{1... | collective-permute-start | bytes 73736 | tf_op jit(solution)/shard_map/ppermute | solution.py:420
  3.1 1.3 %copy.15 = bf16[1,8,2,512]{3,1,2,0:T(8,128)(2,1)} copy(bf16[1,8,2,512]{3,2,1,0:T(2,128)(2,1)} %bitcast.10) | data formatting | bytes 32768
  4.4 1.0 %collective-permute-done.mate_query_ref = bf16[8,1536]{1,0:T(8,128)(2,1)S(1)} collective-permute-done((bf16[8,1536]{1,0:T(8,128)(2,1)}, bf16[8,1536]{1,0:T(8,128)(2,1)S(1)}, u32[]{:S(2)}, u32[]{:S(2)}) %collective-permute-start) | collective-permute-done | bytes 24608 | tf_op jit(solution)/shard_map/ppermute | solution.py:420
  5.4 0.0 copy-start
  5.4 0.6 copy-done
  6.0 80.4 %shard_map.140 = (bf16[8,96]{1,0:T(8,128)(2,1)}, bf16[8,1536]{1,0:T(8,128)(2,1)}) custom-call(bf16[8,1536]{1,0:T(8,128)(2,1)} %query_ref.1, bf16[8,1536]{1,0:T(8,128)(2,1)} %copy-done, bf16[192,512]{1,0:T(8,128)(2,1)} %key_ref.1, bf16[192,512]{1,0:T(8,128)(2,1)} %value_ref.1, s32[1,12]{1,0:T(1,128)} %bitcast.11, s32[1,12]{1,0:T(1,128)} %bitcast.12, ...), custom_call_target="tpu_custom_call" | custom-call | tf_op jit(solution)/shard_map/pallas_call | solution.py:377
  86.5 1.3 %copy.18 = bf16[8,96]{1,0:T(8,128)(2,1)} copy(bf16[8,96]{1,0:T(8,128)(2,1)} %get-tuple-element.4) | data formatting | bytes 3072
  87.7 1.3 %copy.19 = bf16[8,1536]{1,0:T(8,128)(2,1)} copy(bf16[8,1536]{1,0:T(8,128)(2,1)} %get-tuple-element.5) | data formatting | bytes 49152
Async XLA Ops:
  0.6 4.8 %collective-permute-start = (bf16[8,1536]{1,0:T(8,128)(2,1)}, bf16[8,1536]{1,0:T(8,128)(2,1)S(1)}, u32[]{:S(2)}, u32[]{:S(2)}) collective-permute-start(bf16[8,1536]{1,0:T(8,128)(2,1)} %query_ref.1), channel_id=1, source_target_pairs={{0,16},{16,0},{32,48},{48,32},{64,80},{80,64},{96,112},{112,96},{1... | collective-permute-start | bytes 73736 | tf_op jit(solution)/shard_map/ppermute | solution.py:420
  5.4 0.6 copy-start

commit v10 on v9

--- a/solution.py
+++ b/solution.py
@@ -410,6 +410,36 @@
     )(query, mate_query, keys, values, owner, fill, fresh, block, hidden, gain, routes, route_weight, up, down)
 
 
+def swap_kernel(query_ref, out_ref, held, send_sem, recv_sem):
+    g = lax.axis_index("grp")
+    e = lax.axis_index("ep")
+    mate = g + 1 - 2 * (g % 2)
+    barrier = pltpu.get_barrier_semaphore()
+    pl.semaphore_signal(barrier, inc=1, device_id=(mate, e), device_id_type=MESH)
+    pl.semaphore_wait(barrier, 1)
+    copy = pltpu.make_async_remote_copy(
+        src_ref=query_ref, dst_ref=held, send_sem=send_sem, recv_sem=recv_sem,
+        device_id=(mate, e), device_id_type=MESH)
+    copy.start()
+    copy.wait()
+    out_ref[...] = held[...]
+
+
+def swap_call(query):
+    return pl.pallas_call(
+        swap_kernel,
+        out_shape=jax.ShapeDtypeStruct(query.shape, query.dtype),
+        in_specs=[pl.BlockSpec(memory_space=pltpu.VMEM)],
+        out_specs=pl.BlockSpec(memory_space=pltpu.VMEM),
+        scratch_shapes=[
+            pltpu.VMEM(query.shape, query.dtype),
+            pltpu.SemaphoreType.DMA(()),
+            pltpu.SemaphoreType.DMA(()),
+        ],
+        compiler_params=pltpu.CompilerParams(collective_id=1, has_side_effects=True),
+    )(query)
+
+
 def from_partner(block, axis, apart):
     count = lax.axis_size(axis)
     route = []
@@ -443,7 +473,7 @@
     page_length = token_count // page_count
     both_rows = 2 * row_count
     scale = HD ** (-0.5)
-    partner_query = from_partner(query, "grp", 0)
+    partner_query = swap_call(query)
     feature_share = hidden.shape[1]
     layer_out, attn_out = layer_call(
         query, partner_query, key_cache, value_cache, page_owner.reshape(1, -1),

time: 89.4 us -> 90.1 us (level)
  Pallas kernels: 80.4 us -> 85.2 us
  starting transfers between devices: 2.46 us -> 0 us
  waiting for transfers between devices: 1 us -> 0 us
    pallas_call x0 -> x1, Pallas kernels: none -> 4.72 us  [swap_call(): pl.pallas_call(swap_kernel, out_shape=jax.ShapeDtypeStruct(query.shape, q...]
    ppermute x1 -> x0, starting transfers between devices: 2.46 us -> none  [from_partner(): return lax.ppermute(block, axis, route)]
    ppermute x1 -> x0, waiting for transfers between devices: 1 us -> none  [from_partner(): return lax.ppermute(block, axis, route)]
    unnamed x5 -> x3, local copies, waits for them, and re-layouts: 4.53 us -> 3.92 us
  transfers between devices with their start and end apart: 1 -> 0, of which waited for: 1 -> 0; matrix products, arithmetic and copies ran while one was open for 1% -> 0% of each run, Pallas kernels for 0% -> 0%
where the time goes in v10:
time: 90.1 us; the launch traced here: 89.7 us
  Pallas kernels  85.2 us (95%)
  local copies, waits for them, and re-layouts  3.92 us (4%)
    pallas_call x1, Pallas kernels, layer_call(): pl.pallas_call(functools.partial(layer_kernel, rows, n_ep, n_grp, width),...  80.4 us
    pallas_call x1, Pallas kernels, swap_call(): pl.pallas_call(swap_kernel, out_shape=jax.ShapeDtypeStruct(query.shape, q...  4.72 us
    unnamed x3, local copies, waits for them, and re-layouts  3.92 us

profile of v10, /device:TPU:31, one launch (start us, length us, event | category | flops | bytes accessed | tf_op | source)
XLA Modules:
  0.0 89.7 jit_solution(877693000408017014)
XLA Ops:
  0.6 1.3 %copy.15 = bf16[1,8,2,512]{3,1,2,0:T(8,128)(2,1)} copy(bf16[1,8,2,512]{3,2,1,0:T(2,128)(2,1)} %bitcast.10) | data formatting | bytes 32768
  2.0 4.7 %shard_map.140.mate_query_ref = bf16[8,1536]{1,0:T(8,128)(2,1)} custom-call(bf16[8,1536]{1,0:T(8,128)(2,1)} %query_ref.3), custom_call_target="tpu_custom_call" | custom-call | tf_op jit(solution)/shard_map/pallas_call | solution.py:429
  6.7 80.4 %shard_map.141 = (bf16[8,96]{1,0:T(8,128)(2,1)}, bf16[8,1536]{1,0:T(8,128)(2,1)}) custom-call(bf16[8,1536]{1,0:T(8,128)(2,1)} %query_ref.3, bf16[8,1536]{1,0:T(8,128)(2,1)} %shard_map.140.mate_query_ref, bf16[192,512]{1,0:T(8,128)(2,1)} %key_ref.1, bf16[192,512]{1,0:T(8,128)(2,1)} %value_ref.1, s32[1,12]{1,0:T(1,128)} %bitcast.11, s32[1,12]{1,0:T(1,128)} %bitcast.12, ...), custom_call_target="tpu_custom_call" | custom-call | tf_op jit(solution)/shard_map/pallas_call | solution.py:377
  87.1 1.2 %copy.18 = bf16[8,96]{1,0:T(8,128)(2,1)} copy(bf16[8,96]{1,0:T(8,128)(2,1)} %get-tuple-element.4) | data formatting | bytes 3072
  88.4 1.3 %copy.19 = bf16[8,1536]{1,0:T(8,128)(2,1)} copy(bf16[8,1536]{1,0:T(8,128)(2,1)} %get-tuple-element.5) | data formatting | bytes 49152

commit v11 on v10

--- a/solution.py
+++ b/solution.py
@@ -22,10 +22,10 @@
 
 def layer_kernel(
     rows, n_ep, n_grp, width,
-    query_ref, mate_query_ref, key_ref, value_ref, owner_ref, fill_ref,
+    query_ref, key_ref, value_ref, owner_ref, fill_ref,
     fresh_ref, block_ref, hidden_ref, gain_ref, routes_ref, route_weight_ref, up_ref, down_ref,
     out_ref, attn_ref,
-    part_ref, own_ref, got, final, blocks, squares, outgoing, incoming, results, returned,
+    part_ref, own_ref, mate_query, s_q, r_q, got, final, blocks, squares, outgoing, incoming, results, returned,
     s1, r1, s2, r2, s3, r3, s_sq, r_sq, s_out, r_in, s_res, r_ret,
 ):
     g = lax.axis_index("grp")
@@ -75,52 +75,58 @@
         fresh_ref[:, :kv_width], widen, preferred_element_type=jnp.float32).astype(jnp.bfloat16)
     fresh_values = jnp.dot(fresh_ref[:, kv_width:], widen, preferred_element_type=jnp.float32)
     page_length = tokens // pages
-    queries = jnp.concatenate([query_ref[...], mate_query_ref[...]], 0)
-    lane_head = lax.broadcasted_iota(jnp.int32, (both, width), 1) // HD
-    stacked = jnp.concatenate(
-        [jnp.where(lane_head == h, queries, jnp.zeros_like(queries)) for h in range(heads)], 0
-    )
-    row_of = lax.broadcasted_iota(jnp.int32, (both, pages), 0)
-    owns = (owner_ref[...] == row_of).astype(jnp.float32)
+    lane_head = lax.broadcasted_iota(jnp.int32, (rows, width), 1) // HD
     token_of = lax.broadcasted_iota(jnp.int32, (tokens, pages), 0)
     page_of = lax.broadcasted_iota(jnp.int32, (tokens, pages), 1)
     filled = (
         (token_of // page_length == page_of) & (token_of % page_length < fill_ref[...])
     ).astype(jnp.float32)
-    usable = lax.dot_general(
-        owns, filled, (((1,), (1,)), ((), ())), preferred_element_type=jnp.float32
-    ) > 0.5
-    usable = jnp.concatenate([usable] * heads, 0)
-    scores = lax.dot_general(
-        stacked, wide_keys, (((1,), (1,)), ((), ())), preferred_element_type=jnp.float32
-    ) * (HD ** -0.5)
+
+    def attend(queries, first_row):
+        stacked = jnp.concatenate(
+            [jnp.where(lane_head == h, queries.astype(jnp.float32), 0.0) for h in range(heads)], 0
+        ).astype(jnp.bfloat16)
+        row_of = lax.broadcasted_iota(jnp.int32, (rows, pages), 0) + first_row
+        owns = (owner_ref[...] == row_of).astype(jnp.float32)
+        usable = lax.dot_general(
+            owns, filled, (((1,), (1,)), ((), ())), preferred_element_type=jnp.float32
+        ) > 0.5
+        usable = jnp.concatenate([usable] * heads, 0)
+        scores = lax.dot_general(
+            stacked, wide_keys, (((1,), (1,)), ((), ())), preferred_element_type=jnp.float32
+        ) * (HD ** -0.5)
+        local_top = jnp.max(jnp.where(usable, scores, masked_score), 1, keepdims=True)
+        weights = jnp.where(usable, jnp.exp(scores - local_top), 0.0)
+        local_total = jnp.sum(weights, 1, keepdims=True)
+        local_accum = jnp.dot(
+            weights.astype(jnp.bfloat16), wide_values, preferred_element_type=jnp.float32
+        )
+        accum_rows = jnp.zeros((rows, width), jnp.float32)
+        top_rows = jnp.zeros((rows, width), jnp.float32)
+        total_rows = jnp.zeros((rows, width), jnp.float32)
+        for h in range(heads):
+            mine = lane_head == h
+            block = slice(h * rows, (h + 1) * rows)
+            accum_rows = jnp.where(mine, local_accum[block], accum_rows)
+            top_rows = jnp.where(mine, jnp.broadcast_to(local_top[block], (rows, width)), top_rows)
+            total_rows = jnp.where(mine, jnp.broadcast_to(local_total[block], (rows, width)), total_rows)
+        for row in range(rows):
+            part_ref[first_row + row, 0:1, :] = accum_rows[row:row + 1]
+            part_ref[first_row + row, 1:2, :] = top_rows[row:row + 1]
+            part_ref[first_row + row, 2:3, :] = total_rows[row:row + 1]
+        return stacked
+
+    stacked = attend(query_ref[...], 0)
     own_scores = lax.dot_general(
         stacked, fresh_keys, (((1,), (1,)), ((), ())), preferred_element_type=jnp.float32
     ) * (HD ** -0.5)
     own_column = lax.broadcasted_iota(jnp.int32, own_scores.shape, 1)
-    own_row = lax.broadcasted_iota(jnp.int32, own_scores.shape, 0) % both
+    own_row = lax.broadcasted_iota(jnp.int32, own_scores.shape, 0) % rows
     own_top = jnp.sum(jnp.where(own_column == own_row, own_scores, 0.0), 1, keepdims=True)
-    local_top = jnp.max(jnp.where(usable, scores, masked_score), 1, keepdims=True)
-    weights = jnp.where(usable, jnp.exp(scores - local_top), 0.0)
-    local_total = jnp.sum(weights, 1, keepdims=True)
-    local_accum = jnp.dot(
-        weights.astype(jnp.bfloat16), wide_values, preferred_element_type=jnp.float32
-    )
-    accum_rows = jnp.zeros((both, width), jnp.float32)
-    top_rows = jnp.zeros((both, width), jnp.float32)
-    total_rows = jnp.zeros((both, width), jnp.float32)
-    own_rows = jnp.zeros((both, width), jnp.float32)
+    own_rows = jnp.zeros((rows, width), jnp.float32)
     for h in range(heads):
-        mine = lane_head == h
-        block = slice(h * both, (h + 1) * both)
-        accum_rows = jnp.where(mine, local_accum[block], accum_rows)
-        top_rows = jnp.where(mine, jnp.broadcast_to(local_top[block], (both, width)), top_rows)
-        total_rows = jnp.where(mine, jnp.broadcast_to(local_total[block], (both, width)), total_rows)
-        own_rows = jnp.where(mine, jnp.broadcast_to(own_top[block], (both, width)), own_rows)
-    for row in range(both):
-        part_ref[row, 0:1, :] = accum_rows[row:row + 1]
-        part_ref[row, 1:2, :] = top_rows[row:row + 1]
-        part_ref[row, 2:3, :] = total_rows[row:row + 1]
+        own_rows = jnp.where(
+            lane_head == h, jnp.broadcast_to(own_top[h * rows:(h + 1) * rows], (rows, width)), own_rows)
     for row in range(rows):
         own_ref[row, 0:1, :] = fresh_values[row:row + 1]
         own_ref[row, 1:2, :] = own_rows[row:row + 1]
@@ -172,17 +178,18 @@
             src_ref=part_ref.at[row], dst_ref=got.at[slot], send_sem=s1.at[row],
             recv_sem=r1.at[slot], device_id=target, device_id_type=MESH)
 
-    for row in range(2 * rows):
-        if row < rows:
-            @pl.when(e != row)
-            def _():
-                first(row).start()
-
-            @pl.when(e == row)
-            def _():
-                got[e] = part_ref[row]
-        else:
+    swap = pltpu.make_async_remote_copy(
+        src_ref=query_ref, dst_ref=mate_query, send_sem=s_q, recv_sem=r_q,
+        device_id=(mate, e), device_id_type=MESH)
+    swap.start()
+    for row in range(rows):
+        @pl.when(e != row)
+        def _():
             first(row).start()
+
+        @pl.when(e == row)
+        def _():
+            got[e] = part_ref[row]
 
     def spread(step):
         return pltpu.make_async_remote_copy(
@@ -198,6 +205,11 @@
     for step in range(1, n_grp):
         spread(step).start()
     blocks[g] = block_ref[...]
+
+    swap.wait()
+    attend(mate_query[...], rows)
+    for row in range(rows, 2 * rows):
+        first(row).start()
 
     def incoming_part(slot):
         return pltpu.make_async_remote_copy(
@@ -368,7 +380,7 @@
                 give_back(half, peer).wait_send()
 
 
-def layer_call(query, mate_query, keys, values, owner, fill, fresh, block, hidden, gain, routes, route_weight, up, down):
+def layer_call(query, keys, values, owner, fill, fresh, block, hidden, gain, routes, route_weight, up, down):
     n_ep = lax.axis_size("ep")
     n_grp = lax.axis_size("grp")
     rows, share = hidden.shape
@@ -380,11 +392,14 @@
             jax.ShapeDtypeStruct((rows, share), jnp.bfloat16),
             jax.ShapeDtypeStruct((rows, width), jnp.bfloat16),
         ),
-        in_specs=[pl.BlockSpec(memory_space=pltpu.VMEM)] * 14,
+        in_specs=[pl.BlockSpec(memory_space=pltpu.VMEM)] * 13,
         out_specs=(pl.BlockSpec(memory_space=pltpu.VMEM),) * 2,
         scratch_shapes=[
             pltpu.VMEM((2 * rows, 3, width), jnp.float32),
             pltpu.VMEM((rows, 3, width), jnp.float32),
+            pltpu.VMEM((rows, width), jnp.bfloat16),
+            pltpu.SemaphoreType.DMA(()),
+            pltpu.SemaphoreType.DMA(()),
             pltpu.VMEM((2 * n_ep, 3, width), jnp.float32),
             pltpu.VMEM((rows, 1, width), jnp.float32),
             pltpu.VMEM((n_grp,) + block.shape, block.dtype),
@@ -407,7 +422,7 @@
             pltpu.SemaphoreType.DMA((n_grp,)),
         ],
         compiler_params=pltpu.CompilerParams(collective_id=0, has_side_effects=True),
-    )(query, mate_query, keys, values, owner, fill, fresh, block, hidden, gain, routes, route_weight, up, down)
+    )(query, keys, values, owner, fill, fresh, block, hidden, gain, routes, route_weight, up, down)
 
 
 def swap_kernel(query_ref, out_ref, held, send_sem, recv_sem):
@@ -473,10 +488,9 @@
     page_length = token_count // page_count
     both_rows = 2 * row_count
     scale = HD ** (-0.5)
-    partner_query = swap_call(query)
     feature_share = hidden.shape[1]
     layer_out, attn_out = layer_call(
-        query, partner_query, key_cache, value_cache, page_owner.reshape(1, -1),
+        query, key_cache, value_cache, page_owner.reshape(1, -1),
         page_fill.reshape(1, -1), new_kv.reshape(row_count, -1), out_weight, hidden, norm_gain.reshape(1, feature_share),
         routes, route_weight, gate_up[0], down[0],
     )

time: 90.1 us -> 83.8 us (0.930)
  Pallas kernels: 85.2 us -> 79 us
    pallas_call x1 -> x0, Pallas kernels: 4.72 us -> none  [swap_call(): pl.pallas_call(swap_kernel, out_shape=jax.ShapeDtypeStruct(query.shape, q...]
    pallas_call x1, Pallas kernels: 80.4 us -> 79 us  [layer_call(): pl.pallas_call(functools.partial(layer_kernel, rows, n_ep, n_grp, width),...]
where the time goes in v11:
time: 83.8 us; the launch traced here: 83.6 us
  Pallas kernels  79 us (94%)
  local copies, waits for them, and re-layouts  3.92 us (5%)
    pallas_call x1, Pallas kernels, layer_call(): pl.pallas_call(functools.partial(layer_kernel, rows, n_ep, n_grp, width),...  79 us
    unnamed x3, local copies, waits for them, and re-layouts  3.92 us

profile of v11, /device:TPU:31, one launch (start us, length us, event | category | flops | bytes accessed | tf_op | source)
XLA Modules:
  0.0 83.6 jit_solution(15154355436922094322)
XLA Ops:
  0.6 1.3 %copy.15 = bf16[1,8,2,512]{3,1,2,0:T(8,128)(2,1)} copy(bf16[1,8,2,512]{3,2,1,0:T(2,128)(2,1)} %bitcast.10) | data formatting | bytes 32768
  2.0 79.0 %shard_map.140 = (bf16[8,96]{1,0:T(8,128)(2,1)}, bf16[8,1536]{1,0:T(8,128)(2,1)}) custom-call(bf16[8,1536]{1,0:T(8,128)(2,1)} %query_ref.1, bf16[192,512]{1,0:T(8,128)(2,1)} %key_ref.1, bf16[192,512]{1,0:T(8,128)(2,1)} %value_ref.1, s32[1,12]{1,0:T(1,128)} %bitcast.11, s32[1,12]{1,0:T(1,128)} %bitcast.12, bf16[8,1024]{1,0:T(8,128)(2,1)} %bitcast.9, ...), custom_call_target="tpu_custom_call" | custom-call | tf_op jit(solution)/shard_map/pallas_call | solution.py:389
  81.0 1.2 %copy.18 = bf16[8,96]{1,0:T(8,128)(2,1)} copy(bf16[8,96]{1,0:T(8,128)(2,1)} %get-tuple-element.4) | data formatting | bytes 3072
  82.2 1.3 %copy.19 = bf16[8,1536]{1,0:T(8,128)(2,1)} copy(bf16[8,1536]{1,0:T(8,128)(2,1)} %get-tuple-element.5) | data formatting | bytes 49152

commit v12 on v11

--- a/solution.py
+++ b/solution.py
@@ -72,8 +72,8 @@
     wide_keys = jnp.dot(key_ref[...], widen, preferred_element_type=jnp.float32).astype(jnp.bfloat16)
     wide_values = jnp.dot(value_ref[...], widen, preferred_element_type=jnp.float32).astype(jnp.bfloat16)
     fresh_keys = jnp.dot(
-        fresh_ref[:, :kv_width], widen, preferred_element_type=jnp.float32).astype(jnp.bfloat16)
-    fresh_values = jnp.dot(fresh_ref[:, kv_width:], widen, preferred_element_type=jnp.float32)
+        fresh_ref[:, 0, :], widen, preferred_element_type=jnp.float32).astype(jnp.bfloat16)
+    fresh_values = jnp.dot(fresh_ref[:, 1, :], widen, preferred_element_type=jnp.float32)
     page_length = tokens // pages
     lane_head = lax.broadcasted_iota(jnp.int32, (rows, width), 1) // HD
     token_of = lax.broadcasted_iota(jnp.int32, (tokens, pages), 0)
@@ -491,7 +491,7 @@
     feature_share = hidden.shape[1]
     layer_out, attn_out = layer_call(
         query, key_cache, value_cache, page_owner.reshape(1, -1),
-        page_fill.reshape(1, -1), new_kv.reshape(row_count, -1), out_weight, hidden, norm_gain.reshape(1, feature_share),
+        page_fill.reshape(1, -1), new_kv, out_weight, hidden, norm_gain.reshape(1, feature_share),
         routes, route_weight, gate_up[0], down[0],
     )
     return (layer_out, attn_out)

time: 83.8 us -> 82.5 us (0.984)
  local copies, waits for them, and re-layouts: 3.92 us -> 2.59 us
    unnamed x3 -> x2, local copies, waits for them, and re-layouts: 3.92 us -> 2.59 us
where the time goes in v12:
time: 82.5 us; the launch traced here: 82.3 us
  Pallas kernels  79 us (96%)
  local copies, waits for them, and re-layouts  2.59 us (3%)
    pallas_call x1, Pallas kernels, layer_call(): pl.pallas_call(functools.partial(layer_kernel, rows, n_ep, n_grp, width),...  79 us
    unnamed x2, local copies, waits for them, and re-layouts  2.59 us

profile of v12, /device:TPU:31, one launch (start us, length us, event | category | flops | bytes accessed | tf_op | source)
XLA Modules:
  0.0 82.3 jit_solution(9139177879764046460)
XLA Ops:
  0.6 79.0 %shard_map.140 = (bf16[8,96]{1,0:T(8,128)(2,1)}, bf16[8,1536]{1,0:T(8,128)(2,1)}) custom-call(bf16[8,1536]{1,0:T(8,128)(2,1)} %query_ref.1, bf16[192,512]{1,0:T(8,128)(2,1)} %key_ref.1, bf16[192,512]{1,0:T(8,128)(2,1)} %value_ref.1, s32[1,12]{1,0:T(1,128)} %bitcast.7, s32[1,12]{1,0:T(1,128)} %bitcast.8, bf16[8,2,512]{2,1,0:T(2,128)(2,1)} %fresh_ref.1, ...), custom_call_target="tpu_custom_call" | custom-call | tf_op jit(solution)/shard_map/pallas_call | solution.py:389
  79.7 1.2 %copy.17 = bf16[8,96]{1,0:T(8,128)(2,1)} copy(bf16[8,96]{1,0:T(8,128)(2,1)} %get-tuple-element.4) | data formatting | bytes 3072
  80.9 1.3 %copy.18 = bf16[8,1536]{1,0:T(8,128)(2,1)} copy(bf16[8,1536]{1,0:T(8,128)(2,1)} %get-tuple-element.5) | data formatting | bytes 49152

commit v13 on v12

--- a/solution.py
+++ b/solution.py
@@ -425,46 +425,6 @@
     )(query, keys, values, owner, fill, fresh, block, hidden, gain, routes, route_weight, up, down)
 
 
-def swap_kernel(query_ref, out_ref, held, send_sem, recv_sem):
-    g = lax.axis_index("grp")
-    e = lax.axis_index("ep")
-    mate = g + 1 - 2 * (g % 2)
-    barrier = pltpu.get_barrier_semaphore()
-    pl.semaphore_signal(barrier, inc=1, device_id=(mate, e), device_id_type=MESH)
-    pl.semaphore_wait(barrier, 1)
-    copy = pltpu.make_async_remote_copy(
-        src_ref=query_ref, dst_ref=held, send_sem=send_sem, recv_sem=recv_sem,
-        device_id=(mate, e), device_id_type=MESH)
-    copy.start()
-    copy.wait()
-    out_ref[...] = held[...]
-
-
-def swap_call(query):
-    return pl.pallas_call(
-        swap_kernel,
-        out_shape=jax.ShapeDtypeStruct(query.shape, query.dtype),
-        in_specs=[pl.BlockSpec(memory_space=pltpu.VMEM)],
-        out_specs=pl.BlockSpec(memory_space=pltpu.VMEM),
-        scratch_shapes=[
-            pltpu.VMEM(query.shape, query.dtype),
-            pltpu.SemaphoreType.DMA(()),
-            pltpu.SemaphoreType.DMA(()),
-        ],
-        compiler_params=pltpu.CompilerParams(collective_id=1, has_side_effects=True),
-    )(query)
-
-
-def from_partner(block, axis, apart):
-    count = lax.axis_size(axis)
-    route = []
-    for low in range(count):
-        high = low | 1 << apart
-        if high != low and high < count:
-            route += [(low, high), (high, low)]
-    return lax.ppermute(block, axis, route)
-
-
 def per_device(
     hidden,
     query,
@@ -481,13 +441,6 @@
     route_weight,
 ):
     row_count = query.shape[0]
-    group_count = lax.axis_size("grp")
-    head_group = HEADS // KV_HEADS
-    page_count = page_owner.shape[0]
-    token_count = key_cache.shape[0]
-    page_length = token_count // page_count
-    both_rows = 2 * row_count
-    scale = HD ** (-0.5)
     feature_share = hidden.shape[1]
     layer_out, attn_out = layer_call(
         query, key_cache, value_cache, page_owner.reshape(1, -1),

time: 82.5 us -> 82.5 us (level)
  no operation moved by 1% of the time
where the time goes in v13:
time: 82.5 us; the launch traced here: 82.3 us
  Pallas kernels  79 us (96%)
  local copies, waits for them, and re-layouts  2.59 us (3%)
    pallas_call x1, Pallas kernels, layer_call(): pl.pallas_call(functools.partial(layer_kernel, rows, n_ep, n_grp, width),...  79 us
    unnamed x2, local copies, waits for them, and re-layouts  2.59 us

profile of v13, /device:TPU:31, one launch (start us, length us, event | category | flops | bytes accessed | tf_op | source)
XLA Modules:
  0.0 82.3 jit_solution(9139177879764046460)
XLA Ops:
  0.6 79.0 %shard_map.140 = (bf16[8,96]{1,0:T(8,128)(2,1)}, bf16[8,1536]{1,0:T(8,128)(2,1)}) custom-call(bf16[8,1536]{1,0:T(8,128)(2,1)} %query_ref.1, bf16[192,512]{1,0:T(8,128)(2,1)} %key_ref.1, bf16[192,512]{1,0:T(8,128)(2,1)} %value_ref.1, s32[1,12]{1,0:T(1,128)} %bitcast.7, s32[1,12]{1,0:T(1,128)} %bitcast.8, bf16[8,2,512]{2,1,0:T(2,128)(2,1)} %fresh_ref.1, ...), custom_call_target="tpu_custom_call" | custom-call | tf_op jit(solution)/shard_map/pallas_call | solution.py:389
  79.7 1.2 %copy.17 = bf16[8,96]{1,0:T(8,128)(2,1)} copy(bf16[8,96]{1,0:T(8,128)(2,1)} %get-tuple-element.4) | data formatting | bytes 3072
  80.9 1.3 %copy.18 = bf16[8,1536]{1,0:T(8,128)(2,1)} copy(bf16[8,1536]{1,0:T(8,128)(2,1)} %get-tuple-element.5) | data formatting | bytes 49152

commit v14 on v13

--- a/solution.py
+++ b/solution.py
@@ -257,8 +257,8 @@
     attn = jnp.zeros((rows, width), jnp.float32)
     for row in range(rows):
         attn = jnp.where(row_ids == row, jnp.broadcast_to(final[row], (rows, width)), attn)
+    attn_ref[...] = attn
     attn = attn.astype(jnp.bfloat16)
-    attn_ref[...] = attn
 
     for step in range(1, n_grp):
         gathered_block(step).wait_recv()
@@ -350,7 +350,7 @@
 
     back = returned[...].reshape(n_grp * slots, share).astype(jnp.bfloat16)
     mix = jnp.dot(combine, back, preferred_element_type=jnp.float32)
-    out_ref[...] = (mixed + mix).astype(out_ref.dtype)
+    out_ref[...] = mixed + mix
 
     for row in range(2 * rows):
         if row < rows:
@@ -389,8 +389,8 @@
     return pl.pallas_call(
         functools.partial(layer_kernel, rows, n_ep, n_grp, width),
         out_shape=(
-            jax.ShapeDtypeStruct((rows, share), jnp.bfloat16),
-            jax.ShapeDtypeStruct((rows, width), jnp.bfloat16),
+            jax.ShapeDtypeStruct((rows, share), jnp.float32),
+            jax.ShapeDtypeStruct((rows, width), jnp.float32),
         ),
         in_specs=[pl.BlockSpec(memory_space=pltpu.VMEM)] * 13,
         out_specs=(pl.BlockSpec(memory_space=pltpu.VMEM),) * 2,
@@ -447,7 +447,7 @@
         page_fill.reshape(1, -1), new_kv, out_weight, hidden, norm_gain.reshape(1, feature_share),
         routes, route_weight, gate_up[0], down[0],
     )
-    return (layer_out, attn_out)
+    return (layer_out.astype(jnp.bfloat16), attn_out.astype(jnp.bfloat16))
 
 
 def solution(mesh):

time: 82.5 us -> 82.6 us (level)
  other arithmetic: 0 us -> 2.66 us
  local copies, waits for them, and re-layouts: 2.59 us -> 0 us
    convert_element_type x0 -> x2, other arithmetic: none -> 2.66 us  [per_device(): return (layer_out.astype(jnp.bfloat16), attn_out.astype(jnp.bfloat16))]
    unnamed x2 -> x0, local copies, waits for them, and re-layouts: 2.59 us -> none
where the time goes in v14:
time: 82.6 us; the launch traced here: 82.4 us
  Pallas kernels  79.1 us (96%)
  other arithmetic  2.66 us (3%)
    pallas_call x1, Pallas kernels, layer_call(): pl.pallas_call(functools.partial(layer_kernel, rows, n_ep, n_grp, width),...  79.1 us
    convert_element_type x2, other arithmetic, per_device(): return (layer_out.astype(jnp.bfloat16), attn_out.astype(jnp.bfloat16))  2.66 us

profile of v14, /device:TPU:31, one launch (start us, length us, event | category | flops | bytes accessed | tf_op | source)
XLA Modules:
  0.0 82.4 jit_solution(1138702450375626229)
XLA Ops:
  0.6 79.1 %shard_map.140 = (f32[8,96]{1,0:T(8,128)}, f32[8,1536]{1,0:T(8,128)}) custom-call(bf16[8,1536]{1,0:T(8,128)(2,1)} %query_ref.1, bf16[192,512]{1,0:T(8,128)(2,1)} %key_ref.1, bf16[192,512]{1,0:T(8,128)(2,1)} %value_ref.1, s32[1,12]{1,0:T(1,128)} %bitcast.7, s32[1,12]{1,0:T(1,128)} %bitcast.8, bf16[8,2,512]{2,1,0:T(2,128)(2,1)} %fresh_ref.1, ...), custom_call_target="tpu_custom_call" | custom-call | tf_op jit(solution)/shard_map/pallas_call | solution.py:389
  79.7 1.3 %convert_element_type.6 = bf16[8,96]{1,0:T(8,128)(2,1)} convert(f32[8,96]{1,0:T(8,128)} %get-tuple-element.4) | non-fusion elementwise | flops 768 | bytes 4608 | tf_op jit(solution)/shard_map/convert_element_type | solution.py:450
  81.0 1.4 %convert_element_type.7 = bf16[8,1536]{1,0:T(8,128)(2,1)} convert(f32[8,1536]{1,0:T(8,128)} %get-tuple-element.5) | non-fusion elementwise | flops 12288 | bytes 73728 | tf_op jit(solution)/shard_map/convert_element_type | solution.py:450

commit v15 on v14

--- a/solution.py
+++ b/solution.py
@@ -35,12 +35,6 @@
     serving = home == e
     share = width // n_ep
     barrier = pltpu.get_barrier_semaphore()
-    for peer in range(n_ep):
-        @pl.when(e != peer)
-        def _():
-            pl.semaphore_signal(barrier, inc=1, device_id=(g, peer), device_id_type=MESH)
-            pl.semaphore_signal(barrier, inc=1, device_id=(g, peer), device_id_type=MESH)
-        pl.semaphore_signal(barrier, inc=1, device_id=(mate, peer), device_id_type=MESH)
     for step in range(1, n_grp):
         pl.semaphore_signal(
             barrier, inc=1, device_id=(lax.rem(g + step, n_grp), e), device_id_type=MESH
@@ -56,7 +50,12 @@
                 pl.semaphore_signal(
                     barrier, inc=1, device_id=(2 * e + half, peer), device_id_type=MESH
                 )
-    common = 2 * (n_ep - 1) + n_ep + n_grp - 1
+    for peer in range(n_ep):
+        @pl.when(e != peer)
+        def _():
+            pl.semaphore_signal(barrier, inc=1, device_id=(g, peer), device_id_type=MESH)
+        pl.semaphore_signal(barrier, inc=1, device_id=(mate, peer), device_id_type=MESH)
+    common = n_ep - 1 + n_ep + n_grp - 1
 
     heads = width // HD
     both = 2 * rows

time: 82.6 us -> 82.1 us (level)
  no operation moved by 1% of the time
where the time goes in v15:
time: 82.1 us; the launch traced here: 81.9 us
  Pallas kernels  78.6 us (96%)
  other arithmetic  2.66 us (3%)
    pallas_call x1, Pallas kernels, layer_call(): pl.pallas_call(functools.partial(layer_kernel, rows, n_ep, n_grp, width),...  78.6 us
    convert_element_type x2, other arithmetic, per_device(): return (layer_out.astype(jnp.bfloat16), attn_out.astype(jnp.bfloat16))  2.66 us

profile of v15, /device:TPU:31, one launch (start us, length us, event | category | flops | bytes accessed | tf_op | source)
XLA Modules:
  0.0 81.9 jit_solution(7297739596329311196)
XLA Ops:
  0.6 78.6 %shard_map.140 = (f32[8,96]{1,0:T(8,128)}, f32[8,1536]{1,0:T(8,128)}) custom-call(bf16[8,1536]{1,0:T(8,128)(2,1)} %query_ref.1, bf16[192,512]{1,0:T(8,128)(2,1)} %key_ref.1, bf16[192,512]{1,0:T(8,128)(2,1)} %value_ref.1, s32[1,12]{1,0:T(1,128)} %bitcast.7, s32[1,12]{1,0:T(1,128)} %bitcast.8, bf16[8,2,512]{2,1,0:T(2,128)(2,1)} %fresh_ref.1, ...), custom_call_target="tpu_custom_call" | custom-call | tf_op jit(solution)/shard_map/pallas_call | solution.py:388
  79.2 1.3 %convert_element_type.6 = bf16[8,96]{1,0:T(8,128)(2,1)} convert(f32[8,96]{1,0:T(8,128)} %get-tuple-element.4) | non-fusion elementwise | flops 768 | bytes 4608 | tf_op jit(solution)/shard_map/convert_element_type | solution.py:449
  80.5 1.4 %convert_element_type.7 = bf16[8,1536]{1,0:T(8,128)(2,1)} convert(f32[8,1536]{1,0:T(8,128)} %get-tuple-element.5) | non-fusion elementwise | flops 12288 | bytes 73728 | tf_op jit(solution)/shard_map/convert_element_type | solution.py:449

commit v16 on v15

--- a/solution.py
+++ b/solution.py
@@ -177,6 +177,19 @@
             src_ref=part_ref.at[row], dst_ref=got.at[slot], send_sem=s1.at[row],
             recv_sem=r1.at[slot], device_id=target, device_id_type=MESH)
 
+    def spread(step):
+        return pltpu.make_async_remote_copy(
+            src_ref=block_ref, dst_ref=blocks.at[g], send_sem=s3.at[step],
+            recv_sem=r3.at[g], device_id=(lax.rem(g + step, n_grp), e), device_id_type=MESH)
+
+    def gathered_block(step):
+        source = lax.rem(g + n_grp - step, n_grp)
+        return pltpu.make_async_remote_copy(
+            src_ref=block_ref, dst_ref=blocks.at[source], send_sem=s3.at[step],
+            recv_sem=r3.at[source], device_id=(source, e), device_id_type=MESH)
+
+    for step in range(1, n_grp):
+        spread(step).start()
     swap = pltpu.make_async_remote_copy(
         src_ref=query_ref, dst_ref=mate_query, send_sem=s_q, recv_sem=r_q,
         device_id=(mate, e), device_id_type=MESH)
@@ -190,19 +203,6 @@
         def _():
             got[e] = part_ref[row]
 
-    def spread(step):
-        return pltpu.make_async_remote_copy(
-            src_ref=block_ref, dst_ref=blocks.at[g], send_sem=s3.at[step],
-            recv_sem=r3.at[g], device_id=(lax.rem(g + step, n_grp), e), device_id_type=MESH)
-
-    def gathered_block(step):
-        source = lax.rem(g + n_grp - step, n_grp)
-        return pltpu.make_async_remote_copy(
-            src_ref=block_ref, dst_ref=blocks.at[source], send_sem=s3.at[step],
-            recv_sem=r3.at[source], device_id=(source, e), device_id_type=MESH)
-
-    for step in range(1, n_grp):
-        spread(step).start()
     blocks[g] = block_ref[...]
 
     swap.wait()

time: 82.1 us -> 82.1 us (level)
  no operation moved by 1% of the time
where the time goes in v16:
time: 82.1 us; the launch traced here: 81.9 us
  Pallas kernels  78.6 us (96%)
  other arithmetic  2.66 us (3%)
    pallas_call x1, Pallas kernels, layer_call(): pl.pallas_call(functools.partial(layer_kernel, rows, n_ep, n_grp, width),...  78.6 us
    convert_element_type x2, other arithmetic, per_device(): return (layer_out.astype(jnp.bfloat16), attn_out.astype(jnp.bfloat16))  2.66 us

profile of v16, /device:TPU:31, one launch (start us, length us, event | category | flops | bytes accessed | tf_op | source)
XLA Modules:
  0.0 81.9 jit_solution(10611488402251967484)
XLA Ops:
  0.6 78.6 %shard_map.140 = (f32[8,96]{1,0:T(8,128)}, f32[8,1536]{1,0:T(8,128)}) custom-call(bf16[8,1536]{1,0:T(8,128)(2,1)} %query_ref.1, bf16[192,512]{1,0:T(8,128)(2,1)} %key_ref.1, bf16[192,512]{1,0:T(8,128)(2,1)} %value_ref.1, s32[1,12]{1,0:T(1,128)} %bitcast.7, s32[1,12]{1,0:T(1,128)} %bitcast.8, bf16[8,2,512]{2,1,0:T(2,128)(2,1)} %fresh_ref.1, ...), custom_call_target="tpu_custom_call" | custom-call | tf_op jit(solution)/shard_map/pallas_call | solution.py:388
  79.2 1.3 %convert_element_type.6 = bf16[8,96]{1,0:T(8,128)(2,1)} convert(f32[8,96]{1,0:T(8,128)} %get-tuple-element.4) | non-fusion elementwise | flops 768 | bytes 4608 | tf_op jit(solution)/shard_map/convert_element_type | solution.py:449
  80.5 1.4 %convert_element_type.7 = bf16[8,1536]{1,0:T(8,128)(2,1)} convert(f32[8,1536]{1,0:T(8,128)} %get-tuple-element.5) | non-fusion elementwise | flops 12288 | bytes 73728 | tf_op jit(solution)/shard_map/convert_element_type | solution.py:449
